TPU v7x, 32 devices: a whole 2x2x4 slice. The times are simulated.
32 devices in a mesh: parts: 2 (over y), vocab: 4 (over z), mp: 2 (over x), rep: 2 (over core).
Axes of the slice: x: 2, y: 2, z: 4, core: 2. Of those that a mesh axis runs over, the one named last changes fastest.
Arguments:
- resid_base: bfloat16 [128, 4608], P(('parts', 'vocab', 'rep'), 'mp'), parts along dimension 0, may hold values from -60 to 60
- mlp_hidden: bfloat16 [128, 36864], P(('parts', 'vocab', 'rep'), 'mp'), parts along dimension 0, may hold values from -6 to 6
- edit_in: float32 [73728], P(('parts', 'mp')), parts along dimension 0, may hold values from -0.03125 to 0.03125
- edit_out: float32 [9216], P(('parts', 'mp')), parts along dimension 0, may hold values from -6 to 6
- norm_gain: float32 [4608], P('mp'), may hold values from 0.5 to 1.5
- head: bfloat16 [4608, 8192], P(None, ('vocab', 'mp', 'rep')), may hold values from -0.25 to 0.25
- token_ids: int32 [128], P('parts'), parts along dimension 0, may hold values from 0 to 8191
Outputs:
- penalty: float32 [128], P(('parts', 'vocab', 'rep')), parts along dimension 0
- grad_in: float32 [73728], P(('parts', 'mp')), parts along dimension 0
- grad_out: float32 [9216], P(('parts', 'mp')), parts along dimension 0
There are 2 independent parts, one for each index of `parts`. A program takes and returns all parts, laid end to end along the dimension named above; an argument that names none is the same for every part. Nothing has to cross between parts.
All inputs are finite; a program needn't handle non-finite values.
Results may differ from a plain program's by a relative error of at most 0.011.
Values may be sent and summed in bfloat16 or wider, within the bound.
No kernel may reach another device: no remote copies, remote signals or barrier semaphores. Data moves between devices by JAX's collectives and lax.ppermute only.
A program may use at most 64 MiB of HBM per device.

v0:
```python
import jax
import jax.numpy as jnp
from jax import lax
from jax.sharding import PartitionSpec as P

D = 4608


softcap = 30.0
epsilon = 1e-06


def local(resid_base, mlp_hidden, edit_in, edit_out, norm_gain, head, token_ids):
    tok_rows = resid_base.shape[0]
    feat_cols = resid_base.shape[1]
    voc_cols = head.shape[1]
    hidden_f = mlp_hidden.astype(jnp.float32)
    base_f = resid_base.astype(jnp.float32)
    mix_part = jnp.sum(hidden_f * edit_in[None, :], axis=1)
    mix_scale, square_base, base_along, out_square = lax.psum(
        (
            mix_part,
            jnp.sum(base_f * base_f, axis=1),
            jnp.sum(base_f * edit_out[None, :], axis=1),
            jnp.sum(edit_out * edit_out),
        ),
        "mp",
    )
    resid = base_f + mix_scale[:, None] * edit_out[None, :]
    square_edit = square_base + 2.0 * mix_scale * base_along + mix_scale * mix_scale * out_square
    along = base_along + mix_scale * out_square
    edit_scale = lax.rsqrt(square_edit / D + epsilon)
    base_scale = lax.rsqrt(square_base / D + epsilon)
    x_edit = (resid * edit_scale[:, None] * norm_gain[None, :]).astype(jnp.bfloat16)
    x_base = (base_f * base_scale[:, None] * norm_gain[None, :]).astype(jnp.bfloat16)
    stacked = jnp.stack([x_edit, x_base], axis=0)
    direction = lax.all_gather(edit_out * norm_gain, "mp", axis=0, tiled=True)
    weights_all = lax.all_gather(mix_scale * edit_scale, ("vocab", "rep"), axis=0, tiled=True)
    full_cols = lax.all_gather(stacked, "mp", axis=2, tiled=True)
    logits_pre = jnp.einsum(
        "ktd,dv->ktv",
        lax.all_gather(full_cols, ("vocab", "rep"), axis=1, tiled=True),
        head,
        preferred_element_type=jnp.float32,
    )
    capped = softcap * jnp.tanh(logits_pre / softcap)
    totals = lax.psum(jnp.sum(jnp.exp(capped), axis=2), ("vocab", "mp", "rep"))
    log_totals = jnp.log(totals)
    probs = jnp.exp(capped - log_totals[:, :, None])
    z_edit = capped[0]
    z_base = capped[1]
    first_col = lax.axis_index(("vocab", "mp", "rep")) * voc_cols
    columns = first_col + jnp.arange(voc_cols, dtype=jnp.int32)
    onehot = (token_ids[:, None] == columns[None, :]).astype(jnp.float32)
    diff = z_base - z_edit
    kl_part = jnp.sum(probs[1] * diff, axis=1)
    gap_part = jnp.sum(onehot * diff, axis=1)
    dy_rows = ((2.0 * probs[0] - probs[1] - onehot) * (1.0 - (z_edit / softcap) ** 2)).astype(
        jnp.bfloat16
    )
    dx_part = lax.dot_general(
        dy_rows, head, (((1,), (1,)), ((), ())), preferred_element_type=jnp.float32
    )
    align_part = jnp.sum(logits_pre[0] * dy_rows.astype(jnp.float32), axis=1)
    proj_part = jnp.dot(dx_part, direction, precision=lax.Precision.HIGHEST)
    weighted_part = jnp.dot(weights_all, dx_part, precision=lax.Precision.HIGHEST)
    kl_all, gap_all, proj_all, align_all, weighted_all = lax.psum(
        (kl_part, gap_part, proj_part, align_part, weighted_part), ("vocab", "mp", "rep")
    )
    tok_start = lax.axis_index(("vocab", "rep")) * tok_rows
    feat_start = lax.axis_index("mp") * feat_cols
    kl_own = lax.dynamic_slice_in_dim(kl_all, tok_start, tok_rows, 0)
    gap_own = lax.dynamic_slice_in_dim(gap_all, tok_start, tok_rows, 0)
    proj_own = lax.dynamic_slice_in_dim(proj_all, tok_start, tok_rows, 0)
    align_own = lax.dynamic_slice_in_dim(align_all, tok_start, tok_rows, 0)
    lse_own = lax.dynamic_slice_in_dim(log_totals, tok_start, tok_rows, 1)
    penalty = kl_own + gap_own + 2.0 * (lse_own[0] - lse_own[1])
    normed = resid * edit_scale[:, None]
    shrink = edit_scale * align_own / D
    coeff = edit_scale * proj_own - shrink * (edit_scale * along)
    second_part = jnp.sum((mix_scale * shrink)[:, None] * normed, axis=0)
    grad_in_part = jnp.sum(coeff[:, None] * hidden_f, axis=0)
    second_sum, grad_in = lax.psum((second_part, grad_in_part), ("vocab", "rep"))
    weighted_own = lax.dynamic_slice_in_dim(weighted_all, feat_start, feat_cols, 0)
    grad_out = norm_gain * weighted_own - second_sum
    return (penalty, grad_in, grad_out)


def solution(mesh):
    in_specs = (
        P(("parts", "vocab", "rep"), "mp"),
        P(("parts", "vocab", "rep"), "mp"),
        P(("parts", "mp")),
        P(("parts", "mp")),
        P("mp"),
        P(None, ("vocab", "mp", "rep")),
        P("parts"),
    )
    out_specs = (P(("parts", "vocab", "rep")), P(("parts", "mp")), P(("parts", "mp")))
    return jax.shard_map(local, mesh=mesh, in_specs=in_specs, out_specs=out_specs, check_vma=False)
```

profile of v0, /device:TPU:0, one launch (start us, length us, event | category | flops | bytes accessed | tf_op | source)
XLA Modules:
  0.0 233.2 jit_solution(15880379331970252911)
XLA Ops:
  7.2 0.0 all-gather.3.cloned.1.call-start
  7.2 1.3 fusion.23
  8.6 0.9 fusion.15
  9.5 1.2 fusion.2
  10.7 1.2 dynamic-slice
  12.6 6.5 %all-reduce.2 = (f32[8]{0:T(128)S(1)}, f32[8]{0:T(128)S(1)}, f32[8]{0:T(128)S(1)}, f32[]{:T(128)}) all-reduce(f32[8]{0:T(128)S(1)} %get-tuple-element.6, f32[8]{0:T(128)S(1)} %fusion.2, f32[8]{0:T(128)S(1)} %get-tuple-element.5, f32[]{:T(128)} %get-tuple-element.26), channel_id=1, replica_groups=mesh['parts'=2,'vocab'=4,'mp'=2,'rep'=2] {'mp'}, use_global_device_ids=true, to_apply=%region_3.0 | all-reduce | flops 25 | bytes 200 | tf_op jit(solution)/shard_map/psum | solution.py:20
  19.1 0.7 multiply_dynamic-update-slice_fusion
  19.9 0.9 fusion.18
  20.8 5.1 %all_gather.12 = bf16[2,8,4608]{2,1,0:T(8,128)(2,1)} all-gather(bf16[2,8,2304]{2,1,0:T(8,128)(2,1)S(1)} %pad_maximum_fusion), channel_id=1, replica_groups=mesh['parts'=2,'vocab'=4,'mp'=2,'rep'=2] {'mp'}, dimensions={2}, use_global_device_ids=true | all-gather | bytes 221184 | tf_op jit(solution)/shard_map/all_gather | solution.py:39
  25.9 0.0 all-gather.3.cloned.1.call-update
  25.9 0.0 all-reduce.5.cloned.1.call-start
  26.0 14.9 %all-reduce = f32[64]{0:T(128)S(1)} all-reduce(f32[64]{0:T(128)S(1)} %get-tuple-element.15), channel_id=1, replica_groups=mesh['parts'=2,'vocab'=4,'mp'=2,'rep'=2] {'vocab','rep'}, use_global_device_ids=true, to_apply=%add | all-reduce | flops 64 | bytes 512
  40.9 4.4 %all-gather = f32[2,1,2304]{2,1,0:T(1,128)S(1)} all-gather(f32[1,1,2304]{2,1,0:T(1,128)S(1)} %reshape.34), channel_id=1, replica_groups=mesh['parts'=2,'vocab'=4,'mp'=2,'rep'=2] {'mp'}, dimensions={0}, use_global_device_ids=true | all-gather | bytes 27648 | tf_op jit(solution)/shard_map/all_gather | solution.py:37
  45.3 0.0 copy-start.4
  45.3 5.3 %all-gather.3.cloned.1.call-done = bf16[2,64,4608]{2,1,0:T(8,128)(2,1)} async-done(((bf16[2,8,4608]{2,1,0:T(8,128)(2,1)}), bf16[2,64,4608]{2,1,0:T(8,128)(2,1)}) %all-gather.3.cloned.1.call-update) | async-done | bytes 1179664 | tf_op jit(solution)/shard_map/all_gather | solution.py:42
  50.6 3.6 %exponential_reduce_fusion = (f32[2,64]{1,0:T(2,128)S(1)}, f32[2,64,512]{2,1,0:T(8,128)S(1)}) fusion(bf16[2,64,4608]{2,1,0:T(8,128)(2,1)} %all-gather.3.cloned.1.call-done, bf16[4608,512]{1,0:T(8,128)(2,1)} %param.12), kind=kOutput, calls=%fused_computation.9 | convolution fusion | flops 604176256 | bytes 6160896 | tf_op jit(solution)/shard_map/ktd,dv->ktv/dot_general | solution.py:40
  54.2 32.3 %psum.88 = f32[2,64]{1,0:T(2,128)S(1)} all-reduce(f32[2,64]{1,0:T(2,128)S(1)} %get-tuple-element.30), channel_id=1, replica_groups=mesh['parts'=2,'vocab'=4,'mp'=2,'rep'=2] {'vocab','mp','rep'}, use_global_device_ids=true, to_apply=%region_9.0 | all-reduce | flops 128 | bytes 1024 | tf_op jit(solution)/shard_map/psum | solution.py:47
  86.5 0.1 subtract_exponential_fusion
  86.6 0.0 copy-done.4
  86.7 0.2 fusion.9
  86.9 3.9 %fusion.24 = f32[64,4608]{1,0:T(8,128)S(1)} fusion(bf16[64,512]{1,0:T(8,128)(2,1)S(1)} %get-tuple-element.18, bf16[4608,512]{1,0:T(8,128)(2,1)} %param.12), kind=kOutput, calls=%fused_computation.54 | convolution fusion | flops 301989888 | bytes 5963776 | tf_op jit(solution)/shard_map/dot_general | solution.py:61
  90.8 0.0 copy-start.1
  90.8 0.0 copy-start.2
  90.8 0.0 copy-start
  90.8 0.7 convolution_reduce_fusion
  91.5 0.0 copy-start.3
  91.5 1.0 convolution_bitcast_fusion
  92.5 0.1 constant_dynamic-slice_fusion
  92.6 57.6 %all-reduce.1 = (f32[64]{0:T(128)S(1)}, f32[64]{0:T(128)S(1)}, f32[64]{0:T(128)S(1)}, f32[4608]{0:T(1024)S(1)}) all-reduce(f32[64]{0:T(128)S(1)} %add.92, f32[64]{0:T(128)S(1)} %convolution_bitcast_fusion, f32[64]{0:T(128)S(1)} %get-tuple-element.17, ...), channel_id=1, replica_groups=mesh['parts'=2,'vocab'=4,'mp'=2,'rep'=2] {'vocab','mp','rep'}, use_global_device_ids=true, to_apply=%region_11.0 | all-reduce | flops 4800 | bytes 38400 | tf_op jit(solution)/shard_map/psum | solution.py:67
  150.2 0.7 fusion.21
  151.0 0.0 copy-done.1
  151.0 0.0 copy-done.2
  151.0 0.1 multiply_reduce_fusion.1
  151.1 25.9 %psum.95 = f32[2304]{0:T(1024)S(1)} all-reduce(f32[2304]{0:T(1024)S(1)} %multiply_reduce_fusion.1), channel_id=1, replica_groups=mesh['parts'=2,'vocab'=4,'mp'=2,'rep'=2] {'vocab','rep'}, use_global_device_ids=true, to_apply=%region_21.0 | all-reduce | flops 2304 | bytes 18432 | tf_op jit(solution)/shard_map/psum | solution.py:83
  177.0 0.0 copy-done
  177.0 1.0 fusion.3
  178.0 0.0 all-reduce.5.cloned.1.call-update
  178.0 0.0 copy-done.3
  178.0 0.7 multiply_subtract_fusion
  178.7 0.6 bitcast_add_fusion
  179.3 45.6 %all-reduce.5.cloned.1.call-done = f32[18432]{0:T(1024)} async-done(((f32[18432]{0:T(1024)}), f32[18432]{0:T(1024)}) %all-reduce.5.cloned.1.call-update) | async-done | bytes 73744 | tf_op jit(solution)/shard_map/psum | solution.py:83
  224.9 1.5 copy.12
  (6 shorter events, 0.0 us)
Async XLA Ops:
  7.2 43.4 %all-gather.3.cloned.1.call-start = ((), (), s32[]{:S(2)}) async-start(), calls=%async_computation | async-start | bytes 1327104 | tf_op jit(solution)/shard_map/all_gather | solution.py:42
  25.9 199.0 %all-reduce.5.cloned.1.call-start = ((), (), s32[]{:S(2)}) async-start(), calls=%async_computation.1 | async-start | bytes 147456 | tf_op jit(solution)/shard_map/psum | solution.py:83
  45.3 41.4 %copy-start.4 = (s32[64]{0:T(128)S(1)}, s32[64]{0:T(128)}, u32[]{:S(2)}) copy-start(s32[64]{0:T(128)} %param.13) | copy-start | bytes 772
  90.8 60.2 %copy-start.1 = (bf16[8,2304]{1,0:T(8,128)(2,1)S(1)}, bf16[8,2304]{1,0:T(8,128)(2,1)}, u32[]{:S(2)}) copy-start(bf16[8,2304]{1,0:T(8,128)(2,1)} %param.7) | copy-start | bytes 110596
  90.8 60.2 %copy-start.2 = (f32[2304]{0:T(1024)S(1)}, f32[2304]{0:T(1024)}, u32[]{:S(2)}) copy-start(f32[2304]{0:T(1024)} %param.10) | copy-start | bytes 27652
  90.8 86.2 %copy-start = (bf16[8,18432]{1,0:T(8,128)(2,1)S(1)}, bf16[8,18432]{1,0:T(8,128)(2,1)}, u32[]{:S(2)}) copy-start(bf16[8,18432]{1,0:T(8,128)(2,1)} %param.8) | copy-start | bytes 884740
  91.5 86.5 %copy-start.3 = (f32[2304]{0:T(1024)S(1)}, f32[2304]{0:T(1024)}, u32[]{:S(2)}) copy-start(f32[2304]{0:T(1024)} %param.11) | copy-start | bytes 27652
Sparse Core Ops, SparseCore 0:
  26.0 24.5 all-gather.2
  178.1 46.7 all-reduce.4
where the time goes:
time: 235 us; the launch traced here: 233 us
  blocking collectives  147 us (63%)
  waiting for transfers between devices  50.9 us (22%)
  between operations  14.8 us (6%)
  matrix products  9.18 us (4%)
  other arithmetic  8.58 us (4%)
  local copies, waits for them, and re-layouts  2.88 us (1%)
    psum x1, blocking collectives, local(): lax.psum((kl_part, gap_part, proj_part, align_part, weighted_part), ('voc...  57.6 us
    psum x1, waiting for transfers between devices, local(): lax.psum((second_part, grad_in_part), ('vocab', 'rep'))  45.6 us
    psum x1, blocking collectives, local(): totals = lax.psum(jnp.sum(jnp.exp(capped), axis=2), ('vocab', 'mp', 'rep'))  32.3 us
    psum x1, blocking collectives, local(): lax.psum((second_part, grad_in_part), ('vocab', 'rep'))  25.9 us
    unnamed x1, blocking collectives  14.9 us
    psum x1, blocking collectives, local(): lax.psum((mix_part, jnp.sum(base_f * base_f, axis=1), jnp.sum(base_f * ed...  6.48 us
    all_gather x1, waiting for transfers between devices, local(): lax.all_gather(full_cols, ('vocab', 'rep'), axis=1, tiled=True)  5.31 us
    all_gather x1, blocking collectives, local(): full_cols = lax.all_gather(stacked, 'mp', axis=2, tiled=True)  5.14 us
  transfers between devices with their start and end apart: 2, of which 2 were waited for; matrix products, arithmetic and copies ran while one was open for 1% of the time, Pallas kernels for 0%

commit v1 on v0

v1 whole, which is shorter than its diff:
```python
import functools

import jax
import jax.numpy as jnp
from jax import lax
from jax.sharding import PartitionSpec as P

softcap = 30.0
epsilon = 1e-06
bf16 = jnp.bfloat16
f32 = jnp.float32


def split_bf16(value, pieces):
    out = []
    for _ in range(pieces):
        part = lax.reduce_precision(value, 8, 7)
        out.append(part.astype(bf16))
        value = value - part
    return out


def local(nv, nm, nr, resid_base, mlp_hidden, edit_in, edit_out, norm_gain, head, token_ids):
    rows, feat = resid_base.shape
    hidden = mlp_hidden.shape[1]
    model, voc = head.shape
    group = nv * nr * rows
    peers = nv * nm * nr
    quarter = hidden // (nm * nr)
    everyone = ("vocab", "mp", "rep")

    vectors = lax.all_gather(jnp.stack([edit_out, norm_gain]), "mp", axis=1, tiled=True)
    out_all = vectors[0]
    gain_all = vectors[1]

    hidden_f = mlp_hidden.astype(f32)
    mix_part = jnp.sum(hidden_f * edit_in[None, :], axis=1)
    mix_cols = jnp.stack(split_bf16(mix_part, 3), axis=1)
    packed = jnp.concatenate([resid_base, jnp.pad(mix_cols, ((0, 0), (0, 125)))], axis=1)
    packed = jnp.broadcast_to(packed[None], (nv * nm, rows, feat + 128))
    got = lax.all_to_all(packed, ("vocab", "mp"), 0, 0)
    got = lax.all_gather(got, "rep", axis=0).reshape(nr * nv, nm, rows, feat + 128)

    pieces = mlp_hidden.reshape(rows, nm * nr, quarter).transpose(1, 0, 2)
    units = lax.all_to_all(pieces, ("mp", "rep"), 0, 0).reshape(nm, nr, rows, quarter)

    base = jnp.concatenate([got[:, m, :, :feat].reshape(group, feat) for m in range(nm)], axis=1)
    base_f = base.astype(f32)
    mix = jnp.sum(got[:, :, :, feat : feat + 3].astype(f32), axis=(1, 3)).reshape(group)
    resid = base_f + mix[:, None] * out_all[None, :]
    edit_scale = lax.rsqrt(jnp.mean(resid * resid, axis=1) + epsilon)
    base_scale = lax.rsqrt(jnp.mean(base_f * base_f, axis=1) + epsilon)
    along = jnp.sum(resid * out_all[None, :], axis=1)
    x_edit = (resid * edit_scale[:, None] * gain_all[None, :]).astype(bf16)
    x_base = (base_f * base_scale[:, None] * gain_all[None, :]).astype(bf16)
    direction = jnp.stack(split_bf16(out_all * gain_all, 3) + [jnp.zeros((model,), bf16)] * 5)
    pre = jnp.dot(
        jnp.concatenate([x_edit, x_base, direction]), head, preferred_element_type=f32
    )
    pre_edit = pre[:group]
    pre_base = pre[group : 2 * group]
    toward = jnp.sum(pre[2 * group :], axis=0)
    z_edit = softcap * jnp.tanh(pre_edit / softcap)
    z_base = softcap * jnp.tanh(pre_base / softcap)
    slope = 1.0 - (z_edit / softcap) ** 2
    exp_edit = jnp.exp(z_edit)
    exp_base = jnp.exp(z_base)
    ids = token_ids.reshape(nv, nr, rows).transpose(1, 0, 2).reshape(group)
    first_col = lax.axis_index(everyone) * voc
    onehot = (ids[:, None] == (first_col + jnp.arange(voc, dtype=jnp.int32))[None, :]).astype(f32)
    diff = z_base - z_edit
    pe = exp_edit * slope
    pb = exp_base * slope
    po = onehot * slope
    sums = jnp.stack(
        [
            jnp.sum(a, axis=1)
            for a in (
                exp_edit,
                exp_base,
                exp_base * diff,
                onehot * diff,
                pe * pre_edit,
                pb * pre_edit,
                po * pre_edit,
                pe * toward[None, :],
                pb * toward[None, :],
                po * toward[None, :],
            )
        ]
    )
    flat = 10 * group
    padded = -(-flat // 1024) * 1024
    mine = jnp.pad(sums.reshape(flat), (0, padded - flat)).reshape(padded // 128, 128)
    theirs = lax.all_to_all(
        jnp.broadcast_to(mine[None], (peers, padded // 128, 128)), everyone, 0, 0
    )
    sums = jnp.sum(theirs, axis=0).reshape(padded)[:flat].reshape(10, group)
    se, sb, kl, gap, ae, ab, ao, te, tb, to = [sums[i] for i in range(10)]
    inv_e = 2.0 / se
    inv_b = 1.0 / sb
    align = ae * inv_e - ab * inv_b - ao
    proj = te * inv_e - tb * inv_b - to
    penalty = kl * inv_b + gap + 2.0 * (jnp.log(se) - jnp.log(sb))
    shrink = edit_scale * align / model
    coeff = edit_scale * proj - shrink * (edit_scale * along)
    dy = (pe * inv_e[:, None] - pb * inv_b[:, None] - po).astype(bf16).astype(f32)
    dyw = jnp.sum((mix * edit_scale)[:, None] * dy, axis=0)
    dyw_rows = jnp.stack(split_bf16(dyw, 3) + [jnp.zeros((voc,), bf16)] * 5)
    weighted = jnp.sum(
        lax.dot_general(dyw_rows, head, (((1,), (1,)), ((), ())), preferred_element_type=f32), axis=0
    )
    w_hi, w_lo = split_bf16(weighted, 2)
    v_i = lax.axis_index("vocab")
    m_i = lax.axis_index("mp")
    r_i = lax.axis_index("rep")
    own = lax.dynamic_slice_in_dim(coeff.reshape(nr, nv, rows), v_i, 1, 1).reshape(nr, rows)
    part_in = jnp.sum(units.astype(f32) * own[None, :, :, None], axis=(1, 2)).astype(bf16)
    slab = jnp.concatenate([w_hi.reshape(nm, feat), w_lo.reshape(nm, feat), part_in], axis=1)
    width = 2 * feat + quarter
    if width % 128 == 0:
        slab = slab.reshape(nm, width // 128, 128)
    slab = jnp.broadcast_to(slab[None, :, None], (nv, nm, nr) + slab.shape[1:])
    back = lax.all_to_all(slab.reshape((peers,) + slab.shape[3:]), everyone, 0, 0)
    back = back.reshape(nv, nm * nr, width).astype(f32)
    grad_in = jnp.sum(back[:, :, 2 * feat :], axis=0).reshape(hidden)
    weighted_own = jnp.sum(back[:, :, :feat] + back[:, :, feat : 2 * feat], axis=(0, 1))
    pull = mix * shrink * edit_scale
    base_own = lax.dynamic_slice_in_dim(base, m_i * feat, feat, 1).astype(f32)
    second = jnp.sum(pull[:, None] * base_own, axis=0) + jnp.sum(pull * mix) * edit_out
    grad_out = norm_gain * weighted_own - second
    penalty = lax.dynamic_slice(penalty.reshape(nr, nv, rows), (r_i, v_i, 0), (1, 1, rows))
    return (penalty.reshape(rows), grad_in, grad_out)


def solution(mesh):
    in_specs = (
        P(("parts", "vocab", "rep"), "mp"),
        P(("parts", "vocab", "rep"), "mp"),
        P(("parts", "mp")),
        P(("parts", "mp")),
        P("mp"),
        P(None, ("vocab", "mp", "rep")),
        P("parts"),
    )
    out_specs = (P(("parts", "vocab", "rep")), P(("parts", "mp")), P(("parts", "mp")))
    step = functools.partial(local, mesh.shape["vocab"], mesh.shape["mp"], mesh.shape["rep"])
    return jax.shard_map(step, mesh=mesh, in_specs=in_specs, out_specs=out_specs, check_vma=False)
```

time: 235 us -> 67.7 us (0.29)
  blocking collectives: 147 us -> 7.29 us
  waiting for transfers between devices: 50.9 us -> 22.5 us
  starting transfers between devices: 0.08 us -> 17.9 us
  between operations: 14.8 us -> 0.92 us
  local copies, waits for them, and re-layouts: 2.88 us -> 5.31 us
    psum x4 -> x0, blocking collectives: 122 us -> none  [the longest x1 57.6 us: local(): lax.psum((kl_part, gap_part, proj_part, align_part, weighted_part), ('voc...]
    psum x1 -> x0, waiting for transfers between devices: 45.6 us -> none  [local(): lax.psum((second_part, grad_in_part), ('vocab', 'rep'))]
    all_to_all x0 -> x4, waiting for transfers between devices: none -> 22.5 us  [the longest x1 9.72 us: local(): lax.all_to_all(slab.reshape((peers,) + slab.shape[3:]), everyone, 0, 0)]
    all_to_all x0 -> x4, starting transfers between devices: none -> 17.9 us  [the longest x1 7.25 us: local(): got = lax.all_to_all(packed, ('vocab', 'mp'), 0, 0)]
    unnamed x1 -> x0, blocking collectives: 14.9 us -> none
    all_gather x1 -> x0, waiting for transfers between devices: 5.31 us -> none  [local(): lax.all_gather(full_cols, ('vocab', 'rep'), axis=1, tiled=True)]
    unnamed x14 -> x8, local copies, waits for them, and re-layouts: 2.8 us -> 0.12 us
    dot_general x4 -> x2, matrix products: 9.18 us -> 6.83 us  [the longest x1 3.67 us: local(): lax.dot_general(dyw_rows, head, (((1,), (1,)), ((), ())), preferred_eleme...]
  transfers between devices with their start and end apart: 2 -> 4, of which waited for: 2 -> 4; matrix products, arithmetic and copies ran while one was open for 1% -> 9% of each run, Pallas kernels for 0% -> 0%
where the time goes in v1:
time: 67.7 us; the launch traced here: 67.1 us
  waiting for transfers between devices  22.5 us (33%)
  starting transfers between devices  17.9 us (26%)
  blocking collectives  7.29 us (11%)
  matrix products  6.83 us (10%)
  other arithmetic  6.32 us (9%)
  local copies, waits for them, and re-layouts  5.31 us (8%)
  between operations  0.92 us (1%)
    all_to_all x1, waiting for transfers between devices, local(): lax.all_to_all(slab.reshape((peers,) + slab.shape[3:]), everyone, 0, 0)  9.72 us
    all_to_all x1, starting transfers between devices, local(): got = lax.all_to_all(packed, ('vocab', 'mp'), 0, 0)  7.25 us
    all_to_all x1, waiting for transfers between devices, local(): lax.all_to_all(jnp.broadcast_to(mine[None], (peers, padded // 128, 128)),...  6.73 us
    all_gather x1, blocking collectives, local(): lax.all_gather(jnp.stack([edit_out, norm_gain]), 'mp', axis=1, tiled=True)  5.05 us
    all_to_all x1, waiting for transfers between devices, local(): got = lax.all_to_all(packed, ('vocab', 'mp'), 0, 0)  4.48 us
    all_to_all x1, starting transfers between devices, local(): lax.all_to_all(jnp.broadcast_to(mine[None], (peers, padded // 128, 128)),...  3.69 us
    dot_general x1, matrix products, local(): lax.dot_general(dyw_rows, head, (((1,), (1,)), ((), ())), preferred_eleme...  3.67 us
    all_to_all x1, starting transfers between devices, local(): lax.all_to_all(slab.reshape((peers,) + slab.shape[3:]), everyone, 0, 0)  3.54 us
  transfers between devices with their start and end apart: 4, of which 4 were waited for; matrix products, arithmetic and copies ran while one was open for 9% of the time, Pallas kernels for 0%

profile of v1, /device:TPU:0, one launch (start us, length us, event | category | flops | bytes accessed | tf_op | source)
XLA Modules:
  0.0 67.1 jit_solution(5303250059929946400)
XLA Ops:
  0.6 0.0 copy-start.1
  0.7 1.3 %multiply_reduce_fusion.4 = f32[8]{0:T(128)S(1)} fusion(bf16[8,18432]{1,0:T(8,128)(2,1)} %param.8, f32[18432]{0:T(1024)} %param.9), kind=kLoop, calls=%fused_computation.15 | loop fusion | flops 442360 | bytes 368672 | tf_op jit(solution)/shard_map/reduce_sum | solution.py:37
  1.9 0.1 copy.16
  2.0 0.8 %fusion.11 = bf16[8,2432]{1,0:T(8,128)(2,1)S(1)} fusion(bf16[8,3]{1,0:T(8,128)(2,1)S(1)} %copy.16, bf16[8,2304]{1,0:T(8,128)(2,1)} %param.7), kind=kLoop, calls=%fused_computation.48 | loop fusion | flops 116736 | bytes 75824 | tf_op jit(solution)/shard_map/concatenate | solution.py:39
  2.8 0.7 %broadcast_in_dim.10 = bf16[8,8,2432]{2,1,0:T(8,128)(2,1)} broadcast(bf16[8,2432]{1,0:T(8,128)(2,1)S(1)} %fusion.11), dimensions={1,2} | broadcast | bytes 350208 | tf_op jit(solution)/shard_map/broadcast_in_dim | solution.py:40
  3.5 7.3 %all-to-all-start = ((bf16[8,8,2432]{2,1,0:T(8,128)(2,1)}), bf16[8,8,2432]{2,1,0:T(8,128)(2,1)S(1)}, u32[]{:S(2)}, u32[]{:S(2)}) async-start(bf16[8,8,2432]{2,1,0:T(8,128)(2,1)} %broadcast_in_dim.10), calls=%async_computation | async-start | bytes 622592 | tf_op jit(solution)/shard_map/all_to_all | solution.py:41
  10.8 0.0 copy-done
  10.9 5.1 %all_gather.11 = f32[2,4608]{1,0:T(2,128)S(1)} all-gather(f32[2,2304]{1,0:T(2,128)S(1)} %pad_maximum_fusion.1), channel_id=1, replica_groups=mesh['parts'=2,'vocab'=4,'mp'=2,'rep'=2] {'mp'}, dimensions={1}, use_global_device_ids=true | all-gather | bytes 55296 | tf_op jit(solution)/shard_map/all_gather | solution.py:32
  15.9 0.1 fusion.13
  16.1 0.0 copy-done.2
  16.1 0.1 reshape.257
  16.2 0.1 eq.15
  16.3 4.5 %all-to-all-done = bf16[8,8,2432]{2,1,0:T(8,128)(2,1)S(1)} async-done(((bf16[8,8,2432]{2,1,0:T(8,128)(2,1)}), bf16[8,8,2432]{2,1,0:T(8,128)(2,1)S(1)}, u32[]{:S(2)}, u32[]{:S(2)}) %all-to-all-start) | async-done | bytes 311328 | tf_op jit(solution)/shard_map/all_to_all | solution.py:41
  20.8 2.2 %all-gather = bf16[16,8,2432]{2,1,0:T(8,128)(2,1)S(1)} all-gather(bf16[8,8,2432]{2,1,0:T(8,128)(2,1)S(1)} %all-to-all-done), channel_id=2, replica_groups=mesh['parts'=2,'vocab'=4,'mp'=2,'rep'=2] {'rep'}, dimensions={0}, use_global_device_ids=true | all-gather | bytes 933888 | tf_op jit(solution)/shard_map/all_gather | solution.py:42
  23.0 0.1 convert_reduce_fusion
  23.1 0.1 mul.307
  23.2 0.5 multiply_reduce_fusion
  23.8 0.4 fusion.2
  24.2 0.6 concatenate.18
  24.8 3.2 %fusion.38 = f32[136,512]{1,0:T(8,128)S(1)} fusion(bf16[136,4608]{1,0:T(8,128)(2,1)S(1)} %concatenate.18, bf16[4608,512]{1,0:T(8,128)(2,1)} %param.12), kind=kOutput, calls=%fused_computation.118 | convolution fusion | flops 641728512 | bytes 6250496 | tf_op jit(solution)/shard_map/dot_general | solution.py:57
  28.0 0.4 multiply_reduce_fusion.6
  28.4 0.1 reshape.258
  28.5 0.6 broadcast_in_dim.12
  29.1 3.7 %all-to-all-start.1 = ((f32[16,8,128]{2,1,0:T(8,128)}), f32[16,8,128]{2,1,0:T(8,128)S(1)}, u32[]{:S(2)}, u32[]{:S(2)}) async-start(f32[16,8,128]{2,1,0:T(8,128)} %broadcast_in_dim.12), calls=%async_computation.1 | async-start | bytes 131072 | tf_op jit(solution)/shard_map/all_to_all | solution.py:95
  32.8 0.1 rsqrt.30
  32.9 0.1 reduce_sum.253
  33.0 6.7 %all-to-all-done.1 = f32[16,8,128]{2,1,0:T(8,128)S(1)} async-done(((f32[16,8,128]{2,1,0:T(8,128)}), f32[16,8,128]{2,1,0:T(8,128)S(1)}, u32[]{:S(2)}, u32[]{:S(2)}) %all-to-all-start.1) | async-done | bytes 65568 | tf_op jit(solution)/shard_map/all_to_all | solution.py:95
  39.7 3.5 %all-to-all-start.2 = ((bf16[4,8,4608]{2,1,0:T(8,128)(2,1)}), bf16[4,8,4608]{2,1,0:T(8,128)(2,1)S(1)}, u32[]{:S(2)}, u32[]{:S(2)}) async-start(bf16[4,8,4608]{2,1,0:T(8,128)(2,1)} %bitcast.21), calls=%async_computation.2 | async-start | bytes 589824 | tf_op jit(solution)/shard_map/all_to_all | solution.py:45
  43.2 0.1 reshape.259
  43.3 0.6 multiply_reduce_fusion.13
  43.9 0.1 multiply_reduce_fusion.5
  44.1 3.7 %convolution_reduce_fusion = f32[4608]{0:T(1024)S(1)} fusion(bf16[8,512]{1,0:T(8,128)(2,1)S(1)} %stack.76, bf16[4608,512]{1,0:T(8,128)(2,1)} %param.12), kind=kOutput, calls=%fused_computation.9 | convolution fusion | flops 37780992 | bytes 4745216 | tf_op jit(solution)/shard_map/dot_general | solution.py:111
  47.8 0.1 sub.147
  47.9 0.1 sub.150
  48.0 1.5 %all-to-all-done.2 = bf16[4,8,4608]{2,1,0:T(8,128)(2,1)S(1)} async-done(((bf16[4,8,4608]{2,1,0:T(8,128)(2,1)}), bf16[4,8,4608]{2,1,0:T(8,128)(2,1)S(1)}, u32[]{:S(2)}, u32[]{:S(2)}) %all-to-all-start.2) | async-done | bytes 294944 | tf_op jit(solution)/shard_map/all_to_all | solution.py:45
  49.5 0.3 multiply_reduce_fusion.3
  49.8 0.1 reduce_sum.255
  49.9 0.1 reduce_sum.256
  50.1 0.7 %broadcast_in_dim.14 = bf16[4,2,2,72,128]{4,3,2,1,0:T(8,128)(2,1)} broadcast(bf16[2,72,128]{2,1,0:T(8,128)(2,1)S(1)} %bitcast.75), dimensions={1,3,4} | broadcast | bytes 331776 | tf_op jit(solution)/shard_map/broadcast_in_dim | solution.py:123
  50.8 3.5 %all-to-all-start.3 = ((bf16[16,72,128]{2,1,0:T(8,128)(2,1)}), bf16[16,72,128]{2,1,0:T(8,128)(2,1)S(1)}, u32[]{:S(2)}, u32[]{:S(2)}) async-start(bf16[16,72,128]{2,1,0:T(8,128)(2,1)} %bitcast.24), calls=%async_computation.3 | async-start | bytes 589824 | tf_op jit(solution)/shard_map/all_to_all | solution.py:124
  54.4 0.1 add.86
  54.5 0.5 fusion.26
  55.0 0.2 multiply_reduce_fusion.2
  55.2 9.7 %all-to-all-done.3 = bf16[16,72,128]{2,1,0:T(8,128)(2,1)S(1)} async-done(((bf16[16,72,128]{2,1,0:T(8,128)(2,1)}), bf16[16,72,128]{2,1,0:T(8,128)(2,1)S(1)}, u32[]{:S(2)}, u32[]{:S(2)}) %all-to-all-start.3) | async-done | bytes 294944 | tf_op jit(solution)/shard_map/all_to_all | solution.py:124
  64.9 0.2 reshape.264
  65.1 0.1 fusion.4
  65.2 0.7 reshape.263
  65.9 1.1 %add_subtract_fusion = f32[2304]{0:T(1024)} fusion(f32[2304]{0:T(1024)S(1)} %multiply_reduce_fusion.2, f32[2304]{0:T(1024)S(1)} %copy-done.1, f32[2304]{0:T(1024)S(1)} %copy-done, f32[2304]{0:T(1024)S(1)} %fusion.4, f32[]{:T(128)} %get-tuple-element.21), kind=kLoop, calls=%fused_computation.63 | loop fusion | flops 9216 | bytes 46084 | tf_op jit(solution)/shard_map/sub | solution.py:131
  (31 shorter events, 0.5 us)
Async XLA Ops:
  0.6 10.2 %copy-start.1 = (f32[2304]{0:T(1024)S(1)}, f32[2304]{0:T(1024)}, u32[]{:S(2)}) copy-start(f32[2304]{0:T(1024)} %param.10) | copy-start | bytes 27652
  0.6 10.2 %copy-start = (f32[2304]{0:T(1024)S(1)}, f32[2304]{0:T(1024)}, u32[]{:S(2)}) copy-start(f32[2304]{0:T(1024)} %param.11) | copy-start | bytes 27652
  0.7 15.4 %copy-start.2 = (s32[64]{0:T(128)S(1)}, s32[64]{0:T(128)}, u32[]{:S(2)}) copy-start(s32[64]{0:T(128)} %param.13) | copy-start | bytes 772
  3.5 17.2 %all-to-all-start = ((bf16[8,8,2432]{2,1,0:T(8,128)(2,1)}), bf16[8,8,2432]{2,1,0:T(8,128)(2,1)S(1)}, u32[]{:S(2)}, u32[]{:S(2)}) async-start(bf16[8,8,2432]{2,1,0:T(8,128)(2,1)} %broadcast_in_dim.10), calls=%async_computation | async-start | bytes 622592 | tf_op jit(solution)/shard_map/all_to_all | solution.py:41
  29.1 10.6 %all-to-all-start.1 = ((f32[16,8,128]{2,1,0:T(8,128)}), f32[16,8,128]{2,1,0:T(8,128)S(1)}, u32[]{:S(2)}, u32[]{:S(2)}) async-start(f32[16,8,128]{2,1,0:T(8,128)} %broadcast_in_dim.12), calls=%async_computation.1 | async-start | bytes 131072 | tf_op jit(solution)/shard_map/all_to_all | solution.py:95
  39.7 9.8 %all-to-all-start.2 = ((bf16[4,8,4608]{2,1,0:T(8,128)(2,1)}), bf16[4,8,4608]{2,1,0:T(8,128)(2,1)S(1)}, u32[]{:S(2)}, u32[]{:S(2)}) async-start(bf16[4,8,4608]{2,1,0:T(8,128)(2,1)} %bitcast.21), calls=%async_computation.2 | async-start | bytes 589824 | tf_op jit(solution)/shard_map/all_to_all | solution.py:45
  50.8 14.1 %all-to-all-start.3 = ((bf16[16,72,128]{2,1,0:T(8,128)(2,1)}), bf16[16,72,128]{2,1,0:T(8,128)(2,1)S(1)}, u32[]{:S(2)}, u32[]{:S(2)}) async-start(bf16[16,72,128]{2,1,0:T(8,128)(2,1)} %bitcast.24), calls=%async_computation.3 | async-start | bytes 589824 | tf_op jit(solution)/shard_map/all_to_all | solution.py:124

commit v2 on v1

--- a/solution.py
+++ b/solution.py
@@ -3,6 +3,8 @@
 import jax
 import jax.numpy as jnp
 from jax import lax
+from jax.experimental import pallas as pl
+from jax.experimental.pallas import tpu as pltpu
 from jax.sharding import PartitionSpec as P
 
 softcap = 30.0
@@ -20,7 +22,30 @@
     return out
 
 
-def local(nv, nm, nr, resid_base, mlp_hidden, edit_in, edit_out, norm_gain, head, token_ids):
+def from_peers(value, axis, size):
+    moves = [[(i, (i + k) % size) for i in range(size)] for k in range(size)]
+    return [value] + [lax.ppermute(value, axis, moves[k]) for k in range(1, size)]
+
+
+def to_peers(pick, axis, size, index):
+    moves = [[(i, (i + k) % size) for i in range(size)] for k in range(size)]
+    return [pick(index)] + [
+        lax.ppermute(pick((index + k) % size), axis, moves[k]) for k in range(1, size)
+    ]
+
+
+def in_order(values, index):
+    size = len(values)
+    ordered = []
+    for j in range(size):
+        value = values[0]
+        for k in range(1, size):
+            value = jnp.where((index - j) % size == k, values[k], value)
+        ordered.append(value)
+    return ordered
+
+
+def plain(nv, nm, nr, resid_base, mlp_hidden, edit_in, edit_out, norm_gain, head, token_ids):
     rows, feat = resid_base.shape
     hidden = mlp_hidden.shape[1]
     model, voc = head.shape
@@ -29,9 +54,27 @@
     quarter = hidden // (nm * nr)
     everyone = ("vocab", "mp", "rep")
 
-    vectors = lax.all_gather(jnp.stack([edit_out, norm_gain]), "mp", axis=1, tiled=True)
+    v_i = lax.axis_index("vocab")
+    m_i = lax.axis_index("mp")
+    r_i = lax.axis_index("rep")
+
+    vectors = from_peers(jnp.stack([edit_out, norm_gain]), "mp", nm)
+    vectors = jnp.concatenate(in_order(vectors, m_i), axis=1)
     out_all = vectors[0]
     gain_all = vectors[1]
+
+    units = mlp_hidden.reshape(rows, nm, nr, quarter)
+    units = jnp.concatenate(
+        [
+            part
+            for part in to_peers(
+                lambda r: lax.dynamic_index_in_dim(units, r, 2, keepdims=False), "rep", nr, r_i
+            )
+        ]
+    )
+    units = to_peers(
+        lambda m: lax.dynamic_index_in_dim(units, m, 1, keepdims=False), "mp", nm, m_i
+    )
 
     hidden_f = mlp_hidden.astype(f32)
     mix_part = jnp.sum(hidden_f * edit_in[None, :], axis=1)
@@ -39,10 +82,7 @@
     packed = jnp.concatenate([resid_base, jnp.pad(mix_cols, ((0, 0), (0, 125)))], axis=1)
     packed = jnp.broadcast_to(packed[None], (nv * nm, rows, feat + 128))
     got = lax.all_to_all(packed, ("vocab", "mp"), 0, 0)
-    got = lax.all_gather(got, "rep", axis=0).reshape(nr * nv, nm, rows, feat + 128)
-
-    pieces = mlp_hidden.reshape(rows, nm * nr, quarter).transpose(1, 0, 2)
-    units = lax.all_to_all(pieces, ("mp", "rep"), 0, 0).reshape(nm, nr, rows, quarter)
+    got = jnp.concatenate(in_order(from_peers(got, "rep", nr), r_i)).reshape(nr * nv, nm, rows, feat + 128)
 
     base = jnp.concatenate([got[:, m, :, :feat].reshape(group, feat) for m in range(nm)], axis=1)
     base_f = base.astype(f32)
@@ -89,6 +129,20 @@
             )
         ]
     )
+    weight = mix * edit_scale
+    wo = jnp.sum(weight[:, None] * po, axis=0)
+    high_e, low_e = split_bf16(pe, 2)
+    high_b, low_b = split_bf16(pb, 2)
+    tail = jnp.stack(split_bf16(wo, 3) + [jnp.zeros((voc,), bf16)] * 5)
+    outer = lax.dot_general(
+        jnp.concatenate([high_e, high_b, low_e, low_b, tail]),
+        head,
+        (((1,), (1,)), ((), ())),
+        preferred_element_type=f32,
+    )
+    rows_e = outer[:group] + outer[2 * group : 3 * group]
+    rows_b = outer[group : 2 * group] + outer[3 * group : 4 * group]
+    row_o = jnp.sum(outer[4 * group :], axis=0)
     flat = 10 * group
     padded = -(-flat // 1024) * 1024
     mine = jnp.pad(sums.reshape(flat), (0, padded - flat)).reshape(padded // 128, 128)
@@ -104,18 +158,12 @@
     penalty = kl * inv_b + gap + 2.0 * (jnp.log(se) - jnp.log(sb))
     shrink = edit_scale * align / model
     coeff = edit_scale * proj - shrink * (edit_scale * along)
-    dy = (pe * inv_e[:, None] - pb * inv_b[:, None] - po).astype(bf16).astype(f32)
-    dyw = jnp.sum((mix * edit_scale)[:, None] * dy, axis=0)
-    dyw_rows = jnp.stack(split_bf16(dyw, 3) + [jnp.zeros((voc,), bf16)] * 5)
-    weighted = jnp.sum(
-        lax.dot_general(dyw_rows, head, (((1,), (1,)), ((), ())), preferred_element_type=f32), axis=0
-    )
+    weighted = jnp.sum((weight * inv_e)[:, None] * rows_e, axis=0) - jnp.sum((weight * inv_b)[:, None] * rows_b, axis=0) - row_o
     w_hi, w_lo = split_bf16(weighted, 2)
-    v_i = lax.axis_index("vocab")
-    m_i = lax.axis_index("mp")
-    r_i = lax.axis_index("rep")
-    own = lax.dynamic_slice_in_dim(coeff.reshape(nr, nv, rows), v_i, 1, 1).reshape(nr, rows)
-    part_in = jnp.sum(units.astype(f32) * own[None, :, :, None], axis=(1, 2)).astype(bf16)
+    mine = lax.dynamic_index_in_dim(coeff.reshape(nr, nv, rows), v_i, 1, keepdims=False)
+    own = jnp.concatenate([lax.dynamic_index_in_dim(mine, (r_i - k) % nr, 0, keepdims=False) for k in range(nr)])
+    part_in = [jnp.sum(u.astype(f32) * own[:, None], axis=0) for u in units]
+    part_in = jnp.stack(in_order(part_in, m_i)).astype(bf16)
     slab = jnp.concatenate([w_hi.reshape(nm, feat), w_lo.reshape(nm, feat), part_in], axis=1)
     width = 2 * feat + quarter
     if width % 128 == 0:
@@ -133,6 +181,335 @@
     return (penalty.reshape(rows), grad_in, grad_out)
 
 
+def send_kernel(copies, base_ref, hidden_ref, in_ref, packed_ref):
+    rows, hidden = hidden_ref.shape
+    feat = base_ref.shape[1]
+    total = jnp.zeros((rows, 128), f32)
+    for c in range(0, hidden, 128):
+        total += hidden_ref[:, c : c + 128].astype(f32) * in_ref[:, c : c + 128]
+    mix = jnp.sum(total, axis=1, keepdims=True)
+    lane = lax.broadcasted_iota(jnp.int32, (rows, 128), 1)
+    cols = jnp.zeros((rows, 128), f32)
+    for i in range(3):
+        piece = mix.astype(bf16).astype(f32)
+        cols = jnp.where(lane == i, piece, cols)
+        mix = mix - piece
+    cols = cols.astype(bf16)
+    for i in range(copies):
+        packed_ref[i, :, :feat] = base_ref[...]
+        packed_ref[i, :, feat:] = cols
+
+
+def score_kernel(nv, nm, own_ref, other_ref, vec_ref, ids_ref, head_ref, slab_ref, cols_ref, ops_ref, x_ref):
+    rows = own_ref.shape[1]
+    feat = own_ref.shape[2] - 128
+    model, voc = head_ref.shape
+    pair = 2 * rows
+    group = 2 * nv * rows
+    half = group // 2
+
+    lane_t = lax.broadcasted_iota(jnp.int32, (pair, 128), 1)
+    for k, got_ref in enumerate((own_ref, other_ref)):
+        for v in range(0, nv, 2):
+            at = (k * nv + v) * rows
+
+            def tile(m, c):
+                first = got_ref[v * nm + m, :, c : c + 128].astype(f32)
+                second = got_ref[(v + 1) * nm + m, :, c : c + 128].astype(f32)
+                return jnp.concatenate([first, second], axis=0)
+
+            mixed = tile(0, feat)
+            for m in range(1, nm):
+                mixed += tile(m, feat)
+            mix = jnp.sum(mixed, axis=1, keepdims=True)
+            mix_b = jnp.broadcast_to(mix, (pair, 128))
+            sq_b = jnp.zeros((pair, 128), f32)
+            sq_e = jnp.zeros((pair, 128), f32)
+            dot_o = jnp.zeros((pair, 128), f32)
+            for m in range(nm):
+                for c in range(0, feat, 128):
+                    d = m * feat + c
+                    out = vec_ref[0:1, d : d + 128]
+                    b = tile(m, c)
+                    e = b + mix_b * out
+                    sq_b += b * b
+                    sq_e += e * e
+                    dot_o += e * out
+            scale_e = lax.rsqrt(jnp.sum(sq_e, axis=1, keepdims=True) / model + epsilon)
+            scale_b = lax.rsqrt(jnp.sum(sq_b, axis=1, keepdims=True) / model + epsilon)
+            along = jnp.sum(dot_o, axis=1, keepdims=True)
+            cols_ref[at : at + pair, :] = jnp.where(
+                lane_t == 0, mix, jnp.where(lane_t == 1, scale_e, jnp.where(lane_t == 2, along, 0.0))
+            )
+            scale_e = jnp.broadcast_to(scale_e, (pair, 128))
+            scale_b = jnp.broadcast_to(scale_b, (pair, 128))
+            for m in range(nm):
+                for c in range(0, feat, 128):
+                    d = m * feat + c
+                    out = vec_ref[0:1, d : d + 128]
+                    gain = vec_ref[1:2, d : d + 128]
+                    b = tile(m, c)
+                    e = b + mix_b * out
+                    x_ref[at : at + pair, d : d + 128] = (e * scale_e * gain).astype(bf16)
+                    x_ref[group + at : group + at + pair, d : d + 128] = (b * scale_b * gain).astype(bf16)
+    sub = lax.broadcasted_iota(jnp.int32, (16, 128), 0)
+    for d in range(0, model, 128):
+        rest = vec_ref[0:1, d : d + 128] * vec_ref[1:2, d : d + 128]
+        block = jnp.zeros((16, 128), f32)
+        for i in range(3):
+            piece = rest.astype(bf16).astype(f32)
+            block = jnp.where(sub == i, piece, block)
+            rest = rest - piece
+        x_ref[2 * group :, d : d + 128] = block.astype(bf16)
+
+    pre = jnp.dot(x_ref[...], head_ref[...], preferred_element_type=f32)
+    pre_edit = pre[:group]
+    pre_base = pre[group : 2 * group]
+    toward = jnp.sum(pre[2 * group :], axis=0, keepdims=True)
+    th = jnp.tanh(pre_edit / softcap)
+    z_edit = softcap * th
+    z_base = softcap * jnp.tanh(pre_base / softcap)
+    slope = 1.0 - th * th
+    exp_edit = jnp.exp(z_edit)
+    exp_base = jnp.exp(z_base)
+    first_col = lax.axis_index(("vocab", "mp", "rep")) * voc
+    column = lax.broadcasted_iota(jnp.int32, (group, voc), 1) + first_col
+    hit = column == ids_ref[...]
+    diff = z_base - z_edit
+    pe = exp_edit * slope
+    pb = exp_base * slope
+    po = jnp.where(hit, slope, 0.0)
+
+    def total(a):
+        return jnp.sum(a, axis=1, keepdims=True)
+
+    sums = [
+        total(exp_edit),
+        total(exp_base),
+        total(exp_base * diff),
+        total(jnp.where(hit, diff, 0.0)),
+        total(pe * pre_edit),
+        total(pb * pre_edit),
+        total(po * pre_edit),
+        total(pe * toward),
+        total(pb * toward),
+        total(po * toward),
+    ]
+    lane = lax.broadcasted_iota(jnp.int32, (group, 128), 1)
+    first = jnp.zeros((group, 128), f32)
+    second = jnp.zeros((group, 128), f32)
+    for i in range(8):
+        first = jnp.where(lane == i, sums[i], first)
+    for i in range(8, 10):
+        second = jnp.where(lane == i - 8, sums[i], second)
+    straight = jnp.concatenate([first, second], axis=0)
+    swapped = jnp.concatenate([first[half:], first[:half], second[half:], second[:half]], axis=0)
+    table = jnp.where(lax.axis_index("rep") == 0, straight, swapped)
+    table = table.T[:8]
+    for p in range(slab_ref.shape[0]):
+        slab_ref[p] = table
+
+    high_e = pe.astype(bf16)
+    high_b = pb.astype(bf16)
+    ops_ref[:group] = high_e
+    ops_ref[group : 2 * group] = high_b
+    ops_ref[2 * group : 3 * group] = (pe - high_e.astype(f32)).astype(bf16)
+    ops_ref[3 * group : 4 * group] = (pb - high_b.astype(f32)).astype(bf16)
+    weight = cols_ref[:, 0:1] * cols_ref[:, 1:2]
+    rest = jnp.sum(weight * po, axis=0, keepdims=True)
+    sub = lax.broadcasted_iota(jnp.int32, (16, voc), 0)
+    block = jnp.zeros((16, voc), f32)
+    for i in range(3):
+        piece = rest.astype(bf16).astype(f32)
+        block = jnp.where(sub == i, piece, block)
+        rest = rest - piece
+    ops_ref[4 * group :] = block.astype(bf16)
+
+
+def close_kernel(nv, nm, theirs_ref, cols_ref, outer_ref, own_ref, other_ref, out_ref, *refs):
+    units = refs[:nm]
+    slab_ref, second_ref, penalty_ref, coeff_ref, pen_ref, vec_ref = refs[nm:]
+    rows = own_ref.shape[1]
+    feat = own_ref.shape[2] - 128
+    model = outer_ref.shape[1]
+    group = 2 * nv * rows
+    half = group // 2
+    tiles = feat // 128
+    v_i = lax.axis_index("vocab")
+    m_i = lax.axis_index("mp")
+    r_i = lax.axis_index("rep")
+
+    table = theirs_ref[0]
+    for p in range(1, theirs_ref.shape[0]):
+        table += theirs_ref[p]
+    table = jnp.concatenate([table, jnp.zeros((120, 128), f32)], axis=0).T
+    first = table[:group]
+    second = table[group:]
+    swap_first = jnp.concatenate([first[half:], first[:half]], axis=0)
+    swap_second = jnp.concatenate([second[half:], second[:half]], axis=0)
+    first = jnp.where(r_i == 0, first, swap_first)
+    second = jnp.where(r_i == 0, second, swap_second)
+    se, sb, kl, gap, ae, ab, ao, te = [first[:, i : i + 1] for i in range(8)]
+    tb, to = second[:, 0:1], second[:, 1:2]
+    mix = cols_ref[:, 0:1]
+    scale = cols_ref[:, 1:2]
+    along = cols_ref[:, 2:3]
+    inv_e = 2.0 / se
+    inv_b = 1.0 / sb
+    align = ae * inv_e - ab * inv_b - ao
+    proj = te * inv_e - tb * inv_b - to
+    penalty = kl * inv_b + gap + 2.0 * (jnp.log(se) - jnp.log(sb))
+    shrink = scale * align / model
+    coeff = scale * proj - shrink * (scale * along)
+    weight = mix * scale
+    pull = weight * shrink
+    coeff_ref[...] = jnp.broadcast_to(coeff, (group, 128))
+    pen_ref[...] = jnp.broadcast_to(penalty, (group, 128))
+    penalty_ref[...] = pen_ref[pl.ds(pl.multiple_of(v_i * rows, rows), rows), :]
+
+    by_e = jnp.broadcast_to(weight * inv_e, (group, 128))
+    by_b = jnp.broadcast_to(weight * inv_b, (group, 128))
+    for m in range(nm):
+        for t in range(tiles):
+            d = m * feat + t * 128
+            plus = (outer_ref[:group, d : d + 128] + outer_ref[2 * group : 3 * group, d : d + 128]) * by_e
+            less = (outer_ref[group : 2 * group, d : d + 128] + outer_ref[3 * group : 4 * group, d : d + 128]) * by_b
+            row = jnp.sum(plus - less, axis=0, keepdims=True)
+            row -= jnp.sum(outer_ref[4 * group :, d : d + 128], axis=0, keepdims=True)
+            high = row.astype(bf16).astype(f32)
+            vec_ref[m, t : t + 1, :] = high
+            vec_ref[m, tiles + t : tiles + t + 1, :] = row - high
+    own = jnp.concatenate(
+        [
+            coeff_ref[pl.ds(pl.multiple_of((k * nv + v_i) * rows, rows), rows), :]
+            for k in range(2)
+        ],
+        axis=0,
+    )
+    for k in range(nm):
+        m = lax.rem(m_i - k + nm, nm)
+        for t in range(units[k].shape[1] // 128):
+            row = jnp.sum(units[k][:, t * 128 : (t + 1) * 128].astype(f32) * own, axis=0, keepdims=True)
+            vec_ref[m, pl.ds(2 * tiles + t, 1), :] = row
+    for m in range(nm):
+        block = vec_ref[m].astype(bf16)
+        for v in range(nv):
+            for r in range(2):
+                slab_ref[(v * nm + m) * 2 + r] = block
+
+    by_p = jnp.broadcast_to(pull, (group, 128))
+    pulled = jnp.sum(pull * mix, axis=0, keepdims=True)
+    for t in range(tiles):
+        c = t * 128
+        part = jnp.zeros((rows, 128), f32)
+        for k, got_ref in enumerate((own_ref, other_ref)):
+            for v in range(nv):
+                at = (k * nv + v) * rows
+                part += got_ref[v * nm + m_i, :, c : c + 128].astype(f32) * by_p[at : at + rows]
+        second_ref[t : t + 1, :] = (
+            jnp.sum(part, axis=0, keepdims=True) + pulled * out_ref[:, c : c + 128]
+        )
+
+
+def sum_kernel(back_ref, gain_ref, second_ref, in_ref, out_ref):
+    peers = back_ref.shape[0]
+    tiles = gain_ref.shape[0]
+    units = back_ref.shape[1] - 2 * tiles
+    pieces = in_ref.shape[0] // units
+    wide = jnp.zeros((tiles, 128), f32)
+    for q in range(pieces):
+        total = back_ref[q].astype(f32)
+        for p in range(q + pieces, peers, pieces):
+            total += back_ref[p].astype(f32)
+        wide += total[:tiles] + total[tiles : 2 * tiles]
+        in_ref[q * units : (q + 1) * units, :] = total[2 * tiles :]
+    out_ref[...] = gain_ref[...] * wide - second_ref[...]
+
+
+def call(kernel, out_shape, scratch=()):
+    return pl.pallas_call(
+        kernel,
+        out_shape=out_shape,
+        scratch_shapes=scratch,
+        compiler_params=pltpu.CompilerParams(vmem_limit_bytes=40 << 20),
+    )
+
+
+def fused(nv, nm, nr, resid_base, mlp_hidden, edit_in, edit_out, norm_gain, head, token_ids):
+    rows, feat = resid_base.shape
+    hidden = mlp_hidden.shape[1]
+    model, voc = head.shape
+    group = nv * nr * rows
+    peers = nv * nm * nr
+    quarter = hidden // (nm * nr)
+    everyone = ("vocab", "mp", "rep")
+    m_i = lax.axis_index("mp")
+    r_i = lax.axis_index("rep")
+    shape = jax.ShapeDtypeStruct
+
+    packed = call(
+        functools.partial(send_kernel, nv * nm), shape((nv * nm, rows, feat + 128), bf16)
+    )(resid_base, mlp_hidden, edit_in.reshape(1, hidden))
+    got = lax.all_to_all(packed, ("vocab", "mp"), 0, 0)
+    other = lax.ppermute(got, "rep", [(0, 1), (1, 0)])
+
+    vectors = from_peers(jnp.stack([edit_out, norm_gain]), "mp", nm)
+    vectors = jnp.concatenate(in_order(vectors, m_i), axis=1)
+    ids = token_ids.reshape(nv, nr, rows)
+    ids = jnp.concatenate(
+        [lax.dynamic_index_in_dim(ids, (r_i + k) % nr, 1, keepdims=False) for k in range(nr)]
+    ).reshape(group, 1)
+
+    units = mlp_hidden.reshape(rows, nm, nr, quarter)
+    units = jnp.concatenate(
+        to_peers(lambda r: lax.dynamic_index_in_dim(units, r, 2, keepdims=False), "rep", nr, r_i)
+    )
+    units = to_peers(
+        lambda m: lax.dynamic_index_in_dim(units, m, 1, keepdims=False), "mp", nm, m_i
+    )
+
+    slab, cols, ops = call(
+        functools.partial(score_kernel, nv, nm),
+        (
+            shape((peers, 8, 128), f32),
+            shape((group, 128), f32),
+            shape((4 * group + 16, voc), bf16),
+        ),
+        [pltpu.VMEM((2 * group + 16, model), bf16)],
+    )(got, other, vectors, ids, head)
+    theirs = lax.all_to_all(slab, everyone, 0, 0)
+    outer = lax.dot_general(ops, head, (((1,), (1,)), ((), ())), preferred_element_type=f32)
+
+    width = (2 * feat + quarter) // 128
+    slab, second, penalty = call(
+        functools.partial(close_kernel, nv, nm),
+        (
+            shape((peers, width, 128), bf16),
+            shape((feat // 128, 128), f32),
+            shape((rows, 128), f32),
+        ),
+        [
+            pltpu.VMEM((group, 128), f32),
+            pltpu.VMEM((group, 128), f32),
+            pltpu.VMEM((nm, width, 128), f32),
+        ],
+    )(theirs, cols, outer, got, other, edit_out.reshape(1, feat), *units)
+    back = lax.all_to_all(slab, everyone, 0, 0)
+    grad_in, grad_out = call(
+        sum_kernel, (shape((hidden // 128, 128), f32), shape((feat // 128, 128), f32))
+    )(back, norm_gain.reshape(feat // 128, 128), second)
+    return (penalty[:, 0], grad_in.reshape(hidden), grad_out.reshape(feat))
+
+
+def local(nv, nm, nr, resid_base, mlp_hidden, *rest):
+    rows, feat = resid_base.shape
+    quarter = mlp_hidden.shape[1] // (nm * nr)
+    whole_tiles = rows == 8 and feat % 128 == 0 and quarter % 128 == 0
+    small = nr == 2 and nv % 2 == 0 and nv * nr * rows == 64
+    step = fused if whole_tiles and small else plain
+    return step(nv, nm, nr, resid_base, mlp_hidden, *rest)
+
+
 def solution(mesh):
     in_specs = (
         P(("parts", "vocab", "rep"), "mp"),

time: 67.7 us -> 63.6 us (0.939)
  blocking collectives: 7.29 us -> 0 us
  other arithmetic: 6.32 us -> 0.1 us
  local copies, waits for them, and re-layouts: 5.31 us -> 11.2 us
  Pallas kernels: 0 us -> 5.81 us
  waiting for transfers between devices: 22.5 us -> 20.4 us
  matrix products: 6.83 us -> 6.08 us
    all_gather x2 -> x0, blocking collectives: 7.29 us -> none  [the longest x1 5.05 us: local(): lax.all_gather(jnp.stack([edit_out, norm_gain]), 'mp', axis=1, tiled=True)]
    unnamed x8 -> x12, local copies, waits for them, and re-layouts: 0.12 us -> 7.37 us
    pallas_call x0 -> x4, Pallas kernels: none -> 5.81 us  [the longest x1 2.36 us: fused(): call(functools.partial(score_kernel, nv, nm), (shape((peers, 8, 128), f32...]
    ppermute x0 -> x4, starting transfers between devices: none -> 4.61 us  [the longest x1 3 us: from_peers(): lax.ppermute(value, axis, moves[k])]
    all_to_all x4 -> x3, starting transfers between devices: 17.9 us -> 13.9 us  [the longest x1 5.22 us: fused(): back = lax.all_to_all(slab, everyone, 0, 0)]
    reduce_sum x13 -> x0, other arithmetic: 3.68 us -> none  [the longest x1 1.25 us: local(): mix_part = jnp.sum(hidden_f * edit_in[None, :], axis=1)]
    broadcast_in_dim x4 -> x0, local copies, waits for them, and re-layouts: 2.12 us -> none  [the longest x1 0.75 us: local(): slab = jnp.broadcast_to(slab[None, :, None], (nv, nm, nr) + slab.shape[1:])]
    all_to_all x4 -> x3, waiting for transfers between devices: 22.5 us -> 20.4 us  [the longest x1 9.95 us: fused(): back = lax.all_to_all(slab, everyone, 0, 0)]
  transfers between devices with their start and end apart: 4 -> 7, of which waited for: 4 -> 3; matrix products, arithmetic and copies ran while one was open for 9% -> 14% of each run, Pallas kernels for 0% -> 5%
where the time goes in v2:
time: 63.6 us; the launch traced here: 62.9 us
  waiting for transfers between devices  20.4 us (32%)
  starting transfers between devices  18.5 us (29%)
  local copies, waits for them, and re-layouts  11.2 us (18%)
  matrix products  6.08 us (10%)
  Pallas kernels  5.81 us (9%)
  between operations  0.77 us (1%)
    all_to_all x1, waiting for transfers between devices, fused(): back = lax.all_to_all(slab, everyone, 0, 0)  9.95 us
    all_to_all x1, waiting for transfers between devices, fused(): got = lax.all_to_all(packed, ('vocab', 'mp'), 0, 0)  9.63 us
    unnamed x12, local copies, waits for them, and re-layouts  7.37 us
    dot_general x1, matrix products, fused(): lax.dot_general(ops, head, (((1,), (1,)), ((), ())), preferred_element_ty...  6.08 us
    all_to_all x1, starting transfers between devices, fused(): back = lax.all_to_all(slab, everyone, 0, 0)  5.22 us
    all_to_all x1, starting transfers between devices, fused(): got = lax.all_to_all(packed, ('vocab', 'mp'), 0, 0)  4.88 us
    all_to_all x1, starting transfers between devices, fused(): theirs = lax.all_to_all(slab, everyone, 0, 0)  3.75 us
    ppermute x1, starting transfers between devices, from_peers(): lax.ppermute(value, axis, moves[k])  3 us
  transfers between devices with their start and end apart: 7, of which 3 were waited for; matrix products, arithmetic and copies ran while one was open for 14% of the time, Pallas kernels for 5%

profile of v2, /device:TPU:0, one launch (start us, length us, event | category | flops | bytes accessed | tf_op | source)
XLA Modules:
  0.0 62.9 jit_solution(6307576075565855899)
XLA Ops:
  0.6 0.7 %stack.9.out_ref = f32[1,2304]{1,0:T(1,128)S(1)} reshape(f32[2304]{0:T(1024)} %param.10) | data formatting | bytes 18432 | tf_op jit(solution)/shard_map/stack | solution.py:456
  1.3 0.7 %stack.10 = f32[1,2304]{1,0:T(1,128)S(1)} reshape(f32[2304]{0:T(1024)} %param.11) | data formatting | bytes 18432 | tf_op jit(solution)/shard_map/stack | solution.py:456
  2.1 3.0 %collective-permute-start.1 = (f32[2,2304]{1,0:T(2,128)S(1)}, f32[2,2304]{1,0:T(2,128)S(1)}, u32[]{:S(2)}, u32[]{:S(2)}) collective-permute-start(f32[2,2304]{1,0:T(2,128)S(1)} %pad_maximum_fusion.1), channel_id=1, source_target_pairs={{0,2},{2,0},{1,3},{3,1},{4,6},{6,4},{5,7},{7,5},{8,10},{10,8},{9,1... | collective-permute-start | bytes 55304 | tf_op jit(solution)/shard_map/ppermute | solution.py:27
  5.1 1.0 %dynamic-slice_bitcast_fusion = (bf16[8,2,4608]{2,0,1:T(8,128)(2,1)S(1)}, bf16[8,2,4608]{2,0,1:T(8,128)(2,1)S(1)}) fusion(bf16[8,2,2,4608]{3,0,2,1:T(8,128)(2,1)} %bitcast.17, s32[]{:T(128)S(6)} %select_n.67, s32[]{:T(128)S(6)} %select_n.68), kind=kLoop, calls=%fused_computation.8 | loop fusion | bytes 589832 | tf_op jit(solution)/shard_map/jit(dynamic_index_in_dim)/squeeze | solution.py:465
  6.1 0.1 collective-permute-start.2
  6.2 0.0 copy-start.2
  6.2 1.0 %copy-done.2 = bf16[8,18432]{1,0:T(8,128)(2,1)S(1)} copy-done((bf16[8,18432]{1,0:T(8,128)(2,1)S(1)}, bf16[8,18432]{1,0:T(8,128)(2,1)}, u32[]{:S(2)}) %copy-start.2) | copy-done | bytes 294936
  7.1 0.0 copy-start.3
  7.1 0.9 %copy-done.3 = f32[18432]{0:T(1024)S(1)} copy-done((f32[18432]{0:T(1024)S(1)}, f32[18432]{0:T(1024)}, u32[]{:S(2)}) %copy-start.3) | copy-done | bytes 73752
  8.0 0.0 copy-start.5
  8.0 0.8 %copy-done.5 = bf16[8,2304]{1,0:T(8,128)(2,1)S(1)} copy-done((bf16[8,2304]{1,0:T(8,128)(2,1)S(1)}, bf16[8,2304]{1,0:T(8,128)(2,1)}, u32[]{:S(2)}) %copy-start.5) | copy-done | bytes 36888
  8.8 1.0 %shard_map.94 = bf16[8,8,2432]{2,1,0:T(8,128)(2,1)} custom-call(bf16[8,2304]{1,0:T(8,128)(2,1)S(1)} %copy-done.5, bf16[8,18432]{1,0:T(8,128)(2,1)S(1)} %copy-done.2, f32[1,18432]{1,0:T(1,128)S(1)} %bitcast.18), custom_call_target="tpu_custom_call" | custom-call | tf_op jit(solution)/shard_map/pallas_call | solution.py:450
  9.7 4.9 %all-to-all-start = ((bf16[8,8,2432]{2,1,0:T(8,128)(2,1)}), bf16[8,8,2432]{2,1,0:T(8,128)(2,1)S(1)}, u32[]{:S(2)}, u32[]{:S(2)}) async-start(bf16[8,8,2432]{2,1,0:T(8,128)(2,1)} %shard_map.94), calls=%async_computation | async-start | bytes 622592 | tf_op jit(solution)/shard_map/all_to_all | solution.py:453
  14.6 0.7 %reshape.29 = s32[4,2,8]{2,1,0:T(2,128)S(1)} reshape(s32[64]{0:T(128)} %param.13) | data formatting | bytes 512 | tf_op jit(solution)/shard_map/reshape | solution.py:458
  15.4 0.1 reshape.35.ids_ref
  15.5 0.0 collective-permute-done.1
  15.6 9.6 %all-to-all-done.own_ref = bf16[8,8,2432]{2,1,0:T(8,128)(2,1)S(1)} async-done(((bf16[8,8,2432]{2,1,0:T(8,128)(2,1)}), bf16[8,8,2432]{2,1,0:T(8,128)(2,1)S(1)}, u32[]{:S(2)}, u32[]{:S(2)}) %all-to-all-start) | async-done | bytes 311328 | tf_op jit(solution)/shard_map/all_to_all | solution.py:453
  25.2 0.0 collective-permute-start
  25.2 0.0 collective-permute-done.2
  25.2 1.5 %collective-permute-start.3 = (bf16[16,4608]{1,0:T(8,128)(2,1)S(1)}, bf16[16,4608]{1,0:T(8,128)(2,1)S(1)}, u32[]{:S(2)}, u32[]{:S(2)}) collective-permute-start(bf16[16,4608]{1,0:T(8,128)(2,1)S(1)} %get-tuple-element.19), channel_id=1, source_target_pairs={{0,2},{2,0},{1,3},{3,1},{4,6},{6,4},{5,7},{7,5},{8,10},{10,8},{9,1... | collective-permute-start | bytes 442376 | tf_op jit(solution)/shard_map/ppermute | solution.py:33
  26.8 0.0 collective-permute-done.other_ref
  26.8 0.0 copy-start.1
  26.8 2.3 %copy-done.1 = bf16[4608,512]{1,0:T(8,128)(2,1)S(1)} copy-done((bf16[4608,512]{1,0:T(8,128)(2,1)S(1)}, bf16[4608,512]{1,0:T(8,128)(2,1)}, u32[]{:S(2)}) %copy-start.1) | copy-done | bytes 4718616
  29.1 2.4 %shard_map.95 = (f32[16,8,128]{2,1,0:T(8,128)}, f32[64,128]{1,0:T(8,128)S(1)}, bf16[272,512]{1,0:T(8,128)(2,1)S(1)}) custom-call(bf16[8,8,2432]{2,1,0:T(8,128)(2,1)S(1)} %all-to-all-done.own_ref, bf16[8,8,2432]{2,1,0:T(8,128)(2,1)S(1)} %collective-permute-done.other_ref, f32[2,4608]{1,0:T(2,128)S(1)} %pad_maximum_fusion.vec_ref, ...), custom_call_target="tpu_custom_call" | custom-call | tf_op jit(solution)/shard_map/pallas_call | solution.py:471
  31.5 3.8 %all-to-all-start.1 = ((f32[16,8,128]{2,1,0:T(8,128)}), f32[16,8,128]{2,1,0:T(8,128)S(1)}, u32[]{:S(2)}, u32[]{:S(2)}) async-start(f32[16,8,128]{2,1,0:T(8,128)} %get-tuple-element.11), calls=%async_computation.1 | async-start | bytes 131072 | tf_op jit(solution)/shard_map/all_to_all | solution.py:480
  35.3 0.0 copy-start.4
  35.3 6.1 %fusion.4.outer_ref = f32[272,4608]{1,0:T(8,128)} fusion(bf16[272,512]{1,0:T(8,128)(2,1)S(1)} %get-tuple-element.13, bf16[4608,512]{1,0:T(8,128)(2,1)} %head_ref.1), kind=kOutput, calls=%fused_computation.18 | convolution fusion | flops 1283457024 | bytes 10010624 | tf_op jit(solution)/shard_map/dot_general | solution.py:481
  41.4 0.0 collective-permute-done.3.refs_1_
  41.4 0.8 %all-to-all-done.1.theirs_ref = f32[16,8,128]{2,1,0:T(8,128)S(1)} async-done(((f32[16,8,128]{2,1,0:T(8,128)}), f32[16,8,128]{2,1,0:T(8,128)S(1)}, u32[]{:S(2)}, u32[]{:S(2)}) %all-to-all-start.1) | async-done | bytes 65568 | tf_op jit(solution)/shard_map/all_to_all | solution.py:480
  42.2 0.0 copy-start
  42.2 2.4 %copy-done = f32[272,4608]{1,0:T(8,128)S(1)} copy-done((f32[272,4608]{1,0:T(8,128)S(1)}, f32[272,4608]{1,0:T(8,128)}, u32[]{:S(2)}) %copy-start) | copy-done | bytes 5013528
  44.6 1.8 %shard_map.96 = (bf16[16,72,128]{2,1,0:T(8,128)(2,1)}, f32[18,128]{1,0:T(8,128)S(1)}, f32[8,128]{1,0:T(8,128)S(1)}) custom-call(f32[16,8,128]{2,1,0:T(8,128)S(1)} %all-to-all-done.1.theirs_ref, f32[64,128]{1,0:T(8,128)S(1)} %get-tuple-element.12.cols_ref, f32[272,4608]{1,0:T(8,128)S(1)} %copy-done, bf16[8,8,2432]{2,1,0:T(8,128)(2,1)S(1)} %all-to-all-done.own_ref, ...), custom_call_target="tpu_custom_call" | custom-call | tf_op jit(solution)/shard_map/pallas_call | solution.py:484
  46.4 5.2 %all-to-all-start.2 = ((bf16[16,72,128]{2,1,0:T(8,128)(2,1)}), bf16[16,72,128]{2,1,0:T(8,128)(2,1)S(1)}, u32[]{:S(2)}, u32[]{:S(2)}) async-start(bf16[16,72,128]{2,1,0:T(8,128)(2,1)} %get-tuple-element.15), calls=%async_computation.2 | async-start | bytes 589824 | tf_op jit(solution)/shard_map/all_to_all | solution.py:497
  51.6 0.6 slice_reduce_fusion
  52.3 9.9 %all-to-all-done.2.back_ref = bf16[16,72,128]{2,1,0:T(8,128)(2,1)S(1)} async-done(((bf16[16,72,128]{2,1,0:T(8,128)(2,1)}), bf16[16,72,128]{2,1,0:T(8,128)(2,1)S(1)}, u32[]{:S(2)}, u32[]{:S(2)}) %all-to-all-start.2) | async-done | bytes 294944 | tf_op jit(solution)/shard_map/all_to_all | solution.py:497
  62.2 0.0 copy-done.4
  62.2 0.7 %shard_map.97 = (f32[144,128]{1,0:T(8,128)}, f32[18,128]{1,0:T(8,128)}) custom-call(bf16[16,72,128]{2,1,0:T(8,128)(2,1)S(1)} %all-to-all-done.2.back_ref, f32[18,128]{1,0:T(8,128)S(1)} %bitcast.19, f32[18,128]{1,0:T(8,128)S(1)} %get-tuple-element.16.second_ref), custom_call_target="tpu_custom_call" | custom-call | tf_op jit(solution)/shard_map/pallas_call | solution.py:498
  (6 shorter events, 0.1 us)
Async XLA Ops:
  2.1 13.4 %collective-permute-start.1 = (f32[2,2304]{1,0:T(2,128)S(1)}, f32[2,2304]{1,0:T(2,128)S(1)}, u32[]{:S(2)}, u32[]{:S(2)}) collective-permute-start(f32[2,2304]{1,0:T(2,128)S(1)} %pad_maximum_fusion.1), channel_id=1, source_target_pairs={{0,2},{2,0},{1,3},{3,1},{4,6},{6,4},{5,7},{7,5},{8,10},{10,8},{9,1... | collective-permute-start | bytes 55304 | tf_op jit(solution)/shard_map/ppermute | solution.py:27
  6.1 19.1 %collective-permute-start.2 = (bf16[8,2,4608]{2,0,1:T(8,128)(2,1)S(1)}, bf16[8,2,4608]{2,0,1:T(8,128)(2,1)S(1)}, u32[]{:S(2)}, u32[]{:S(2)}) collective-permute-start(bf16[8,2,4608]{2,0,1:T(8,128)(2,1)S(1)} %get-tuple-element.21), channel_id=1, source_target_pairs={{0,1},{1,0},{2,3},{3,2},{4,5},{5,4},{6,7},{7,6},{8,9},{9,8},{10,11... | collective-permute-start | bytes 442376 | tf_op jit(solution)/shard_map/ppermute | solution.py:33
  6.2 1.0 %copy-start.2 = (bf16[8,18432]{1,0:T(8,128)(2,1)S(1)}, bf16[8,18432]{1,0:T(8,128)(2,1)}, u32[]{:S(2)}) copy-start(bf16[8,18432]{1,0:T(8,128)(2,1)} %hidden_ref.1) | copy-start | bytes 884740
  7.1 0.9 %copy-start.3 = (f32[18432]{0:T(1024)S(1)}, f32[18432]{0:T(1024)}, u32[]{:S(2)}) copy-start(f32[18432]{0:T(1024)} %param.9) | copy-start | bytes 221188
  8.0 0.8 %copy-start.5 = (bf16[8,2304]{1,0:T(8,128)(2,1)S(1)}, bf16[8,2304]{1,0:T(8,128)(2,1)}, u32[]{:S(2)}) copy-start(bf16[8,2304]{1,0:T(8,128)(2,1)} %base_ref.1) | copy-start | bytes 110596
  9.7 15.5 %all-to-all-start = ((bf16[8,8,2432]{2,1,0:T(8,128)(2,1)}), bf16[8,8,2432]{2,1,0:T(8,128)(2,1)S(1)}, u32[]{:S(2)}, u32[]{:S(2)}) async-start(bf16[8,8,2432]{2,1,0:T(8,128)(2,1)} %shard_map.94), calls=%async_computation | async-start | bytes 622592 | tf_op jit(solution)/shard_map/all_to_all | solution.py:453
  25.2 1.6 %collective-permute-start = (bf16[8,8,2432]{2,1,0:T(8,128)(2,1)S(1)}, bf16[8,8,2432]{2,1,0:T(8,128)(2,1)S(1)}, u32[]{:S(2)}, u32[]{:S(2)}) collective-permute-start(bf16[8,8,2432]{2,1,0:T(8,128)(2,1)S(1)} %all-to-all-done.own_ref), channel_id=1, source_target_pairs={{0,1},{1,0},{2,3},{3,2},{4,5},{5,4},{6,7},{7,6},{8,9},{9,8},{10,11... | collective-permute-start | bytes 933896 | tf_op jit(solution)/shard_map/ppermute | solution.py:454
  25.2 16.1 %collective-permute-start.3 = (bf16[16,4608]{1,0:T(8,128)(2,1)S(1)}, bf16[16,4608]{1,0:T(8,128)(2,1)S(1)}, u32[]{:S(2)}, u32[]{:S(2)}) collective-permute-start(bf16[16,4608]{1,0:T(8,128)(2,1)S(1)} %get-tuple-element.19), channel_id=1, source_target_pairs={{0,2},{2,0},{1,3},{3,1},{4,6},{6,4},{5,7},{7,5},{8,10},{10,8},{9,1... | collective-permute-start | bytes 442376 | tf_op jit(solution)/shard_map/ppermute | solution.py:33
  26.8 2.3 %copy-start.1 = (bf16[4608,512]{1,0:T(8,128)(2,1)S(1)}, bf16[4608,512]{1,0:T(8,128)(2,1)}, u32[]{:S(2)}) copy-start(bf16[4608,512]{1,0:T(8,128)(2,1)} %head_ref.1) | copy-start | bytes 14155780
  31.5 10.7 %all-to-all-start.1 = ((f32[16,8,128]{2,1,0:T(8,128)}), f32[16,8,128]{2,1,0:T(8,128)S(1)}, u32[]{:S(2)}, u32[]{:S(2)}) async-start(f32[16,8,128]{2,1,0:T(8,128)} %get-tuple-element.11), calls=%async_computation.1 | async-start | bytes 131072 | tf_op jit(solution)/shard_map/all_to_all | solution.py:480
  35.3 27.0 %copy-start.4 = (f32[2304]{0:T(1024)S(1)}, f32[2304]{0:T(1024)}, u32[]{:S(2)}) copy-start(f32[2304]{0:T(1024)} %param.11) | copy-start | bytes 27652
  42.2 2.4 %copy-start = (f32[272,4608]{1,0:T(8,128)S(1)}, f32[272,4608]{1,0:T(8,128)}, u32[]{:S(2)}) copy-start(f32[272,4608]{1,0:T(8,128)} %fusion.4.outer_ref) | copy-start | bytes 15040516
  46.4 15.8 %all-to-all-start.2 = ((bf16[16,72,128]{2,1,0:T(8,128)(2,1)}), bf16[16,72,128]{2,1,0:T(8,128)(2,1)S(1)}, u32[]{:S(2)}, u32[]{:S(2)}) async-start(bf16[16,72,128]{2,1,0:T(8,128)(2,1)} %get-tuple-element.15), calls=%async_computation.2 | async-start | bytes 589824 | tf_op jit(solution)/shard_map/all_to_all | solution.py:497

commit v3 on v2

--- a/solution.py
+++ b/solution.py
@@ -181,9 +181,25 @@
     return (penalty.reshape(rows), grad_in, grad_out)
 
 
-def send_kernel(copies, base_ref, hidden_ref, in_ref, packed_ref):
+def send_kernel(copies, pieces, base_hbm, hidden_hbm, in_hbm, out_hbm, gain_hbm, packed_hbm, vec_ref, keep_ref, give_ref, base_ref, hidden_ref, in_ref, packed_ref, sems):
     rows, hidden = hidden_ref.shape
     feat = base_ref.shape[1]
+    quarter = hidden // (2 * pieces)
+    get_hidden = pltpu.make_async_copy(hidden_hbm, hidden_ref, sems.at[0])
+    get_in = pltpu.make_async_copy(in_hbm, in_ref, sems.at[1])
+    get_base = pltpu.make_async_copy(base_hbm, base_ref, sems.at[2])
+    get_out = pltpu.make_async_copy(out_hbm, vec_ref.at[0], sems.at[3])
+    get_gain = pltpu.make_async_copy(gain_hbm, vec_ref.at[1], sems.at[4])
+    get_hidden.start()
+    get_in.start()
+    get_base.start()
+    get_out.start()
+    get_gain.start()
+    get_base.wait()
+    for i in range(copies):
+        packed_ref[i, :, :feat] = base_ref[...]
+    get_hidden.wait()
+    get_in.wait()
     total = jnp.zeros((rows, 128), f32)
     for c in range(0, hidden, 128):
         total += hidden_ref[:, c : c + 128].astype(f32) * in_ref[:, c : c + 128]
@@ -196,17 +212,50 @@
         mix = mix - piece
     cols = cols.astype(bf16)
     for i in range(copies):
-        packed_ref[i, :, :feat] = base_ref[...]
         packed_ref[i, :, feat:] = cols
-
-
-def score_kernel(nv, nm, own_ref, other_ref, vec_ref, ids_ref, head_ref, slab_ref, cols_ref, ops_ref, x_ref):
+    put = pltpu.make_async_copy(packed_ref, packed_hbm, sems.at[5])
+    put.start()
+    r_i = lax.axis_index("rep")
+    for i in range(pieces):
+        for ref, r in ((keep_ref, r_i), (give_ref, 1 - r_i)):
+            start = pl.multiple_of((2 * i + r) * quarter, 128)
+            ref[i] = hidden_ref[:, pl.ds(start, quarter)]
+    get_out.wait()
+    get_gain.wait()
+    put.wait()
+
+
+def stage_kernel(after_ref, head_hbm, head_ref, sems):
+    copies = sems.shape[0]
+    part = head_ref.shape[0] // copies
+    moves = []
+    for i in range(copies):
+        span = pl.ds(i * part, part)
+        moves.append(pltpu.make_async_copy(head_hbm.at[span], head_ref.at[span], sems.at[i]))
+        moves[-1].start()
+    for move in moves:
+        move.wait()
+
+
+def score_kernel(nv, nm, own_ref, other_ref, vec_ref, ids_ref, early_ref, head_hbm, slab_hbm, cols_ref, ops_hbm, x_ref, slab_ref, ops_ref, late_ref, sems):
     rows = own_ref.shape[1]
     feat = own_ref.shape[2] - 128
-    model, voc = head_ref.shape
+    model, voc = head_hbm.shape
     pair = 2 * rows
     group = 2 * nv * rows
     half = group // 2
+
+    early = early_ref.shape[0]
+    part = (model - early) // 2
+    moves = []
+    for i in range(2):
+        move = pltpu.make_async_copy(
+            head_hbm.at[pl.ds(early + i * part, part)],
+            late_ref.at[pl.ds(i * part, part)],
+            sems.at[2 + i],
+        )
+        move.start()
+        moves.append(move)
 
     lane_t = lax.broadcasted_iota(jnp.int32, (pair, 128), 1)
     for k, got_ref in enumerate((own_ref, other_ref)):
@@ -228,8 +277,7 @@
             dot_o = jnp.zeros((pair, 128), f32)
             for m in range(nm):
                 for c in range(0, feat, 128):
-                    d = m * feat + c
-                    out = vec_ref[0:1, d : d + 128]
+                    out = vec_ref[m, 0, c // 128 : c // 128 + 1, :]
                     b = tile(m, c)
                     e = b + mix_b * out
                     sq_b += b * b
@@ -246,15 +294,17 @@
             for m in range(nm):
                 for c in range(0, feat, 128):
                     d = m * feat + c
-                    out = vec_ref[0:1, d : d + 128]
-                    gain = vec_ref[1:2, d : d + 128]
+                    t = c // 128
+                    out = vec_ref[m, 0, t : t + 1, :]
+                    gain = vec_ref[m, 1, t : t + 1, :]
                     b = tile(m, c)
                     e = b + mix_b * out
                     x_ref[at : at + pair, d : d + 128] = (e * scale_e * gain).astype(bf16)
                     x_ref[group + at : group + at + pair, d : d + 128] = (b * scale_b * gain).astype(bf16)
     sub = lax.broadcasted_iota(jnp.int32, (16, 128), 0)
     for d in range(0, model, 128):
-        rest = vec_ref[0:1, d : d + 128] * vec_ref[1:2, d : d + 128]
+        m, t = d // feat, d % feat // 128
+        rest = vec_ref[m, 0, t : t + 1, :] * vec_ref[m, 1, t : t + 1, :]
         block = jnp.zeros((16, 128), f32)
         for i in range(3):
             piece = rest.astype(bf16).astype(f32)
@@ -262,7 +312,10 @@
             rest = rest - piece
         x_ref[2 * group :, d : d + 128] = block.astype(bf16)
 
-    pre = jnp.dot(x_ref[...], head_ref[...], preferred_element_type=f32)
+    pre = jnp.dot(x_ref[:, :early], early_ref[...], preferred_element_type=f32)
+    for move in moves:
+        move.wait()
+    pre += jnp.dot(x_ref[:, early:], late_ref[...], preferred_element_type=f32)
     pre_edit = pre[:group]
     pre_base = pre[group : 2 * group]
     toward = jnp.sum(pre[2 * group :], axis=0, keepdims=True)
@@ -308,6 +361,8 @@
     table = table.T[:8]
     for p in range(slab_ref.shape[0]):
         slab_ref[p] = table
+    put_slab = pltpu.make_async_copy(slab_ref, slab_hbm, sems.at[0])
+    put_slab.start()
 
     high_e = pe.astype(bf16)
     high_b = pb.astype(bf16)
@@ -324,11 +379,39 @@
         block = jnp.where(sub == i, piece, block)
         rest = rest - piece
     ops_ref[4 * group :] = block.astype(bf16)
-
-
-def close_kernel(nv, nm, theirs_ref, cols_ref, outer_ref, own_ref, other_ref, out_ref, *refs):
+    put_ops = pltpu.make_async_copy(ops_ref, ops_hbm, sems.at[1])
+    put_ops.start()
+    put_slab.wait()
+    put_ops.wait()
+
+
+def outer_kernel(ops_hbm, head_hbm, outer_ref, ops_ref, head_ref, sems):
+    both = outer_ref.shape[0] - 16
+    part = 512
+    get = pltpu.make_async_copy(ops_hbm, ops_ref, sems.at[0])
+    get.start()
+    moves = []
+    for i in range(head_hbm.shape[0] // part):
+        span = pl.ds(i * part, part)
+        moves.append(pltpu.make_async_copy(head_hbm.at[span], head_ref.at[span], sems.at[1 + i]))
+        moves[i].start()
+    get.wait()
+    for i, move in enumerate(moves):
+        move.wait()
+        c = i * part
+        block = lax.dot_general(
+            ops_ref[...],
+            head_ref[c : c + part, :],
+            (((1,), (1,)), ((), ())),
+            preferred_element_type=f32,
+        )
+        outer_ref[:both, c : c + part] = block[:both] + block[both : 2 * both]
+        outer_ref[both:, c : c + part] = block[2 * both :]
+
+
+def close_kernel(nv, nm, theirs_ref, cols_ref, outer_ref, own_ref, all_ref, *refs):
     units = refs[:nm]
-    slab_ref, second_ref, penalty_ref, coeff_ref, pen_ref, vec_ref = refs[nm:]
+    slab_hbm, penalty_hbm, coeff_ref, pen_ref, pull_ref, vec_ref, slab_ref, second_ref, sems = refs[nm:]
     rows = own_ref.shape[1]
     feat = own_ref.shape[2] - 128
     model = outer_ref.shape[1]
@@ -365,17 +448,33 @@
     pull = weight * shrink
     coeff_ref[...] = jnp.broadcast_to(coeff, (group, 128))
     pen_ref[...] = jnp.broadcast_to(penalty, (group, 128))
-    penalty_ref[...] = pen_ref[pl.ds(pl.multiple_of(v_i * rows, rows), rows), :]
+    put_pen = pltpu.make_async_copy(
+        pen_ref.at[pl.ds(pl.multiple_of(v_i * rows, rows), rows)], penalty_hbm, sems.at[0]
+    )
+    put_pen.start()
+
+    pull_ref[...] = jnp.broadcast_to(pull, (group, 128))
+    pulls = pull_ref[pl.ds(pl.multiple_of(v_i * rows, rows), rows), :]
+    pull_ref[...] = jnp.broadcast_to(pull * mix, (group, 128))
+    pulled = jnp.sum(pull_ref[pl.ds(pl.multiple_of(v_i * rows, rows), rows), :], axis=0, keepdims=True)
+    for t in range(tiles):
+        part = own_ref[v_i * nm + m_i, :, t * 128 : (t + 1) * 128].astype(f32) * pulls
+        second_ref[t : t + 1, :] = (
+            jnp.sum(part, axis=0, keepdims=True) + pulled * all_ref[m_i, 0, t : t + 1, :]
+        )
 
     by_e = jnp.broadcast_to(weight * inv_e, (group, 128))
     by_b = jnp.broadcast_to(weight * inv_b, (group, 128))
     for m in range(nm):
         for t in range(tiles):
             d = m * feat + t * 128
-            plus = (outer_ref[:group, d : d + 128] + outer_ref[2 * group : 3 * group, d : d + 128]) * by_e
-            less = (outer_ref[group : 2 * group, d : d + 128] + outer_ref[3 * group : 4 * group, d : d + 128]) * by_b
+            plus = outer_ref[:group, d : d + 128] * by_e
+            less = outer_ref[group : 2 * group, d : d + 128] * by_b
             row = jnp.sum(plus - less, axis=0, keepdims=True)
-            row -= jnp.sum(outer_ref[4 * group :, d : d + 128], axis=0, keepdims=True)
+            row -= jnp.sum(outer_ref[2 * group :, d : d + 128], axis=0, keepdims=True)
+            row = row * all_ref[m, 1, t : t + 1, :] - jnp.where(
+                m_i == m, second_ref[t : t + 1, :], 0.0
+            )
             high = row.astype(bf16).astype(f32)
             vec_ref[m, t : t + 1, :] = high
             vec_ref[m, tiles + t : tiles + t + 1, :] = row - high
@@ -396,24 +495,16 @@
         for v in range(nv):
             for r in range(2):
                 slab_ref[(v * nm + m) * 2 + r] = block
-
-    by_p = jnp.broadcast_to(pull, (group, 128))
-    pulled = jnp.sum(pull * mix, axis=0, keepdims=True)
-    for t in range(tiles):
-        c = t * 128
-        part = jnp.zeros((rows, 128), f32)
-        for k, got_ref in enumerate((own_ref, other_ref)):
-            for v in range(nv):
-                at = (k * nv + v) * rows
-                part += got_ref[v * nm + m_i, :, c : c + 128].astype(f32) * by_p[at : at + rows]
-        second_ref[t : t + 1, :] = (
-            jnp.sum(part, axis=0, keepdims=True) + pulled * out_ref[:, c : c + 128]
-        )
-
-
-def sum_kernel(back_ref, gain_ref, second_ref, in_ref, out_ref):
+    put_slab = pltpu.make_async_copy(slab_ref, slab_hbm, sems.at[1])
+    put_slab.start()
+
+    put_pen.wait()
+    put_slab.wait()
+
+
+def sum_kernel(back_ref, in_ref, out_ref):
     peers = back_ref.shape[0]
-    tiles = gain_ref.shape[0]
+    tiles = out_ref.shape[0]
     units = back_ref.shape[1] - 2 * tiles
     pieces = in_ref.shape[0] // units
     wide = jnp.zeros((tiles, 128), f32)
@@ -423,15 +514,20 @@
             total += back_ref[p].astype(f32)
         wide += total[:tiles] + total[tiles : 2 * tiles]
         in_ref[q * units : (q + 1) * units, :] = total[2 * tiles :]
-    out_ref[...] = gain_ref[...] * wide - second_ref[...]
-
-
-def call(kernel, out_shape, scratch=()):
+    out_ref[...] = wide
+
+
+def in_hbm(value):
+    return pltpu.with_memory_space_constraint(value, pltpu.HBM)
+
+
+def call(kernel, out_shape, scratch=(), megabytes=6, **more):
     return pl.pallas_call(
         kernel,
         out_shape=out_shape,
         scratch_shapes=scratch,
-        compiler_params=pltpu.CompilerParams(vmem_limit_bytes=40 << 20),
+        compiler_params=pltpu.CompilerParams(vmem_limit_bytes=megabytes << 20),
+        **more,
     )
 
 
@@ -447,57 +543,108 @@
     r_i = lax.axis_index("rep")
     shape = jax.ShapeDtypeStruct
 
-    packed = call(
-        functools.partial(send_kernel, nv * nm), shape((nv * nm, rows, feat + 128), bf16)
-    )(resid_base, mlp_hidden, edit_in.reshape(1, hidden))
+    tiles = feat // 128
+    hbm = pl.BlockSpec(memory_space=pltpu.HBM)
+    vmem = pl.BlockSpec(memory_space=pltpu.VMEM)
+    out_tiles = edit_out.reshape(tiles, 128)
+    gain_tiles = norm_gain.reshape(tiles, 128)
+
+    early = model // 2
+
+    packed, vectors, keep, give = call(
+        functools.partial(send_kernel, nv * nm, nm),
+        (
+            pltpu.HBM((nv * nm, rows, feat + 128), bf16),
+            shape((2, tiles, 128), f32),
+            shape((nm, rows, quarter), bf16),
+            shape((nm, rows, quarter), bf16),
+        ),
+        [
+            pltpu.VMEM((rows, feat), bf16),
+            pltpu.VMEM((rows, hidden), bf16),
+            pltpu.VMEM((1, hidden), f32),
+            pltpu.VMEM((nv * nm, rows, feat + 128), bf16),
+            pltpu.SemaphoreType.DMA((6,)),
+        ],
+        in_specs=[hbm] * 5,
+        out_specs=(hbm, vmem, vmem, vmem),
+    )(
+        *(
+            in_hbm(a)
+            for a in (resid_base, mlp_hidden, edit_in.reshape(1, hidden), out_tiles, gain_tiles)
+        )
+    )
     got = lax.all_to_all(packed, ("vocab", "mp"), 0, 0)
     other = lax.ppermute(got, "rep", [(0, 1), (1, 0)])
-
-    vectors = from_peers(jnp.stack([edit_out, norm_gain]), "mp", nm)
-    vectors = jnp.concatenate(in_order(vectors, m_i), axis=1)
+    vectors = from_peers(vectors, "mp", nm)
+    staged = call(
+        stage_kernel,
+        pltpu.VMEM((early, voc), bf16),
+        [pltpu.SemaphoreType.DMA((4,))],
+        in_specs=[vmem, hbm],
+        out_specs=vmem,
+    )(got, in_hbm(head))
+    vectors = jnp.stack(in_order(vectors, m_i))
     ids = token_ids.reshape(nv, nr, rows)
     ids = jnp.concatenate(
         [lax.dynamic_index_in_dim(ids, (r_i + k) % nr, 1, keepdims=False) for k in range(nr)]
     ).reshape(group, 1)
 
-    units = mlp_hidden.reshape(rows, nm, nr, quarter)
-    units = jnp.concatenate(
-        to_peers(lambda r: lax.dynamic_index_in_dim(units, r, 2, keepdims=False), "rep", nr, r_i)
-    )
+    units = jnp.concatenate([keep, lax.ppermute(give, "rep", [(0, 1), (1, 0)])], axis=1)
     units = to_peers(
-        lambda m: lax.dynamic_index_in_dim(units, m, 1, keepdims=False), "mp", nm, m_i
-    )
-
+        lambda m: lax.dynamic_index_in_dim(units, m, 0, keepdims=False), "mp", nm, m_i
+    )
     slab, cols, ops = call(
         functools.partial(score_kernel, nv, nm),
         (
-            shape((peers, 8, 128), f32),
+            pltpu.HBM((peers, 8, 128), f32),
             shape((group, 128), f32),
-            shape((4 * group + 16, voc), bf16),
+            pltpu.HBM((4 * group + 16, voc), bf16),
         ),
-        [pltpu.VMEM((2 * group + 16, model), bf16)],
-    )(got, other, vectors, ids, head)
+        [
+            pltpu.VMEM((2 * group + 16, model), bf16),
+            pltpu.VMEM((peers, 8, 128), f32),
+            pltpu.VMEM((4 * group + 16, voc), bf16),
+            pltpu.VMEM((model - early, voc), bf16),
+            pltpu.SemaphoreType.DMA((4,)),
+        ],
+        8,
+        in_specs=[vmem] * 5 + [hbm],
+        out_specs=(hbm, vmem, hbm),
+    )(got, other, vectors, ids, staged, in_hbm(head))
     theirs = lax.all_to_all(slab, everyone, 0, 0)
-    outer = lax.dot_general(ops, head, (((1,), (1,)), ((), ())), preferred_element_type=f32)
+    outer = call(
+        outer_kernel,
+        shape((2 * group + 16, model), f32),
+        [
+            pltpu.VMEM((4 * group + 16, voc), bf16),
+            pltpu.VMEM((model, voc), bf16),
+            pltpu.SemaphoreType.DMA((1 + model // 512,)),
+        ],
+        12,
+        in_specs=[hbm, hbm],
+    )(in_hbm(ops), in_hbm(head))
 
     width = (2 * feat + quarter) // 128
-    slab, second, penalty = call(
+    slab, penalty = call(
         functools.partial(close_kernel, nv, nm),
-        (
-            shape((peers, width, 128), bf16),
-            shape((feat // 128, 128), f32),
-            shape((rows, 128), f32),
-        ),
+        (pltpu.HBM((peers, width, 128), bf16), pltpu.HBM((rows, 128), f32)),
         [
             pltpu.VMEM((group, 128), f32),
             pltpu.VMEM((group, 128), f32),
+            pltpu.VMEM((group, 128), f32),
             pltpu.VMEM((nm, width, 128), f32),
+            pltpu.VMEM((peers, width, 128), bf16),
+            pltpu.VMEM((tiles, 128), f32),
+            pltpu.SemaphoreType.DMA((2,)),
         ],
-    )(theirs, cols, outer, got, other, edit_out.reshape(1, feat), *units)
+        in_specs=[vmem] * (5 + nm),
+        out_specs=(hbm, hbm),
+    )(theirs, cols, outer, got, vectors, *units)
     back = lax.all_to_all(slab, everyone, 0, 0)
     grad_in, grad_out = call(
-        sum_kernel, (shape((hidden // 128, 128), f32), shape((feat // 128, 128), f32))
-    )(back, norm_gain.reshape(feat // 128, 128), second)
+        sum_kernel, (shape((hidden // 128, 128), f32), shape((tiles, 128), f32))
+    )(back)
     return (penalty[:, 0], grad_in.reshape(hidden), grad_out.reshape(feat))
 
 

time: 63.6 us -> 54.5 us (0.86)
  local copies, waits for them, and re-layouts: 11.2 us -> 2.85 us
  Pallas kernels: 5.81 us -> 13.8 us
  matrix products: 6.08 us -> 0 us
  waiting for transfers between devices: 20.4 us -> 18.8 us
  starting transfers between devices: 18.5 us -> 17.8 us
    pallas_call x4 -> x6, Pallas kernels: 5.81 us -> 13.8 us  [the longest x1 4.3 us: fused(): call(outer_kernel, shape((2 * group + 16, model), f32), [pltpu.VMEM((4 *...]
    unnamed x12 -> x1, local copies, waits for them, and re-layouts: 7.37 us -> 0.01 us
    dot_general x1 -> x0, matrix products: 6.08 us -> none  [fused(): lax.dot_general(ops, head, (((1,), (1,)), ((), ())), preferred_element_ty...]
    all_to_all x1, waiting for transfers between devices: 9.63 us -> 4.74 us  [fused(): got = lax.all_to_all(packed, ('vocab', 'mp'), 0, 0)]
    all_to_all x1, starting transfers between devices: 4.88 us -> 7.26 us  [fused(): got = lax.all_to_all(packed, ('vocab', 'mp'), 0, 0)]
    ppermute x1, waiting for transfers between devices: 0.01 us -> 2.25 us  [from_peers(): lax.ppermute(value, axis, moves[k])]
    all_to_all x1, waiting for transfers between devices: 0.8 us -> 2.54 us  [fused(): theirs = lax.all_to_all(slab, everyone, 0, 0)]
    all_to_all x1, starting transfers between devices: 5.22 us -> 3.55 us  [fused(): back = lax.all_to_all(slab, everyone, 0, 0)]
  transfers between devices with their start and end apart: 7 -> 7, of which waited for: 3 -> 4; matrix products, arithmetic and copies ran while one was open for 14% -> 5% of each run, Pallas kernels for 5% -> 18%
where the time goes in v3:
time: 54.5 us; the launch traced here: 54 us
  waiting for transfers between devices  18.8 us (34%)
  starting transfers between devices  17.8 us (33%)
  Pallas kernels  13.8 us (25%)
  local copies, waits for them, and re-layouts  2.85 us (5%)
  between operations  0.8 us (1%)
    all_to_all x1, waiting for transfers between devices, fused(): back = lax.all_to_all(slab, everyone, 0, 0)  9.22 us
    all_to_all x1, starting transfers between devices, fused(): got = lax.all_to_all(packed, ('vocab', 'mp'), 0, 0)  7.26 us
    all_to_all x1, waiting for transfers between devices, fused(): got = lax.all_to_all(packed, ('vocab', 'mp'), 0, 0)  4.74 us
    pallas_call x1, Pallas kernels, fused(): call(outer_kernel, shape((2 * group + 16, model), f32), [pltpu.VMEM((4 *...  4.3 us
    pallas_call x1, Pallas kernels, fused(): call(functools.partial(score_kernel, nv, nm), (pltpu.HBM((peers, 8, 128),...  3.58 us
    all_to_all x1, starting transfers between devices, fused(): back = lax.all_to_all(slab, everyone, 0, 0)  3.55 us
    all_to_all x1, starting transfers between devices, fused(): theirs = lax.all_to_all(slab, everyone, 0, 0)  3.51 us
    all_to_all x1, waiting for transfers between devices, fused(): theirs = lax.all_to_all(slab, everyone, 0, 0)  2.54 us
  transfers between devices with their start and end apart: 7, of which 4 were waited for; matrix products, arithmetic and copies ran while one was open for 5% of the time, Pallas kernels for 18%

profile of v3, /device:TPU:0, one launch (start us, length us, event | category | flops | bytes accessed | tf_op | source)
XLA Modules:
  0.0 54.0 jit_solution(11651015048162239015)
XLA Ops:
  0.6 2.0 %shard_map.94 = (bf16[8,8,2432]{2,1,0:T(8,128)(2,1)}, f32[2,18,128]{2,1,0:T(8,128)S(1)}, bf16[2,8,4608]{2,1,0:T(8,128)(2,1)S(1)}, bf16[2,8,4608]{2,1,0:T(8,128)(2,1)S(1)}) custom-call(bf16[8,2304]{1,0:T(8,128)(2,1)} %base_hbm.1, bf16[8,18432]{1,0:T(8,128)(2,1)} %hidden_hbm.1, f32[1,18432]{1,0:T(1,128)} %bitcast.15, f32[18,128]{1,0:T(8,128)} %bitcast.16, ...), custom_call_target="tpu_custom_call" | custom-call | tf_op jit(solution)/shard_map/pallas_call | solution.py:554
  2.6 7.3 %all-to-all-start = ((bf16[8,8,2432]{2,1,0:T(8,128)(2,1)}), bf16[8,8,2432]{2,1,0:T(8,128)(2,1)S(1)}, u32[]{:S(2)}, u32[]{:S(2)}) async-start(bf16[8,8,2432]{2,1,0:T(8,128)(2,1)} %get-tuple-element.14), calls=%async_computation | async-start | bytes 622592 | tf_op jit(solution)/shard_map/all_to_all | solution.py:577
  9.9 2.0 %collective-permute-start.1 = (f32[2,18,128]{2,1,0:T(8,128)S(1)}, f32[2,18,128]{2,1,0:T(8,128)S(1)}, u32[]{:S(2)}, u32[]{:S(2)}) collective-permute-start(f32[2,18,128]{2,1,0:T(8,128)S(1)} %get-tuple-element.15), channel_id=1, source_target_pairs={{0,2},{2,0},{1,3},{3,1},{4,6},{6,4},{5,7},{7,5},{8,10},{10,8},{9,1... | collective-permute-start | bytes 55304 | tf_op jit(solution)/shard_map/ppermute | solution.py:27
  11.9 0.0 collective-permute-start.2
  11.9 0.7 %reshape.30 = s32[4,2,8]{2,1,0:T(2,128)S(1)} reshape(s32[64]{0:T(128)} %param.13) | data formatting | bytes 512 | tf_op jit(solution)/shard_map/reshape | solution.py:588
  12.7 0.1 reshape.34.ids_ref
  12.8 2.2 %collective-permute-done.1 = f32[2,18,128]{2,1,0:T(8,128)S(1)} collective-permute-done((f32[2,18,128]{2,1,0:T(8,128)S(1)}, f32[2,18,128]{2,1,0:T(8,128)S(1)}, u32[]{:S(2)}, u32[]{:S(2)}) %collective-permute-start.1) | collective-permute-done | bytes 18464 | tf_op jit(solution)/shard_map/ppermute | solution.py:27
  15.1 0.0 collective-permute-done.2
  15.1 4.7 %all-to-all-done.after_ref.own_ref = bf16[8,8,2432]{2,1,0:T(8,128)(2,1)S(1)} async-done(((bf16[8,8,2432]{2,1,0:T(8,128)(2,1)}), bf16[8,8,2432]{2,1,0:T(8,128)(2,1)S(1)}, u32[]{:S(2)}, u32[]{:S(2)}) %all-to-all-start) | async-done | bytes 311328 | tf_op jit(solution)/shard_map/all_to_all | solution.py:577
  19.8 0.0 collective-permute-start
  19.8 0.7 %dynamic-slice_bitcast_fusion = (bf16[16,4608]{1,0:T(8,128)(2,1)}, bf16[16,4608]{1,0:T(8,128)(2,1)S(1)}) fusion(bf16[2,16,4608]{2,1,0:T(8,128)(2,1)S(1)} %constant_dynamic-update-slice_fusion, s32[]{:T(128)S(6)} %select_n.63, s32[]{:T(128)S(6)} %select_n.61), kind=kLoop, calls=%fused_computation | loop fusion | bytes 589832 | tf_op jit(solution)/shard_map/jit(dynamic_index_in_dim)/squeeze | solution.py:595
  20.5 1.4 %collective-permute-start.3 = (bf16[16,4608]{1,0:T(8,128)(2,1)}, bf16[16,4608]{1,0:T(8,128)(2,1)S(1)}, u32[]{:S(2)}, u32[]{:S(2)}) collective-permute-start(bf16[16,4608]{1,0:T(8,128)(2,1)} %get-tuple-element.25), channel_id=1, source_target_pairs={{0,2},{2,0},{1,3},{3,1},{4,6},{6,4},{5,7},{7,5},{8,10},{10,8},{9,1... | collective-permute-start | bytes 442376 | tf_op jit(solution)/shard_map/ppermute | solution.py:33
  22.0 1.6 %shard_map.95.early_ref = bf16[2304,512]{1,0:T(8,128)(2,1)S(1)} custom-call(bf16[8,8,2432]{2,1,0:T(8,128)(2,1)S(1)} %all-to-all-done.after_ref.own_ref, bf16[4608,512]{1,0:T(8,128)(2,1)} %head_hbm.5), custom_call_target="tpu_custom_call" | custom-call | tf_op jit(solution)/shard_map/pallas_call | solution.py:580
  23.6 0.0 collective-permute-done.other_ref
  23.6 3.6 %shard_map.96 = (f32[16,8,128]{2,1,0:T(8,128)}, f32[64,128]{1,0:T(8,128)S(1)}, bf16[272,512]{1,0:T(8,128)(2,1)}) custom-call(bf16[8,8,2432]{2,1,0:T(8,128)(2,1)S(1)} %all-to-all-done.after_ref.own_ref, bf16[8,8,2432]{2,1,0:T(8,128)(2,1)S(1)} %collective-permute-done.other_ref, f32[2,2,18,128]{3,2,1,0:T(8,128)S(1)} %pad_maximum_fusion.vec_ref.all_ref, ...), custom_call_target="tpu_custom_call" | custom-call | tf_op jit(solution)/shard_map/pallas_call | solution.py:597
  27.2 3.5 %all-to-all-start.1 = ((f32[16,8,128]{2,1,0:T(8,128)}), f32[16,8,128]{2,1,0:T(8,128)S(1)}, u32[]{:S(2)}, u32[]{:S(2)}) async-start(f32[16,8,128]{2,1,0:T(8,128)} %get-tuple-element.16), calls=%async_computation.1 | async-start | bytes 131072 | tf_op jit(solution)/shard_map/all_to_all | solution.py:615
  30.7 4.3 %shard_map.97.outer_ref = f32[144,4608]{1,0:T(8,128)S(1)} custom-call(bf16[272,512]{1,0:T(8,128)(2,1)} %get-tuple-element.18.ops_hbm, bf16[4608,512]{1,0:T(8,128)(2,1)} %head_hbm.5), custom_call_target="tpu_custom_call" | custom-call | tf_op jit(solution)/shard_map/pallas_call | solution.py:616
  35.0 0.0 collective-permute-done.3.refs_1_
  35.0 2.5 %all-to-all-done.1.theirs_ref = f32[16,8,128]{2,1,0:T(8,128)S(1)} async-done(((f32[16,8,128]{2,1,0:T(8,128)}), f32[16,8,128]{2,1,0:T(8,128)S(1)}, u32[]{:S(2)}, u32[]{:S(2)}) %all-to-all-start.1) | async-done | bytes 65568 | tf_op jit(solution)/shard_map/all_to_all | solution.py:615
  37.6 1.7 %shard_map.98 = (bf16[16,72,128]{2,1,0:T(8,128)(2,1)}, f32[8,128]{1,0:T(8,128)}) custom-call(f32[16,8,128]{2,1,0:T(8,128)S(1)} %all-to-all-done.1.theirs_ref, f32[64,128]{1,0:T(8,128)S(1)} %get-tuple-element.17.cols_ref, f32[144,4608]{1,0:T(8,128)S(1)} %shard_map.97.outer_ref, bf16[8,8,2432]{2,1,0:T(8,128)(2,1)S(1)} %all-to-all-done.after_ref.own_ref, ...), custom_call_target="tpu_custom_call" | custom-call | tf_op jit(solution)/shard_map/pallas_call | solution.py:629
  39.3 3.5 %all-to-all-start.2 = ((bf16[16,72,128]{2,1,0:T(8,128)(2,1)}), bf16[16,72,128]{2,1,0:T(8,128)(2,1)S(1)}, u32[]{:S(2)}, u32[]{:S(2)}) async-start(bf16[16,72,128]{2,1,0:T(8,128)(2,1)} %get-tuple-element.22), calls=%async_computation.2 | async-start | bytes 589824 | tf_op jit(solution)/shard_map/all_to_all | solution.py:644
  42.8 1.3 %slice_reduce_fusion = f32[8]{0:T(128)} fusion(f32[8,128]{1,0:T(8,128)} %get-tuple-element.21), kind=kLoop, calls=%fused_computation.8 | loop fusion | bytes 64 | tf_op jit(solution)/shard_map/slice | solution.py:648
  44.1 9.2 %all-to-all-done.2.back_ref = bf16[16,72,128]{2,1,0:T(8,128)(2,1)S(1)} async-done(((bf16[16,72,128]{2,1,0:T(8,128)(2,1)}), bf16[16,72,128]{2,1,0:T(8,128)(2,1)S(1)}, u32[]{:S(2)}, u32[]{:S(2)}) %all-to-all-start.2) | async-done | bytes 294944 | tf_op jit(solution)/shard_map/all_to_all | solution.py:644
  53.3 0.7 %shard_map.99 = (f32[144,128]{1,0:T(8,128)}, f32[18,128]{1,0:T(8,128)}) custom-call(bf16[16,72,128]{2,1,0:T(8,128)(2,1)S(1)} %all-to-all-done.2.back_ref), custom_call_target="tpu_custom_call" | custom-call | tf_op jit(solution)/shard_map/pallas_call | solution.py:645
  (6 shorter events, 0.1 us)
Async XLA Ops:
  2.6 17.2 %all-to-all-start = ((bf16[8,8,2432]{2,1,0:T(8,128)(2,1)}), bf16[8,8,2432]{2,1,0:T(8,128)(2,1)S(1)}, u32[]{:S(2)}, u32[]{:S(2)}) async-start(bf16[8,8,2432]{2,1,0:T(8,128)(2,1)} %get-tuple-element.14), calls=%async_computation | async-start | bytes 622592 | tf_op jit(solution)/shard_map/all_to_all | solution.py:577
  9.9 5.2 %collective-permute-start.1 = (f32[2,18,128]{2,1,0:T(8,128)S(1)}, f32[2,18,128]{2,1,0:T(8,128)S(1)}, u32[]{:S(2)}, u32[]{:S(2)}) collective-permute-start(f32[2,18,128]{2,1,0:T(8,128)S(1)} %get-tuple-element.15), channel_id=1, source_target_pairs={{0,2},{2,0},{1,3},{3,1},{4,6},{6,4},{5,7},{7,5},{8,10},{10,8},{9,1... | collective-permute-start | bytes 55304 | tf_op jit(solution)/shard_map/ppermute | solution.py:27
  11.9 3.2 %collective-permute-start.2 = (bf16[2,8,4608]{2,1,0:T(8,128)(2,1)S(1)}, bf16[2,8,4608]{2,1,0:T(8,128)(2,1)S(1)}, u32[]{:S(2)}, u32[]{:S(2)}) collective-permute-start(bf16[2,8,4608]{2,1,0:T(8,128)(2,1)S(1)} %get-tuple-element.20), channel_id=1, source_target_pairs={{0,1},{1,0},{2,3},{3,2},{4,5},{5,4},{6,7},{7,6},{8,9},{9,8},{10,11... | collective-permute-start | bytes 442376 | tf_op jit(solution)/shard_map/ppermute | solution.py:593
  19.8 3.8 %collective-permute-start = (bf16[8,8,2432]{2,1,0:T(8,128)(2,1)S(1)}, bf16[8,8,2432]{2,1,0:T(8,128)(2,1)S(1)}, u32[]{:S(2)}, u32[]{:S(2)}) collective-permute-start(bf16[8,8,2432]{2,1,0:T(8,128)(2,1)S(1)} %all-to-all-done.after_ref.own_ref), channel_id=1, source_target_pairs={{0,1},{1,0},{2,3},{3,2},{4,5},{5,4},{6,7},{7,6},{8,9},{9,8},{10,11... | collective-permute-start | bytes 933896 | tf_op jit(solution)/shard_map/ppermute | solution.py:578
  20.5 14.5 %collective-permute-start.3 = (bf16[16,4608]{1,0:T(8,128)(2,1)}, bf16[16,4608]{1,0:T(8,128)(2,1)S(1)}, u32[]{:S(2)}, u32[]{:S(2)}) collective-permute-start(bf16[16,4608]{1,0:T(8,128)(2,1)} %get-tuple-element.25), channel_id=1, source_target_pairs={{0,2},{2,0},{1,3},{3,1},{4,6},{6,4},{5,7},{7,5},{8,10},{10,8},{9,1... | collective-permute-start | bytes 442376 | tf_op jit(solution)/shard_map/ppermute | solution.py:33
  27.2 10.4 %all-to-all-start.1 = ((f32[16,8,128]{2,1,0:T(8,128)}), f32[16,8,128]{2,1,0:T(8,128)S(1)}, u32[]{:S(2)}, u32[]{:S(2)}) async-start(f32[16,8,128]{2,1,0:T(8,128)} %get-tuple-element.16), calls=%async_computation.1 | async-start | bytes 131072 | tf_op jit(solution)/shard_map/all_to_all | solution.py:615
  39.3 14.1 %all-to-all-start.2 = ((bf16[16,72,128]{2,1,0:T(8,128)(2,1)}), bf16[16,72,128]{2,1,0:T(8,128)(2,1)S(1)}, u32[]{:S(2)}, u32[]{:S(2)}) async-start(bf16[16,72,128]{2,1,0:T(8,128)(2,1)} %get-tuple-element.22), calls=%async_computation.2 | async-start | bytes 589824 | tf_op jit(solution)/shard_map/all_to_all | solution.py:644

commit v4 on v3

--- a/solution.py
+++ b/solution.py
@@ -181,7 +181,9 @@
     return (penalty.reshape(rows), grad_in, grad_out)
 
 
-def send_kernel(copies, pieces, base_hbm, hidden_hbm, in_hbm, out_hbm, gain_hbm, packed_hbm, vec_ref, keep_ref, give_ref, base_ref, hidden_ref, in_ref, packed_ref, sems):
+def send_kernel(copies, pieces, base_hbm, hidden_hbm, in_hbm, out_hbm, gain_hbm, packed_hbm, vec_ref, *refs):
+    unit_refs = refs[: 2 * pieces]
+    base_ref, hidden_ref, in_ref, packed_ref, sems = refs[2 * pieces :]
     rows, hidden = hidden_ref.shape
     feat = base_ref.shape[1]
     quarter = hidden // (2 * pieces)
@@ -215,92 +217,80 @@
         packed_ref[i, :, feat:] = cols
     put = pltpu.make_async_copy(packed_ref, packed_hbm, sems.at[5])
     put.start()
+    m_i = lax.axis_index("mp")
     r_i = lax.axis_index("rep")
     for i in range(pieces):
-        for ref, r in ((keep_ref, r_i), (give_ref, 1 - r_i)):
-            start = pl.multiple_of((2 * i + r) * quarter, 128)
-            ref[i] = hidden_ref[:, pl.ds(start, quarter)]
+        for j in range(2):
+            to = 2 * lax.rem(m_i + i, pieces) + lax.rem(r_i + j, 2)
+            start = pl.multiple_of(to * quarter, 128)
+            unit_refs[2 * i + j][...] = hidden_ref[:, pl.ds(start, quarter)]
     get_out.wait()
     get_gain.wait()
     put.wait()
 
 
-def stage_kernel(after_ref, head_hbm, head_ref, sems):
-    copies = sems.shape[0]
-    part = head_ref.shape[0] // copies
+def normed_rows(nv, nm, got_ref, vec_ref, cols_ref, x_ref):
+    rows = got_ref.shape[1]
+    feat = got_ref.shape[2] - 128
+    model = nm * feat
+    half = nv * rows
+    pair = 2 * rows
+    lane = lax.broadcasted_iota(jnp.int32, (pair, 128), 1)
+    for v in range(0, nv, 2):
+        at = v * rows
+
+        def tile(m, c):
+            first = got_ref[v * nm + m, :, c : c + 128].astype(f32)
+            second = got_ref[(v + 1) * nm + m, :, c : c + 128].astype(f32)
+            return jnp.concatenate([first, second], axis=0)
+
+        mixed = tile(0, feat)
+        for m in range(1, nm):
+            mixed += tile(m, feat)
+        mix = jnp.sum(mixed, axis=1, keepdims=True)
+        mix_b = jnp.broadcast_to(mix, (pair, 128))
+        sq_b = jnp.zeros((pair, 128), f32)
+        sq_e = jnp.zeros((pair, 128), f32)
+        dot_o = jnp.zeros((pair, 128), f32)
+        for m in range(nm):
+            for c in range(0, feat, 128):
+                out = vec_ref[m, 0, c // 128 : c // 128 + 1, :]
+                b = tile(m, c)
+                e = b + mix_b * out
+                sq_b += b * b
+                sq_e += e * e
+                dot_o += e * out
+        scale_e = lax.rsqrt(jnp.sum(sq_e, axis=1, keepdims=True) / model + epsilon)
+        scale_b = lax.rsqrt(jnp.sum(sq_b, axis=1, keepdims=True) / model + epsilon)
+        along = jnp.sum(dot_o, axis=1, keepdims=True)
+        cols_ref[at : at + pair, :] = jnp.where(
+            lane == 0, mix, jnp.where(lane == 1, scale_e, jnp.where(lane == 2, along, 0.0))
+        )
+        scale_e = jnp.broadcast_to(scale_e, (pair, 128))
+        scale_b = jnp.broadcast_to(scale_b, (pair, 128))
+        for m in range(nm):
+            for c in range(0, feat, 128):
+                d = m * feat + c
+                t = c // 128
+                out = vec_ref[m, 0, t : t + 1, :]
+                gain = vec_ref[m, 1, t : t + 1, :]
+                b = tile(m, c)
+                e = b + mix_b * out
+                x_ref[at : at + pair, d : d + 128] = (e * scale_e * gain).astype(bf16)
+                x_ref[half + at : half + at + pair, d : d + 128] = (b * scale_b * gain).astype(bf16)
+
+
+def early_kernel(nv, nm, own_ref, vec_ref, head_hbm, head_ref, pre_ref, cols_ref, x_ref, sems):
+    model = head_hbm.shape[0]
+    part = model // sems.shape[0]
     moves = []
-    for i in range(copies):
+    for i in range(sems.shape[0]):
         span = pl.ds(i * part, part)
         moves.append(pltpu.make_async_copy(head_hbm.at[span], head_ref.at[span], sems.at[i]))
-        moves[-1].start()
-    for move in moves:
-        move.wait()
-
-
-def score_kernel(nv, nm, own_ref, other_ref, vec_ref, ids_ref, early_ref, head_hbm, slab_hbm, cols_ref, ops_hbm, x_ref, slab_ref, ops_ref, late_ref, sems):
-    rows = own_ref.shape[1]
+        moves[i].start()
     feat = own_ref.shape[2] - 128
-    model, voc = head_hbm.shape
-    pair = 2 * rows
-    group = 2 * nv * rows
-    half = group // 2
-
-    early = early_ref.shape[0]
-    part = (model - early) // 2
-    moves = []
-    for i in range(2):
-        move = pltpu.make_async_copy(
-            head_hbm.at[pl.ds(early + i * part, part)],
-            late_ref.at[pl.ds(i * part, part)],
-            sems.at[2 + i],
-        )
-        move.start()
-        moves.append(move)
-
-    lane_t = lax.broadcasted_iota(jnp.int32, (pair, 128), 1)
-    for k, got_ref in enumerate((own_ref, other_ref)):
-        for v in range(0, nv, 2):
-            at = (k * nv + v) * rows
-
-            def tile(m, c):
-                first = got_ref[v * nm + m, :, c : c + 128].astype(f32)
-                second = got_ref[(v + 1) * nm + m, :, c : c + 128].astype(f32)
-                return jnp.concatenate([first, second], axis=0)
-
-            mixed = tile(0, feat)
-            for m in range(1, nm):
-                mixed += tile(m, feat)
-            mix = jnp.sum(mixed, axis=1, keepdims=True)
-            mix_b = jnp.broadcast_to(mix, (pair, 128))
-            sq_b = jnp.zeros((pair, 128), f32)
-            sq_e = jnp.zeros((pair, 128), f32)
-            dot_o = jnp.zeros((pair, 128), f32)
-            for m in range(nm):
-                for c in range(0, feat, 128):
-                    out = vec_ref[m, 0, c // 128 : c // 128 + 1, :]
-                    b = tile(m, c)
-                    e = b + mix_b * out
-                    sq_b += b * b
-                    sq_e += e * e
-                    dot_o += e * out
-            scale_e = lax.rsqrt(jnp.sum(sq_e, axis=1, keepdims=True) / model + epsilon)
-            scale_b = lax.rsqrt(jnp.sum(sq_b, axis=1, keepdims=True) / model + epsilon)
-            along = jnp.sum(dot_o, axis=1, keepdims=True)
-            cols_ref[at : at + pair, :] = jnp.where(
-                lane_t == 0, mix, jnp.where(lane_t == 1, scale_e, jnp.where(lane_t == 2, along, 0.0))
-            )
-            scale_e = jnp.broadcast_to(scale_e, (pair, 128))
-            scale_b = jnp.broadcast_to(scale_b, (pair, 128))
-            for m in range(nm):
-                for c in range(0, feat, 128):
-                    d = m * feat + c
-                    t = c // 128
-                    out = vec_ref[m, 0, t : t + 1, :]
-                    gain = vec_ref[m, 1, t : t + 1, :]
-                    b = tile(m, c)
-                    e = b + mix_b * out
-                    x_ref[at : at + pair, d : d + 128] = (e * scale_e * gain).astype(bf16)
-                    x_ref[group + at : group + at + pair, d : d + 128] = (b * scale_b * gain).astype(bf16)
+    half = cols_ref.shape[0]
+    normed_rows(nv, nm, own_ref, vec_ref, cols_ref, x_ref)
     sub = lax.broadcasted_iota(jnp.int32, (16, 128), 0)
     for d in range(0, model, 128):
         m, t = d // feat, d % feat // 128
@@ -310,15 +300,26 @@
             piece = rest.astype(bf16).astype(f32)
             block = jnp.where(sub == i, piece, block)
             rest = rest - piece
-        x_ref[2 * group :, d : d + 128] = block.astype(bf16)
-
-    pre = jnp.dot(x_ref[:, :early], early_ref[...], preferred_element_type=f32)
-    for move in moves:
+        x_ref[2 * half :, d : d + 128] = block.astype(bf16)
+    pre = None
+    for i, move in enumerate(moves):
         move.wait()
-    pre += jnp.dot(x_ref[:, early:], late_ref[...], preferred_element_type=f32)
-    pre_edit = pre[:group]
-    pre_base = pre[group : 2 * group]
-    toward = jnp.sum(pre[2 * group :], axis=0, keepdims=True)
+        span = slice(i * part, (i + 1) * part)
+        block = jnp.dot(x_ref[:, span], head_ref[span, :], preferred_element_type=f32)
+        pre = block if pre is None else pre + block
+    pre_ref[...] = pre
+
+
+def score_kernel(nv, nm, other_ref, vec_ref, ids_ref, head_ref, early_ref, early_cols_ref, slab_hbm, cols_ref, ops_hbm, x_ref, slab_ref, ops_ref, sems):
+    voc = head_ref.shape[1]
+    half = early_cols_ref.shape[0]
+    group = 2 * half
+    cols_ref[:half] = early_cols_ref[...]
+    normed_rows(nv, nm, other_ref, vec_ref, cols_ref.at[half:], x_ref)
+    late = jnp.dot(x_ref[...], head_ref[...], preferred_element_type=f32)
+    pre_edit = jnp.concatenate([early_ref[:half], late[:half]], axis=0)
+    pre_base = jnp.concatenate([early_ref[half:group], late[half:]], axis=0)
+    toward = jnp.sum(early_ref[group:], axis=0, keepdims=True)
     th = jnp.tanh(pre_edit / softcap)
     z_edit = softcap * th
     z_base = softcap * jnp.tanh(pre_base / softcap)
@@ -410,8 +411,8 @@
 
 
 def close_kernel(nv, nm, theirs_ref, cols_ref, outer_ref, own_ref, all_ref, *refs):
-    units = refs[:nm]
-    slab_hbm, penalty_hbm, coeff_ref, pen_ref, pull_ref, vec_ref, slab_ref, second_ref, sems = refs[nm:]
+    units = refs[: 2 * nm]
+    slab_hbm, penalty_hbm, coeff_ref, pen_ref, pull_ref, vec_ref, slab_ref, second_ref, sems = refs[2 * nm :]
     rows = own_ref.shape[1]
     feat = own_ref.shape[2] - 128
     model = outer_ref.shape[1]
@@ -475,21 +476,17 @@
             row = row * all_ref[m, 1, t : t + 1, :] - jnp.where(
                 m_i == m, second_ref[t : t + 1, :], 0.0
             )
-            high = row.astype(bf16).astype(f32)
-            vec_ref[m, t : t + 1, :] = high
-            vec_ref[m, tiles + t : tiles + t + 1, :] = row - high
-    own = jnp.concatenate(
-        [
-            coeff_ref[pl.ds(pl.multiple_of((k * nv + v_i) * rows, rows), rows), :]
-            for k in range(2)
-        ],
-        axis=0,
-    )
+            vec_ref[m, t : t + 1, :] = row
+    own = [
+        coeff_ref[pl.ds(pl.multiple_of((k * nv + v_i) * rows, rows), rows), :] for k in range(2)
+    ]
     for k in range(nm):
         m = lax.rem(m_i - k + nm, nm)
-        for t in range(units[k].shape[1] // 128):
-            row = jnp.sum(units[k][:, t * 128 : (t + 1) * 128].astype(f32) * own, axis=0, keepdims=True)
-            vec_ref[m, pl.ds(2 * tiles + t, 1), :] = row
+        for t in range(units[0].shape[1] // 128):
+            c = t * 128
+            row = units[2 * k][:, c : c + 128].astype(f32) * own[0]
+            row += units[2 * k + 1][:, c : c + 128].astype(f32) * own[1]
+            vec_ref[m, pl.ds(tiles + t, 1), :] = jnp.sum(row, axis=0, keepdims=True)
     for m in range(nm):
         block = vec_ref[m].astype(bf16)
         for v in range(nv):
@@ -505,15 +502,15 @@
 def sum_kernel(back_ref, in_ref, out_ref):
     peers = back_ref.shape[0]
     tiles = out_ref.shape[0]
-    units = back_ref.shape[1] - 2 * tiles
+    units = back_ref.shape[1] - tiles
     pieces = in_ref.shape[0] // units
     wide = jnp.zeros((tiles, 128), f32)
     for q in range(pieces):
         total = back_ref[q].astype(f32)
         for p in range(q + pieces, peers, pieces):
             total += back_ref[p].astype(f32)
-        wide += total[:tiles] + total[tiles : 2 * tiles]
-        in_ref[q * units : (q + 1) * units, :] = total[2 * tiles :]
+        wide += total[:tiles]
+        in_ref[q * units : (q + 1) * units, :] = total[tiles:]
     out_ref[...] = wide
 
 
@@ -549,16 +546,13 @@
     out_tiles = edit_out.reshape(tiles, 128)
     gain_tiles = norm_gain.reshape(tiles, 128)
 
-    early = model // 2
-
-    packed, vectors, keep, give = call(
+    packed, vectors, *units = call(
         functools.partial(send_kernel, nv * nm, nm),
         (
             pltpu.HBM((nv * nm, rows, feat + 128), bf16),
             shape((2, tiles, 128), f32),
-            shape((nm, rows, quarter), bf16),
-            shape((nm, rows, quarter), bf16),
-        ),
+        )
+        + (shape((rows, quarter), bf16),) * (2 * nm),
         [
             pltpu.VMEM((rows, feat), bf16),
             pltpu.VMEM((rows, hidden), bf16),
@@ -567,7 +561,7 @@
             pltpu.SemaphoreType.DMA((6,)),
         ],
         in_specs=[hbm] * 5,
-        out_specs=(hbm, vmem, vmem, vmem),
+        out_specs=(hbm,) + (vmem,) * (1 + 2 * nm),
     )(
         *(
             in_hbm(a)
@@ -577,23 +571,35 @@
     got = lax.all_to_all(packed, ("vocab", "mp"), 0, 0)
     other = lax.ppermute(got, "rep", [(0, 1), (1, 0)])
     vectors = from_peers(vectors, "mp", nm)
-    staged = call(
-        stage_kernel,
-        pltpu.VMEM((early, voc), bf16),
-        [pltpu.SemaphoreType.DMA((4,))],
-        in_specs=[vmem, hbm],
-        out_specs=vmem,
-    )(got, in_hbm(head))
     vectors = jnp.stack(in_order(vectors, m_i))
+    half = group // 2
+    staged, early, early_cols = call(
+        functools.partial(early_kernel, nv, nm),
+        (
+            pltpu.VMEM((model, voc), bf16),
+            shape((group + 16, voc), f32),
+            shape((half, 128), f32),
+        ),
+        [pltpu.VMEM((group + 16, model), bf16), pltpu.SemaphoreType.DMA((6,))],
+        8,
+        in_specs=[vmem, vmem, hbm],
+        out_specs=(vmem, vmem, vmem),
+    )(got, vectors, in_hbm(head))
     ids = token_ids.reshape(nv, nr, rows)
     ids = jnp.concatenate(
         [lax.dynamic_index_in_dim(ids, (r_i + k) % nr, 1, keepdims=False) for k in range(nr)]
     ).reshape(group, 1)
 
-    units = jnp.concatenate([keep, lax.ppermute(give, "rep", [(0, 1), (1, 0)])], axis=1)
-    units = to_peers(
-        lambda m: lax.dynamic_index_in_dim(units, m, 0, keepdims=False), "mp", nm, m_i
-    )
+    for i in range(nm):
+        for j in range(2):
+            if i or j:
+                moves = [
+                    (2 * m + r, 2 * ((m + i) % nm) + (r + j) % 2)
+                    for m in range(nm)
+                    for r in range(2)
+                ]
+                units[2 * i + j] = lax.ppermute(units[2 * i + j], ("mp", "rep"), moves)
+
     slab, cols, ops = call(
         functools.partial(score_kernel, nv, nm),
         (
@@ -602,16 +608,14 @@
             pltpu.HBM((4 * group + 16, voc), bf16),
         ),
         [
-            pltpu.VMEM((2 * group + 16, model), bf16),
+            pltpu.VMEM((group, model), bf16),
             pltpu.VMEM((peers, 8, 128), f32),
             pltpu.VMEM((4 * group + 16, voc), bf16),
-            pltpu.VMEM((model - early, voc), bf16),
-            pltpu.SemaphoreType.DMA((4,)),
+            pltpu.SemaphoreType.DMA((2,)),
         ],
-        8,
-        in_specs=[vmem] * 5 + [hbm],
+        in_specs=[vmem] * 6,
         out_specs=(hbm, vmem, hbm),
-    )(got, other, vectors, ids, staged, in_hbm(head))
+    )(other, vectors, ids, staged, early, early_cols)
     theirs = lax.all_to_all(slab, everyone, 0, 0)
     outer = call(
         outer_kernel,
@@ -625,7 +629,7 @@
         in_specs=[hbm, hbm],
     )(in_hbm(ops), in_hbm(head))
 
-    width = (2 * feat + quarter) // 128
+    width = (feat + quarter) // 128
     slab, penalty = call(
         functools.partial(close_kernel, nv, nm),
         (pltpu.HBM((peers, width, 128), bf16), pltpu.HBM((rows, 128), f32)),
@@ -638,7 +642,7 @@
             pltpu.VMEM((tiles, 128), f32),
             pltpu.SemaphoreType.DMA((2,)),
         ],
-        in_specs=[vmem] * (5 + nm),
+        in_specs=[vmem] * (5 + 2 * nm),
         out_specs=(hbm, hbm),
     )(theirs, cols, outer, got, vectors, *units)
     back = lax.all_to_all(slab, everyone, 0, 0)

time: 54.5 us -> 53.7 us (0.985)
  waiting for transfers between devices: 18.8 us -> 15.8 us
  starting transfers between devices: 17.8 us -> 20.5 us
  local copies, waits for them, and re-layouts: 2.85 us -> 2.13 us
    all_to_all x1, waiting for transfers between devices: 2.54 us -> 0.01 us  [fused(): theirs = lax.all_to_all(slab, everyone, 0, 0)]
    all_to_all x1, waiting for transfers between devices: 4.74 us -> 7.08 us  [fused(): got = lax.all_to_all(packed, ('vocab', 'mp'), 0, 0)]
    ppermute x1, waiting for transfers between devices: 2.25 us -> 0.01 us  [from_peers(): lax.ppermute(value, axis, moves[k])]
    all_to_all x1, starting transfers between devices: 3.55 us -> 5.33 us  [fused(): back = lax.all_to_all(slab, everyone, 0, 0)]
    pallas_call x1, Pallas kernels: 3.58 us -> 2.23 us  [fused(): call(functools.partial(score_kernel, nv, nm), (pltpu.HBM((peers, 8, 128),...]
    all_to_all x1, waiting for transfers between devices: 9.22 us -> 8.21 us  [fused(): back = lax.all_to_all(slab, everyone, 0, 0)]
    pallas_call x1, Pallas kernels: 1.63 us -> 2.63 us  [fused(): call(functools.partial(early_kernel, nv, nm), (pltpu.VMEM((model, voc), b...]
    squeeze x1 -> x0, local copies, waits for them, and re-layouts: 0.69 us -> none  [fused(): lax.dynamic_index_in_dim(units, m, 0, keepdims=False)]
  transfers between devices with their start and end apart: 7 -> 8, of which waited for: 4 -> 3; matrix products, arithmetic and copies ran while one was open for 5% -> 4% of each run, Pallas kernels for 18% -> 13%
where the time goes in v4:
time: 53.7 us; the launch traced here: 53.3 us
  starting transfers between devices  20.5 us (38%)
  waiting for transfers between devices  15.8 us (29%)
  Pallas kernels  14 us (26%)
  local copies, waits for them, and re-layouts  2.13 us (4%)
  between operations  0.77 us (1%)
    all_to_all x1, waiting for transfers between devices, fused(): back = lax.all_to_all(slab, everyone, 0, 0)  8.21 us
    all_to_all x1, starting transfers between devices, fused(): got = lax.all_to_all(packed, ('vocab', 'mp'), 0, 0)  7.26 us
    all_to_all x1, waiting for transfers between devices, fused(): got = lax.all_to_all(packed, ('vocab', 'mp'), 0, 0)  7.08 us
    all_to_all x1, starting transfers between devices, fused(): back = lax.all_to_all(slab, everyone, 0, 0)  5.33 us
    pallas_call x1, Pallas kernels, fused(): call(outer_kernel, shape((2 * group + 16, model), f32), [pltpu.VMEM((4 *...  4.29 us
    all_to_all x1, starting transfers between devices, fused(): theirs = lax.all_to_all(slab, everyone, 0, 0)  3.81 us
    pallas_call x1, Pallas kernels, fused(): call(functools.partial(early_kernel, nv, nm), (pltpu.VMEM((model, voc), b...  2.63 us
    pallas_call x1, Pallas kernels, fused(): call(functools.partial(send_kernel, nv * nm, nm), (pltpu.HBM((nv * nm, ro...  2.61 us
  transfers between devices with their start and end apart: 8, of which 3 were waited for; matrix products, arithmetic and copies ran while one was open for 4% of the time, Pallas kernels for 13%

profile of v4, /device:TPU:0, one launch (start us, length us, event | category | flops | bytes accessed | tf_op | source)
XLA Modules:
  0.0 53.3 jit_solution(2335020256123179006)
XLA Ops:
  0.6 2.6 %shard_map.94 = (bf16[8,8,2432]{2,1,0:T(8,128)(2,1)}, f32[2,18,128]{2,1,0:T(8,128)S(1)}, bf16[8,4608]{1,0:T(8,128)(2,1)S(1)}, bf16[8,4608]{1,0:T(8,128)(2,1)}, b...) custom-call(bf16[8,2304]{1,0:T(8,128)(2,1)} %base_hbm.1, bf16[8,18432]{1,0:T(8,128)(2,1)} %hidden_hbm.1, ...), custom_call_target="tpu_custom_call" | custom-call | tf_op jit(solution)/shard_map/pallas_call | solution.py:549
  3.3 7.3 %all-to-all-start = ((bf16[8,8,2432]{2,1,0:T(8,128)(2,1)}), bf16[8,8,2432]{2,1,0:T(8,128)(2,1)S(1)}, u32[]{:S(2)}, u32[]{:S(2)}) async-start(bf16[8,8,2432]{2,1,0:T(8,128)(2,1)} %get-tuple-element.19), calls=%async_computation | async-start | bytes 622592 | tf_op jit(solution)/shard_map/all_to_all | solution.py:571
  10.5 2.0 %collective-permute-start.1 = (f32[2,18,128]{2,1,0:T(8,128)S(1)}, f32[2,18,128]{2,1,0:T(8,128)S(1)}, u32[]{:S(2)}, u32[]{:S(2)}) collective-permute-start(f32[2,18,128]{2,1,0:T(8,128)S(1)} %get-tuple-element.20), channel_id=1, source_target_pairs={{0,2},{2,0},{1,3},{3,1},{4,6},{6,4},{5,7},{7,5},{8,10},{10,8},{9,1... | collective-permute-start | bytes 55304 | tf_op jit(solution)/shard_map/ppermute | solution.py:27
  12.5 0.7 %reshape.30 = s32[4,2,8]{2,1,0:T(2,128)S(1)} reshape(s32[64]{0:T(128)} %param.13) | data formatting | bytes 512 | tf_op jit(solution)/shard_map/reshape | solution.py:588
  13.3 0.1 reshape.34.ids_ref
  13.4 7.1 %all-to-all-done.own_ref = bf16[8,8,2432]{2,1,0:T(8,128)(2,1)S(1)} async-done(((bf16[8,8,2432]{2,1,0:T(8,128)(2,1)}), bf16[8,8,2432]{2,1,0:T(8,128)(2,1)S(1)}, u32[]{:S(2)}, u32[]{:S(2)}) %all-to-all-start) | async-done | bytes 311328 | tf_op jit(solution)/shard_map/all_to_all | solution.py:571
  20.5 0.0 collective-permute-start
  20.5 0.0 collective-permute-done.1
  20.5 2.6 %shard_map.95 = (bf16[4608,512]{1,0:T(8,128)(2,1)S(1)}, f32[80,512]{1,0:T(8,128)S(1)}, f32[32,128]{1,0:T(8,128)S(1)}) custom-call(bf16[8,8,2432]{2,1,0:T(8,128)(2,1)S(1)} %all-to-all-done.own_ref, f32[2,2,18,128]{3,2,1,0:T(8,128)S(1)} %pad_maximum_fusion.vec_ref.all_ref, bf16[4608,512]{1,0:T(8,128)(2,1)} %head_hbm.3), custom_call_target="tpu_custom_call" | custom-call | tf_op jit(solution)/shard_map/pallas_call | solution.py:576
  23.2 0.0 collective-permute-done.other_ref
  23.2 2.2 %shard_map.96 = (f32[16,8,128]{2,1,0:T(8,128)}, f32[64,128]{1,0:T(8,128)S(1)}, bf16[272,512]{1,0:T(8,128)(2,1)}) custom-call(bf16[8,8,2432]{2,1,0:T(8,128)(2,1)S(1)} %collective-permute-done.other_ref, f32[2,2,18,128]{3,2,1,0:T(8,128)S(1)} %pad_maximum_fusion.vec_ref.all_ref, s32[64,1]{1,0:T(8,128)S(1)} %reshape.34.ids_ref, ...), custom_call_target="tpu_custom_call" | custom-call | tf_op jit(solution)/shard_map/pallas_call | solution.py:603
  25.4 3.8 %all-to-all-start.1 = ((f32[16,8,128]{2,1,0:T(8,128)}), f32[16,8,128]{2,1,0:T(8,128)S(1)}, u32[]{:S(2)}, u32[]{:S(2)}) async-start(f32[16,8,128]{2,1,0:T(8,128)} %get-tuple-element.24), calls=%async_computation.1 | async-start | bytes 131072 | tf_op jit(solution)/shard_map/all_to_all | solution.py:619
  29.2 0.4 collective-permute-start.2
  29.6 1.7 %collective-permute-start.3 = (bf16[8,4608]{1,0:T(8,128)(2,1)S(1)}, bf16[8,4608]{1,0:T(8,128)(2,1)S(1)}, u32[]{:S(2)}, u32[]{:S(2)}) collective-permute-start(bf16[8,4608]{1,0:T(8,128)(2,1)S(1)} %get-tuple-element.29), channel_id=1, source_target_pairs={{0,2},{1,3},{2,0},{3,1},{4,6},{5,7},{6,4},{7,5},{8,10},{9,11},{10,... | collective-permute-start | bytes 221192 | tf_op jit(solution)/shard_map/ppermute | solution.py:601
  31.3 0.0 collective-permute-start.4
  31.3 4.3 %shard_map.97.outer_ref = f32[144,4608]{1,0:T(8,128)S(1)} custom-call(bf16[272,512]{1,0:T(8,128)(2,1)} %get-tuple-element.26.ops_hbm, bf16[4608,512]{1,0:T(8,128)(2,1)} %head_hbm.3), custom_call_target="tpu_custom_call" | custom-call | tf_op jit(solution)/shard_map/pallas_call | solution.py:620
  35.6 0.0 collective-permute-done.2.refs_1_
  35.6 0.0 collective-permute-done.3.refs_2_
  35.6 0.5 %collective-permute-done.4.refs_3_ = bf16[8,4608]{1,0:T(8,128)(2,1)S(1)} collective-permute-done((bf16[8,4608]{1,0:T(8,128)(2,1)S(1)}, bf16[8,4608]{1,0:T(8,128)(2,1)S(1)}, u32[]{:S(2)}, u32[]{:S(2)}) %collective-permute-start.4) | collective-permute-done | bytes 73760 | tf_op jit(solution)/shard_map/ppermute | solution.py:601
  36.2 0.0 all-to-all-done.1.theirs_ref
  36.2 1.6 %shard_map.98 = (bf16[16,54,128]{2,1,0:T(8,128)(2,1)}, f32[8,128]{1,0:T(8,128)}) custom-call(f32[16,8,128]{2,1,0:T(8,128)S(1)} %all-to-all-done.1.theirs_ref, f32[64,128]{1,0:T(8,128)S(1)} %get-tuple-element.25.cols_ref, f32[144,4608]{1,0:T(8,128)S(1)} %shard_map.97.outer_ref, bf16[8,8,2432]{2,1,0:T(8,128)(2,1)S(1)} %all-to-all-done.own_ref, ...), custom_call_target="tpu_custom_call" | custom-call | tf_op jit(solution)/shard_map/pallas_call | solution.py:633
  37.8 5.3 %all-to-all-start.2 = ((bf16[16,54,128]{2,1,0:T(8,128)(2,1)}), bf16[16,54,128]{2,1,0:T(8,128)(2,1)S(1)}, u32[]{:S(2)}, u32[]{:S(2)}) async-start(bf16[16,54,128]{2,1,0:T(8,128)(2,1)} %get-tuple-element.32), calls=%async_computation.2 | async-start | bytes 458752 | tf_op jit(solution)/shard_map/all_to_all | solution.py:648
  43.1 1.3 %slice_reduce_fusion = f32[8]{0:T(128)} fusion(f32[8,128]{1,0:T(8,128)} %get-tuple-element.31), kind=kLoop, calls=%fused_computation.4 | loop fusion | bytes 64 | tf_op jit(solution)/shard_map/slice | solution.py:652
  44.4 8.2 %all-to-all-done.2.back_ref = bf16[16,54,128]{2,1,0:T(8,128)(2,1)S(1)} async-done(((bf16[16,54,128]{2,1,0:T(8,128)(2,1)}), bf16[16,54,128]{2,1,0:T(8,128)(2,1)S(1)}, u32[]{:S(2)}, u32[]{:S(2)}) %all-to-all-start.2) | async-done | bytes 221216 | tf_op jit(solution)/shard_map/all_to_all | solution.py:648
  52.6 0.7 %shard_map.99 = (f32[144,128]{1,0:T(8,128)}, f32[18,128]{1,0:T(8,128)}) custom-call(bf16[16,54,128]{2,1,0:T(8,128)(2,1)S(1)} %all-to-all-done.2.back_ref), custom_call_target="tpu_custom_call" | custom-call | tf_op jit(solution)/shard_map/pallas_call | solution.py:649
  (4 shorter events, 0.0 us)
Async XLA Ops:
  3.3 17.2 %all-to-all-start = ((bf16[8,8,2432]{2,1,0:T(8,128)(2,1)}), bf16[8,8,2432]{2,1,0:T(8,128)(2,1)S(1)}, u32[]{:S(2)}, u32[]{:S(2)}) async-start(bf16[8,8,2432]{2,1,0:T(8,128)(2,1)} %get-tuple-element.19), calls=%async_computation | async-start | bytes 622592 | tf_op jit(solution)/shard_map/all_to_all | solution.py:571
  10.5 10.0 %collective-permute-start.1 = (f32[2,18,128]{2,1,0:T(8,128)S(1)}, f32[2,18,128]{2,1,0:T(8,128)S(1)}, u32[]{:S(2)}, u32[]{:S(2)}) collective-permute-start(f32[2,18,128]{2,1,0:T(8,128)S(1)} %get-tuple-element.20), channel_id=1, source_target_pairs={{0,2},{2,0},{1,3},{3,1},{4,6},{6,4},{5,7},{7,5},{8,10},{10,8},{9,1... | collective-permute-start | bytes 55304 | tf_op jit(solution)/shard_map/ppermute | solution.py:27
  20.5 2.7 %collective-permute-start = (bf16[8,8,2432]{2,1,0:T(8,128)(2,1)S(1)}, bf16[8,8,2432]{2,1,0:T(8,128)(2,1)S(1)}, u32[]{:S(2)}, u32[]{:S(2)}) collective-permute-start(bf16[8,8,2432]{2,1,0:T(8,128)(2,1)S(1)} %all-to-all-done.own_ref), channel_id=1, source_target_pairs={{0,1},{1,0},{2,3},{3,2},{4,5},{5,4},{6,7},{7,6},{8,9},{9,8},{10,11... | collective-permute-start | bytes 933896 | tf_op jit(solution)/shard_map/ppermute | solution.py:572
  25.4 10.8 %all-to-all-start.1 = ((f32[16,8,128]{2,1,0:T(8,128)}), f32[16,8,128]{2,1,0:T(8,128)S(1)}, u32[]{:S(2)}, u32[]{:S(2)}) async-start(f32[16,8,128]{2,1,0:T(8,128)} %get-tuple-element.24), calls=%async_computation.1 | async-start | bytes 131072 | tf_op jit(solution)/shard_map/all_to_all | solution.py:619
  29.2 6.4 %collective-permute-start.2 = (bf16[8,4608]{1,0:T(8,128)(2,1)}, bf16[8,4608]{1,0:T(8,128)(2,1)S(1)}, u32[]{:S(2)}, u32[]{:S(2)}) collective-permute-start(bf16[8,4608]{1,0:T(8,128)(2,1)} %get-tuple-element.28), channel_id=1, source_target_pairs={{0,1},{1,0},{2,3},{3,2},{4,5},{5,4},{6,7},{7,6},{8,9},{9,8},{10,11... | collective-permute-start | bytes 221192 | tf_op jit(solution)/shard_map/ppermute | solution.py:601
  29.6 6.0 %collective-permute-start.3 = (bf16[8,4608]{1,0:T(8,128)(2,1)S(1)}, bf16[8,4608]{1,0:T(8,128)(2,1)S(1)}, u32[]{:S(2)}, u32[]{:S(2)}) collective-permute-start(bf16[8,4608]{1,0:T(8,128)(2,1)S(1)} %get-tuple-element.29), channel_id=1, source_target_pairs={{0,2},{1,3},{2,0},{3,1},{4,6},{5,7},{6,4},{7,5},{8,10},{9,11},{10,... | collective-permute-start | bytes 221192 | tf_op jit(solution)/shard_map/ppermute | solution.py:601
  31.3 4.9 %collective-permute-start.4 = (bf16[8,4608]{1,0:T(8,128)(2,1)S(1)}, bf16[8,4608]{1,0:T(8,128)(2,1)S(1)}, u32[]{:S(2)}, u32[]{:S(2)}) collective-permute-start(bf16[8,4608]{1,0:T(8,128)(2,1)S(1)} %get-tuple-element.30), channel_id=1, source_target_pairs={{0,3},{1,2},{2,1},{3,0},{4,7},{5,6},{6,5},{7,4},{8,11},{9,10},{10,... | collective-permute-start | bytes 221192 | tf_op jit(solution)/shard_map/ppermute | solution.py:601
  37.8 14.9 %all-to-all-start.2 = ((bf16[16,54,128]{2,1,0:T(8,128)(2,1)}), bf16[16,54,128]{2,1,0:T(8,128)(2,1)S(1)}, u32[]{:S(2)}, u32[]{:S(2)}) async-start(bf16[16,54,128]{2,1,0:T(8,128)(2,1)} %get-tuple-element.32), calls=%async_computation.2 | async-start | bytes 458752 | tf_op jit(solution)/shard_map/all_to_all | solution.py:648

commit v5 on v4

--- a/solution.py
+++ b/solution.py
@@ -183,23 +183,39 @@
 
 def send_kernel(copies, pieces, base_hbm, hidden_hbm, in_hbm, out_hbm, gain_hbm, packed_hbm, vec_ref, *refs):
     unit_refs = refs[: 2 * pieces]
-    base_ref, hidden_ref, in_ref, packed_ref, sems = refs[2 * pieces :]
+    base_ref, hidden_ref, in_ref, packed_ref, mix_ref, sems = refs[2 * pieces :]
     rows, hidden = hidden_ref.shape
     feat = base_ref.shape[1]
     quarter = hidden // (2 * pieces)
     get_hidden = pltpu.make_async_copy(hidden_hbm, hidden_ref, sems.at[0])
     get_in = pltpu.make_async_copy(in_hbm, in_ref, sems.at[1])
     get_base = pltpu.make_async_copy(base_hbm, base_ref, sems.at[2])
-    get_out = pltpu.make_async_copy(out_hbm, vec_ref.at[0], sems.at[3])
-    get_gain = pltpu.make_async_copy(gain_hbm, vec_ref.at[1], sems.at[4])
+    later = [
+        pltpu.make_async_copy(out_hbm, vec_ref.at[0], sems.at[3]),
+        pltpu.make_async_copy(gain_hbm, vec_ref.at[1], sems.at[4]),
+    ]
+    m_i = lax.axis_index("mp")
+    r_i = lax.axis_index("rep")
+    for i in range(pieces):
+        for j in range(2):
+            to = 2 * lax.rem(m_i + i, pieces) + lax.rem(r_i + j, 2)
+            start = pl.multiple_of(to * quarter, 128)
+            k = 2 * i + j
+            later.append(
+                pltpu.make_async_copy(
+                    hidden_hbm.at[:, pl.ds(start, quarter)], unit_refs[k], sems.at[7 + k]
+                )
+            )
+    get_base.start()
     get_hidden.start()
     get_in.start()
-    get_base.start()
-    get_out.start()
-    get_gain.start()
+    for move in later:
+        move.start()
     get_base.wait()
     for i in range(copies):
-        packed_ref[i, :, :feat] = base_ref[...]
+        packed_ref[i] = base_ref[...]
+    put_base = pltpu.make_async_copy(packed_ref, packed_hbm.at[:, :, pl.ds(0, feat)], sems.at[5])
+    put_base.start()
     get_hidden.wait()
     get_in.wait()
     total = jnp.zeros((rows, 128), f32)
@@ -214,19 +230,13 @@
         mix = mix - piece
     cols = cols.astype(bf16)
     for i in range(copies):
-        packed_ref[i, :, feat:] = cols
-    put = pltpu.make_async_copy(packed_ref, packed_hbm, sems.at[5])
-    put.start()
-    m_i = lax.axis_index("mp")
-    r_i = lax.axis_index("rep")
-    for i in range(pieces):
-        for j in range(2):
-            to = 2 * lax.rem(m_i + i, pieces) + lax.rem(r_i + j, 2)
-            start = pl.multiple_of(to * quarter, 128)
-            unit_refs[2 * i + j][...] = hidden_ref[:, pl.ds(start, quarter)]
-    get_out.wait()
-    get_gain.wait()
-    put.wait()
+        mix_ref[i] = cols
+    put_mix = pltpu.make_async_copy(mix_ref, packed_hbm.at[:, :, pl.ds(feat, 128)], sems.at[6])
+    put_mix.start()
+    for move in later:
+        move.wait()
+    put_base.wait()
+    put_mix.wait()
 
 
 def normed_rows(nv, nm, got_ref, vec_ref, cols_ref, x_ref):
@@ -287,7 +297,8 @@
     for i in range(sems.shape[0]):
         span = pl.ds(i * part, part)
         moves.append(pltpu.make_async_copy(head_hbm.at[span], head_ref.at[span], sems.at[i]))
-        moves[i].start()
+    for move in moves:
+        move.start()
     feat = own_ref.shape[2] - 128
     half = cols_ref.shape[0]
     normed_rows(nv, nm, own_ref, vec_ref, cols_ref, x_ref)
@@ -333,6 +344,24 @@
     pe = exp_edit * slope
     pb = exp_base * slope
     po = jnp.where(hit, slope, 0.0)
+
+    high_e = pe.astype(bf16)
+    high_b = pb.astype(bf16)
+    ops_ref[:group] = high_e
+    ops_ref[group : 2 * group] = high_b
+    ops_ref[2 * group : 3 * group] = (pe - high_e.astype(f32)).astype(bf16)
+    ops_ref[3 * group : 4 * group] = (pb - high_b.astype(f32)).astype(bf16)
+    weight = cols_ref[:, 0:1] * cols_ref[:, 1:2]
+    rest = jnp.sum(weight * po, axis=0, keepdims=True)
+    sub = lax.broadcasted_iota(jnp.int32, (16, voc), 0)
+    block = jnp.zeros((16, voc), f32)
+    for i in range(3):
+        piece = rest.astype(bf16).astype(f32)
+        block = jnp.where(sub == i, piece, block)
+        rest = rest - piece
+    ops_ref[4 * group :] = block.astype(bf16)
+    put_ops = pltpu.make_async_copy(ops_ref, ops_hbm, sems.at[1])
+    put_ops.start()
 
     def total(a):
         return jnp.sum(a, axis=1, keepdims=True)
@@ -365,37 +394,21 @@
     put_slab = pltpu.make_async_copy(slab_ref, slab_hbm, sems.at[0])
     put_slab.start()
 
-    high_e = pe.astype(bf16)
-    high_b = pb.astype(bf16)
-    ops_ref[:group] = high_e
-    ops_ref[group : 2 * group] = high_b
-    ops_ref[2 * group : 3 * group] = (pe - high_e.astype(f32)).astype(bf16)
-    ops_ref[3 * group : 4 * group] = (pb - high_b.astype(f32)).astype(bf16)
-    weight = cols_ref[:, 0:1] * cols_ref[:, 1:2]
-    rest = jnp.sum(weight * po, axis=0, keepdims=True)
-    sub = lax.broadcasted_iota(jnp.int32, (16, voc), 0)
-    block = jnp.zeros((16, voc), f32)
-    for i in range(3):
-        piece = rest.astype(bf16).astype(f32)
-        block = jnp.where(sub == i, piece, block)
-        rest = rest - piece
-    ops_ref[4 * group :] = block.astype(bf16)
-    put_ops = pltpu.make_async_copy(ops_ref, ops_hbm, sems.at[1])
-    put_ops.start()
     put_slab.wait()
     put_ops.wait()
 
 
 def outer_kernel(ops_hbm, head_hbm, outer_ref, ops_ref, head_ref, sems):
     both = outer_ref.shape[0] - 16
-    part = 512
+    part = head_hbm.shape[0] // (sems.shape[0] - 1)
     get = pltpu.make_async_copy(ops_hbm, ops_ref, sems.at[0])
     get.start()
     moves = []
     for i in range(head_hbm.shape[0] // part):
         span = pl.ds(i * part, part)
         moves.append(pltpu.make_async_copy(head_hbm.at[span], head_ref.at[span], sems.at[1 + i]))
-        moves[i].start()
+    for move in moves:
+        move.start()
     get.wait()
     for i, move in enumerate(moves):
         move.wait()
@@ -464,8 +477,19 @@
             jnp.sum(part, axis=0, keepdims=True) + pulled * all_ref[m_i, 0, t : t + 1, :]
         )
 
+    own = [
+        coeff_ref[pl.ds(pl.multiple_of((k * nv + v_i) * rows, rows), rows), :] for k in range(2)
+    ]
+    for k in range(nm):
+        m = lax.rem(m_i - k + nm, nm)
+        for t in range(units[0].shape[1] // 128):
+            c = t * 128
+            row = units[2 * k][:, c : c + 128].astype(f32) * own[0]
+            row += units[2 * k + 1][:, c : c + 128].astype(f32) * own[1]
+            vec_ref[m, pl.ds(tiles + t, 1), :] = jnp.sum(row, axis=0, keepdims=True)
     by_e = jnp.broadcast_to(weight * inv_e, (group, 128))
     by_b = jnp.broadcast_to(weight * inv_b, (group, 128))
+    puts = []
     for m in range(nm):
         for t in range(tiles):
             d = m * feat + t * 128
@@ -477,26 +501,21 @@
                 m_i == m, second_ref[t : t + 1, :], 0.0
             )
             vec_ref[m, t : t + 1, :] = row
-    own = [
-        coeff_ref[pl.ds(pl.multiple_of((k * nv + v_i) * rows, rows), rows), :] for k in range(2)
-    ]
-    for k in range(nm):
-        m = lax.rem(m_i - k + nm, nm)
-        for t in range(units[0].shape[1] // 128):
-            c = t * 128
-            row = units[2 * k][:, c : c + 128].astype(f32) * own[0]
-            row += units[2 * k + 1][:, c : c + 128].astype(f32) * own[1]
-            vec_ref[m, pl.ds(tiles + t, 1), :] = jnp.sum(row, axis=0, keepdims=True)
-    for m in range(nm):
         block = vec_ref[m].astype(bf16)
         for v in range(nv):
             for r in range(2):
-                slab_ref[(v * nm + m) * 2 + r] = block
-    put_slab = pltpu.make_async_copy(slab_ref, slab_hbm, sems.at[1])
-    put_slab.start()
-
+                slab_ref[m, 2 * v + r] = block
+        for v in range(nv):
+            put = pltpu.make_async_copy(
+                slab_ref.at[m, pl.ds(2 * v, 2)],
+                slab_hbm.at[pl.ds((v * nm + m) * 2, 2)],
+                sems.at[1 + v * nm + m],
+            )
+            put.start()
+            puts.append(put)
     put_pen.wait()
-    put_slab.wait()
+    for put in puts:
+        put.wait()
 
 
 def sum_kernel(back_ref, in_ref, out_ref):
@@ -557,8 +576,9 @@
             pltpu.VMEM((rows, feat), bf16),
             pltpu.VMEM((rows, hidden), bf16),
             pltpu.VMEM((1, hidden), f32),
-            pltpu.VMEM((nv * nm, rows, feat + 128), bf16),
-            pltpu.SemaphoreType.DMA((6,)),
+            pltpu.VMEM((nv * nm, rows, feat), bf16),
+            pltpu.VMEM((nv * nm, rows, 128), bf16),
+            pltpu.SemaphoreType.DMA((7 + 2 * nm,)),
         ],
         in_specs=[hbm] * 5,
         out_specs=(hbm,) + (vmem,) * (1 + 2 * nm),
@@ -570,7 +590,17 @@
     )
     got = lax.all_to_all(packed, ("vocab", "mp"), 0, 0)
     other = lax.ppermute(got, "rep", [(0, 1), (1, 0)])
+    for i in range(nm):
+        for j in range(2):
+            if i or j:
+                moves = [
+                    (2 * m + r, 2 * ((m + i) % nm) + (r + j) % 2)
+                    for m in range(nm)
+                    for r in range(2)
+                ]
+                units[2 * i + j] = lax.ppermute(units[2 * i + j], ("mp", "rep"), moves)
     vectors = from_peers(vectors, "mp", nm)
+    vectors, units = lax.optimization_barrier((vectors, units))
     vectors = jnp.stack(in_order(vectors, m_i))
     half = group // 2
     staged, early, early_cols = call(
@@ -589,16 +619,6 @@
     ids = jnp.concatenate(
         [lax.dynamic_index_in_dim(ids, (r_i + k) % nr, 1, keepdims=False) for k in range(nr)]
     ).reshape(group, 1)
-
-    for i in range(nm):
-        for j in range(2):
-            if i or j:
-                moves = [
-                    (2 * m + r, 2 * ((m + i) % nm) + (r + j) % 2)
-                    for m in range(nm)
-                    for r in range(2)
-                ]
-                units[2 * i + j] = lax.ppermute(units[2 * i + j], ("mp", "rep"), moves)
 
     slab, cols, ops = call(
         functools.partial(score_kernel, nv, nm),
@@ -623,7 +643,7 @@
         [
             pltpu.VMEM((4 * group + 16, voc), bf16),
             pltpu.VMEM((model, voc), bf16),
-            pltpu.SemaphoreType.DMA((1 + model // 512,)),
+            pltpu.SemaphoreType.DMA((4,)),
         ],
         12,
         in_specs=[hbm, hbm],
@@ -638,9 +658,9 @@
             pltpu.VMEM((group, 128), f32),
             pltpu.VMEM((group, 128), f32),
             pltpu.VMEM((nm, width, 128), f32),
-            pltpu.VMEM((peers, width, 128), bf16),
+            pltpu.VMEM((nm, 2 * nv, width, 128), bf16),
             pltpu.VMEM((tiles, 128), f32),
-            pltpu.SemaphoreType.DMA((2,)),
+            pltpu.SemaphoreType.DMA((1 + nm * nv,)),
         ],
         in_specs=[vmem] * (5 + 2 * nm),
         out_specs=(hbm, hbm),

time: 53.7 us -> 51.5 us (0.959)
  starting transfers between devices: 20.5 us -> 18.9 us
  Pallas kernels: 14 us -> 12.5 us
  waiting for transfers between devices: 15.8 us -> 16.9 us
    all_to_all x1, waiting for transfers between devices: 7.08 us -> 0.01 us  [fused(): got = lax.all_to_all(packed, ('vocab', 'mp'), 0, 0)]
    ppermute x3, waiting for transfers between devices: 0.54 us -> 4.81 us  [fused(): units[2 * i + j] = lax.ppermute(units[2 * i + j], ('mp', 'rep'), moves)]
    all_to_all x1, waiting for transfers between devices: 0.01 us -> 3.45 us  [fused(): theirs = lax.all_to_all(slab, everyone, 0, 0)]
    all_to_all x1, starting transfers between devices: 5.33 us -> 3.54 us  [fused(): back = lax.all_to_all(slab, everyone, 0, 0)]
    pallas_call x1, Pallas kernels: 4.29 us -> 3.44 us  [fused(): call(outer_kernel, shape((2 * group + 16, model), f32), [pltpu.VMEM((4 *...]
    pallas_call x1, Pallas kernels: 2.61 us -> 1.94 us  [fused(): call(functools.partial(send_kernel, nv * nm, nm), (pltpu.HBM((nv * nm, ro...]
  transfers between devices with their start and end apart: 8 -> 8, of which waited for: 3 -> 5; matrix products, arithmetic and copies ran while one was open for 4% -> 4% of each run, Pallas kernels for 13% -> 12%
where the time goes in v5:
time: 51.5 us; the launch traced here: 51.1 us
  starting transfers between devices  18.9 us (37%)
  waiting for transfers between devices  16.9 us (33%)
  Pallas kernels  12.5 us (24%)
  local copies, waits for them, and re-layouts  2.13 us (4%)
  between operations  0.75 us (1%)
    all_to_all x1, waiting for transfers between devices, fused(): back = lax.all_to_all(slab, everyone, 0, 0)  8.17 us
    all_to_all x1, starting transfers between devices, fused(): got = lax.all_to_all(packed, ('vocab', 'mp'), 0, 0)  7.26 us
    ppermute x3, waiting for transfers between devices, fused(): units[2 * i + j] = lax.ppermute(units[2 * i + j], ('mp', 'rep'), moves)  4.81 us
    all_to_all x1, starting transfers between devices, fused(): theirs = lax.all_to_all(slab, everyone, 0, 0)  4.04 us
    all_to_all x1, starting transfers between devices, fused(): back = lax.all_to_all(slab, everyone, 0, 0)  3.54 us
    all_to_all x1, waiting for transfers between devices, fused(): theirs = lax.all_to_all(slab, everyone, 0, 0)  3.45 us
    pallas_call x1, Pallas kernels, fused(): call(outer_kernel, shape((2 * group + 16, model), f32), [pltpu.VMEM((4 *...  3.44 us
    pallas_call x1, Pallas kernels, fused(): call(functools.partial(early_kernel, nv, nm), (pltpu.VMEM((model, voc), b...  2.63 us
  transfers between devices with their start and end apart: 8, of which 5 were waited for; matrix products, arithmetic and copies ran while one was open for 4% of the time, Pallas kernels for 12%

profile of v5, /device:TPU:0, one launch (start us, length us, event | category | flops | bytes accessed | tf_op | source)
XLA Modules:
  0.0 51.1 jit_solution(2923391833876274655)
XLA Ops:
  0.6 1.9 %shard_map.94 = (bf16[8,8,2432]{2,1,0:T(8,128)(2,1)}, f32[2,18,128]{2,1,0:T(8,128)S(1)}, bf16[8,4608]{1,0:T(8,128)(2,1)S(1)}, bf16[8,4608]{1,0:T(8,128)(2,1)S(1)...) custom-call(bf16[8,2304]{1,0:T(8,128)(2,1)} %base_hbm.1, bf16[8,18432]{1,0:T(8,128)(2,1)} %hidden_hbm.1, ...), custom_call_target="tpu_custom_call" | custom-call | tf_op jit(solution)/shard_map/pallas_call | solution.py:568
  2.6 7.3 %all-to-all-start = ((bf16[8,8,2432]{2,1,0:T(8,128)(2,1)}), bf16[8,8,2432]{2,1,0:T(8,128)(2,1)S(1)}, u32[]{:S(2)}, u32[]{:S(2)}) async-start(bf16[8,8,2432]{2,1,0:T(8,128)(2,1)} %get-tuple-element.25), calls=%async_computation | async-start | bytes 622592 | tf_op jit(solution)/shard_map/all_to_all | solution.py:591
  9.8 2.0 %collective-permute-start.1 = (f32[2,18,128]{2,1,0:T(8,128)S(1)}, f32[2,18,128]{2,1,0:T(8,128)S(1)}, u32[]{:S(2)}, u32[]{:S(2)}) collective-permute-start(f32[2,18,128]{2,1,0:T(8,128)S(1)} %get-tuple-element.32), channel_id=1, source_target_pairs={{0,2},{2,0},{1,3},{3,1},{4,6},{6,4},{5,7},{7,5},{8,10},{10,8},{9,1... | collective-permute-start | bytes 55304 | tf_op jit(solution)/shard_map/ppermute | solution.py:27
  11.9 0.0 collective-permute-start.2
  11.9 0.1 collective-permute-start.3
  11.9 1.8 %collective-permute-start.4 = (bf16[8,4608]{1,0:T(8,128)(2,1)S(1)}, bf16[8,4608]{1,0:T(8,128)(2,1)S(1)}, u32[]{:S(2)}, u32[]{:S(2)}) collective-permute-start(bf16[8,4608]{1,0:T(8,128)(2,1)S(1)} %get-tuple-element.30), channel_id=1, source_target_pairs={{0,3},{1,2},{2,1},{3,0},{4,7},{5,6},{6,5},{7,4},{8,11},{9,10},{10,... | collective-permute-start | bytes 221192 | tf_op jit(solution)/shard_map/ppermute | solution.py:601
  13.7 0.7 %reshape.30 = s32[4,2,8]{2,1,0:T(2,128)S(1)} reshape(s32[64]{0:T(128)} %param.13) | data formatting | bytes 512 | tf_op jit(solution)/shard_map/reshape | solution.py:618
  14.5 0.1 reshape.34.ids_ref
  14.6 0.4 collective-permute-done.1
  15.0 0.0 collective-permute-done.2.refs_1_
  15.0 2.8 %collective-permute-done.3.refs_2_ = bf16[8,4608]{1,0:T(8,128)(2,1)S(1)} collective-permute-done((bf16[8,4608]{1,0:T(8,128)(2,1)S(1)}, bf16[8,4608]{1,0:T(8,128)(2,1)S(1)}, u32[]{:S(2)}, u32[]{:S(2)}) %collective-permute-start.3) | collective-permute-done | bytes 73760 | tf_op jit(solution)/shard_map/ppermute | solution.py:601
  17.9 2.0 %collective-permute-done.4.refs_3_ = bf16[8,4608]{1,0:T(8,128)(2,1)S(1)} collective-permute-done((bf16[8,4608]{1,0:T(8,128)(2,1)S(1)}, bf16[8,4608]{1,0:T(8,128)(2,1)S(1)}, u32[]{:S(2)}, u32[]{:S(2)}) %collective-permute-start.4) | collective-permute-done | bytes 73760 | tf_op jit(solution)/shard_map/ppermute | solution.py:601
  19.9 0.0 all-to-all-done.own_ref
  19.9 0.1 collective-permute-start
  20.0 2.6 %shard_map.95 = (bf16[4608,512]{1,0:T(8,128)(2,1)S(1)}, f32[80,512]{1,0:T(8,128)S(1)}, f32[32,128]{1,0:T(8,128)S(1)}) custom-call(bf16[8,8,2432]{2,1,0:T(8,128)(2,1)S(1)} %all-to-all-done.own_ref, f32[2,2,18,128]{3,2,1,0:T(8,128)S(1)} %pad_maximum_fusion.vec_ref.all_ref, bf16[4608,512]{1,0:T(8,128)(2,1)} %head_hbm.3), custom_call_target="tpu_custom_call" | custom-call | tf_op jit(solution)/shard_map/pallas_call | solution.py:606
  22.6 0.0 collective-permute-done.other_ref
  22.6 2.2 %shard_map.96 = (f32[16,8,128]{2,1,0:T(8,128)}, f32[64,128]{1,0:T(8,128)S(1)}, bf16[272,512]{1,0:T(8,128)(2,1)}) custom-call(bf16[8,8,2432]{2,1,0:T(8,128)(2,1)S(1)} %collective-permute-done.other_ref, f32[2,2,18,128]{3,2,1,0:T(8,128)S(1)} %pad_maximum_fusion.vec_ref.all_ref, s32[64,1]{1,0:T(8,128)S(1)} %reshape.34.ids_ref, ...), custom_call_target="tpu_custom_call" | custom-call | tf_op jit(solution)/shard_map/pallas_call | solution.py:623
  24.8 4.0 %all-to-all-start.1 = ((f32[16,8,128]{2,1,0:T(8,128)}), f32[16,8,128]{2,1,0:T(8,128)S(1)}, u32[]{:S(2)}, u32[]{:S(2)}) async-start(f32[16,8,128]{2,1,0:T(8,128)} %get-tuple-element.36), calls=%async_computation.1 | async-start | bytes 131072 | tf_op jit(solution)/shard_map/all_to_all | solution.py:639
  28.9 3.4 %shard_map.97.outer_ref = f32[144,4608]{1,0:T(8,128)S(1)} custom-call(bf16[272,512]{1,0:T(8,128)(2,1)} %get-tuple-element.38.ops_hbm, bf16[4608,512]{1,0:T(8,128)(2,1)} %head_hbm.3), custom_call_target="tpu_custom_call" | custom-call | tf_op jit(solution)/shard_map/pallas_call | solution.py:640
  32.3 3.4 %all-to-all-done.1.theirs_ref = f32[16,8,128]{2,1,0:T(8,128)S(1)} async-done(((f32[16,8,128]{2,1,0:T(8,128)}), f32[16,8,128]{2,1,0:T(8,128)S(1)}, u32[]{:S(2)}, u32[]{:S(2)}) %all-to-all-start.1) | async-done | bytes 65568 | tf_op jit(solution)/shard_map/all_to_all | solution.py:639
  35.8 1.6 %shard_map.98 = (bf16[16,54,128]{2,1,0:T(8,128)(2,1)}, f32[8,128]{1,0:T(8,128)}) custom-call(f32[16,8,128]{2,1,0:T(8,128)S(1)} %all-to-all-done.1.theirs_ref, f32[64,128]{1,0:T(8,128)S(1)} %get-tuple-element.37.cols_ref, f32[144,4608]{1,0:T(8,128)S(1)} %shard_map.97.outer_ref, bf16[8,8,2432]{2,1,0:T(8,128)(2,1)S(1)} %all-to-all-done.own_ref, ...), custom_call_target="tpu_custom_call" | custom-call | tf_op jit(solution)/shard_map/pallas_call | solution.py:653
  37.4 3.5 %all-to-all-start.2 = ((bf16[16,54,128]{2,1,0:T(8,128)(2,1)}), bf16[16,54,128]{2,1,0:T(8,128)(2,1)S(1)}, u32[]{:S(2)}, u32[]{:S(2)}) async-start(bf16[16,54,128]{2,1,0:T(8,128)(2,1)} %get-tuple-element.44), calls=%async_computation.2 | async-start | bytes 458752 | tf_op jit(solution)/shard_map/all_to_all | solution.py:668
  40.9 1.3 %slice_reduce_fusion = f32[8]{0:T(128)} fusion(f32[8,128]{1,0:T(8,128)} %get-tuple-element.43), kind=kLoop, calls=%fused_computation.4 | loop fusion | bytes 64 | tf_op jit(solution)/shard_map/slice | solution.py:672
  42.3 8.2 %all-to-all-done.2.back_ref = bf16[16,54,128]{2,1,0:T(8,128)(2,1)S(1)} async-done(((bf16[16,54,128]{2,1,0:T(8,128)(2,1)}), bf16[16,54,128]{2,1,0:T(8,128)(2,1)S(1)}, u32[]{:S(2)}, u32[]{:S(2)}) %all-to-all-start.2) | async-done | bytes 221216 | tf_op jit(solution)/shard_map/all_to_all | solution.py:668
  50.4 0.7 %shard_map.99 = (f32[144,128]{1,0:T(8,128)}, f32[18,128]{1,0:T(8,128)}) custom-call(bf16[16,54,128]{2,1,0:T(8,128)(2,1)S(1)} %all-to-all-done.2.back_ref), custom_call_target="tpu_custom_call" | custom-call | tf_op jit(solution)/shard_map/pallas_call | solution.py:669
  (4 shorter events, 0.0 us)
Async XLA Ops:
  2.6 17.3 %all-to-all-start = ((bf16[8,8,2432]{2,1,0:T(8,128)(2,1)}), bf16[8,8,2432]{2,1,0:T(8,128)(2,1)S(1)}, u32[]{:S(2)}, u32[]{:S(2)}) async-start(bf16[8,8,2432]{2,1,0:T(8,128)(2,1)} %get-tuple-element.25), calls=%async_computation | async-start | bytes 622592 | tf_op jit(solution)/shard_map/all_to_all | solution.py:591
  9.8 5.2 %collective-permute-start.1 = (f32[2,18,128]{2,1,0:T(8,128)S(1)}, f32[2,18,128]{2,1,0:T(8,128)S(1)}, u32[]{:S(2)}, u32[]{:S(2)}) collective-permute-start(f32[2,18,128]{2,1,0:T(8,128)S(1)} %get-tuple-element.32), channel_id=1, source_target_pairs={{0,2},{2,0},{1,3},{3,1},{4,6},{6,4},{5,7},{7,5},{8,10},{10,8},{9,1... | collective-permute-start | bytes 55304 | tf_op jit(solution)/shard_map/ppermute | solution.py:27
  11.9 3.2 %collective-permute-start.2 = (bf16[8,4608]{1,0:T(8,128)(2,1)S(1)}, bf16[8,4608]{1,0:T(8,128)(2,1)S(1)}, u32[]{:S(2)}, u32[]{:S(2)}) collective-permute-start(bf16[8,4608]{1,0:T(8,128)(2,1)S(1)} %get-tuple-element.28), channel_id=1, source_target_pairs={{0,1},{1,0},{2,3},{3,2},{4,5},{5,4},{6,7},{7,6},{8,9},{9,8},{10,11... | collective-permute-start | bytes 221192 | tf_op jit(solution)/shard_map/ppermute | solution.py:601
  11.9 6.0 %collective-permute-start.3 = (bf16[8,4608]{1,0:T(8,128)(2,1)S(1)}, bf16[8,4608]{1,0:T(8,128)(2,1)S(1)}, u32[]{:S(2)}, u32[]{:S(2)}) collective-permute-start(bf16[8,4608]{1,0:T(8,128)(2,1)S(1)} %get-tuple-element.29), channel_id=1, source_target_pairs={{0,2},{1,3},{2,0},{3,1},{4,6},{5,7},{6,4},{7,5},{8,10},{9,11},{10,... | collective-permute-start | bytes 221192 | tf_op jit(solution)/shard_map/ppermute | solution.py:601
  11.9 7.9 %collective-permute-start.4 = (bf16[8,4608]{1,0:T(8,128)(2,1)S(1)}, bf16[8,4608]{1,0:T(8,128)(2,1)S(1)}, u32[]{:S(2)}, u32[]{:S(2)}) collective-permute-start(bf16[8,4608]{1,0:T(8,128)(2,1)S(1)} %get-tuple-element.30), channel_id=1, source_target_pairs={{0,3},{1,2},{2,1},{3,0},{4,7},{5,6},{6,5},{7,4},{8,11},{9,10},{10,... | collective-permute-start | bytes 221192 | tf_op jit(solution)/shard_map/ppermute | solution.py:601
  19.9 2.8 %collective-permute-start = (bf16[8,8,2432]{2,1,0:T(8,128)(2,1)S(1)}, bf16[8,8,2432]{2,1,0:T(8,128)(2,1)S(1)}, u32[]{:S(2)}, u32[]{:S(2)}) collective-permute-start(bf16[8,8,2432]{2,1,0:T(8,128)(2,1)S(1)} %all-to-all-done.own_ref), channel_id=1, source_target_pairs={{0,1},{1,0},{2,3},{3,2},{4,5},{5,4},{6,7},{7,6},{8,9},{9,8},{10,11... | collective-permute-start | bytes 933896 | tf_op jit(solution)/shard_map/ppermute | solution.py:592
  24.8 10.9 %all-to-all-start.1 = ((f32[16,8,128]{2,1,0:T(8,128)}), f32[16,8,128]{2,1,0:T(8,128)S(1)}, u32[]{:S(2)}, u32[]{:S(2)}) async-start(f32[16,8,128]{2,1,0:T(8,128)} %get-tuple-element.36), calls=%async_computation.1 | async-start | bytes 131072 | tf_op jit(solution)/shard_map/all_to_all | solution.py:639
  37.4 13.0 %all-to-all-start.2 = ((bf16[16,54,128]{2,1,0:T(8,128)(2,1)}), bf16[16,54,128]{2,1,0:T(8,128)(2,1)S(1)}, u32[]{:S(2)}, u32[]{:S(2)}) async-start(bf16[16,54,128]{2,1,0:T(8,128)(2,1)} %get-tuple-element.44), calls=%async_computation.2 | async-start | bytes 458752 | tf_op jit(solution)/shard_map/all_to_all | solution.py:668

commit v6 on v5

--- a/solution.py
+++ b/solution.py
@@ -182,8 +182,8 @@
 
 
 def send_kernel(copies, pieces, base_hbm, hidden_hbm, in_hbm, out_hbm, gain_hbm, packed_hbm, vec_ref, *refs):
-    unit_refs = refs[: 2 * pieces]
-    base_ref, hidden_ref, in_ref, packed_ref, mix_ref, sems = refs[2 * pieces :]
+    unit_refs = refs[:2]
+    base_ref, hidden_ref, in_ref, packed_ref, mix_ref, sems = refs[2:]
     rows, hidden = hidden_ref.shape
     feat = base_ref.shape[1]
     quarter = hidden // (2 * pieces)
@@ -194,16 +194,15 @@
         pltpu.make_async_copy(out_hbm, vec_ref.at[0], sems.at[3]),
         pltpu.make_async_copy(gain_hbm, vec_ref.at[1], sems.at[4]),
     ]
-    m_i = lax.axis_index("mp")
     r_i = lax.axis_index("rep")
     for i in range(pieces):
         for j in range(2):
-            to = 2 * lax.rem(m_i + i, pieces) + lax.rem(r_i + j, 2)
-            start = pl.multiple_of(to * quarter, 128)
-            k = 2 * i + j
+            start = pl.multiple_of((2 * i + lax.rem(r_i + j, 2)) * quarter, 128)
             later.append(
                 pltpu.make_async_copy(
-                    hidden_hbm.at[:, pl.ds(start, quarter)], unit_refs[k], sems.at[7 + k]
+                    hidden_hbm.at[:, pl.ds(start, quarter)],
+                    unit_refs[j].at[i],
+                    sems.at[7 + 2 * i + j],
                 )
             )
     get_base.start()
@@ -400,13 +399,14 @@
 
 def outer_kernel(ops_hbm, head_hbm, outer_ref, ops_ref, head_ref, sems):
     both = outer_ref.shape[0] - 16
-    part = head_hbm.shape[0] // (sems.shape[0] - 1)
+    part = outer_ref.shape[1] // (sems.shape[0] - 1)
     get = pltpu.make_async_copy(ops_hbm, ops_ref, sems.at[0])
     get.start()
     moves = []
-    for i in range(head_hbm.shape[0] // part):
+    for i in range(outer_ref.shape[1] // part):
         span = pl.ds(i * part, part)
-        moves.append(pltpu.make_async_copy(head_hbm.at[span], head_ref.at[span], sems.at[1 + i]))
+        source = head_hbm.at[span]
+        moves.append(pltpu.make_async_copy(source, head_ref.at[span], sems.at[1 + i]))
     for move in moves:
         move.start()
     get.wait()
@@ -424,8 +424,8 @@
 
 
 def close_kernel(nv, nm, theirs_ref, cols_ref, outer_ref, own_ref, all_ref, *refs):
-    units = refs[: 2 * nm]
-    slab_hbm, penalty_hbm, coeff_ref, pen_ref, pull_ref, vec_ref, slab_ref, second_ref, sems = refs[2 * nm :]
+    units = refs[:nm]
+    slab_hbm, penalty_hbm, coeff_ref, pen_ref, pull_ref, vec_ref, slab_ref, second_ref, sems = refs[nm:]
     rows = own_ref.shape[1]
     feat = own_ref.shape[2] - 128
     model = outer_ref.shape[1]
@@ -484,8 +484,8 @@
         m = lax.rem(m_i - k + nm, nm)
         for t in range(units[0].shape[1] // 128):
             c = t * 128
-            row = units[2 * k][:, c : c + 128].astype(f32) * own[0]
-            row += units[2 * k + 1][:, c : c + 128].astype(f32) * own[1]
+            row = units[k][:rows, c : c + 128].astype(f32) * own[0]
+            row += units[k][rows:, c : c + 128].astype(f32) * own[1]
             vec_ref[m, pl.ds(tiles + t, 1), :] = jnp.sum(row, axis=0, keepdims=True)
     by_e = jnp.broadcast_to(weight * inv_e, (group, 128))
     by_b = jnp.broadcast_to(weight * inv_b, (group, 128))
@@ -565,13 +565,13 @@
     out_tiles = edit_out.reshape(tiles, 128)
     gain_tiles = norm_gain.reshape(tiles, 128)
 
-    packed, vectors, *units = call(
+    packed, vectors, keep, give = call(
         functools.partial(send_kernel, nv * nm, nm),
         (
             pltpu.HBM((nv * nm, rows, feat + 128), bf16),
             shape((2, tiles, 128), f32),
         )
-        + (shape((rows, quarter), bf16),) * (2 * nm),
+        + (shape((nm, rows, quarter), bf16),) * 2,
         [
             pltpu.VMEM((rows, feat), bf16),
             pltpu.VMEM((rows, hidden), bf16),
@@ -581,7 +581,7 @@
             pltpu.SemaphoreType.DMA((7 + 2 * nm,)),
         ],
         in_specs=[hbm] * 5,
-        out_specs=(hbm,) + (vmem,) * (1 + 2 * nm),
+        out_specs=(hbm,) + (vmem,) * 3,
     )(
         *(
             in_hbm(a)
@@ -590,15 +590,8 @@
     )
     got = lax.all_to_all(packed, ("vocab", "mp"), 0, 0)
     other = lax.ppermute(got, "rep", [(0, 1), (1, 0)])
-    for i in range(nm):
-        for j in range(2):
-            if i or j:
-                moves = [
-                    (2 * m + r, 2 * ((m + i) % nm) + (r + j) % 2)
-                    for m in range(nm)
-                    for r in range(2)
-                ]
-                units[2 * i + j] = lax.ppermute(units[2 * i + j], ("mp", "rep"), moves)
+    units = jnp.concatenate([keep, lax.ppermute(give, "rep", [(0, 1), (1, 0)])], axis=1)
+    units = [lax.dynamic_index_in_dim(units, (m_i + k) % nm, 0, keepdims=False) for k in range(nm)]
     vectors = from_peers(vectors, "mp", nm)
     vectors, units = lax.optimization_barrier((vectors, units))
     vectors = jnp.stack(in_order(vectors, m_i))
@@ -637,17 +630,21 @@
         out_specs=(hbm, vmem, hbm),
     )(other, vectors, ids, staged, early, early_cols)
     theirs = lax.all_to_all(slab, everyone, 0, 0)
+    parts = 3
     outer = call(
         outer_kernel,
         shape((2 * group + 16, model), f32),
         [
             pltpu.VMEM((4 * group + 16, voc), bf16),
             pltpu.VMEM((model, voc), bf16),
-            pltpu.SemaphoreType.DMA((4,)),
+            pltpu.SemaphoreType.DMA((1 + parts,)),
         ],
         12,
         in_specs=[hbm, hbm],
     )(in_hbm(ops), in_hbm(head))
+
+    moves = [[(m, (m + k) % nm) for m in range(nm)] for k in range(nm)]
+    units = [units[0]] + [lax.ppermute(units[k], "mp", moves[k]) for k in range(1, nm)]
 
     width = (feat + quarter) // 128
     slab, penalty = call(
@@ -662,7 +659,7 @@
             pltpu.VMEM((tiles, 128), f32),
             pltpu.SemaphoreType.DMA((1 + nm * nv,)),
         ],
-        in_specs=[vmem] * (5 + 2 * nm),
+        in_specs=[vmem] * (5 + nm),
         out_specs=(hbm, hbm),
     )(theirs, cols, outer, got, vectors, *units)
     back = lax.all_to_all(slab, everyone, 0, 0)

time: 51.5 us -> 51.2 us (level)
  local copies, waits for them, and re-layouts: 2.13 us -> 2.84 us
  starting transfers between devices: 18.9 us -> 18.2 us
    ppermute x3 -> x2, waiting for transfers between devices: 4.81 us -> 0.45 us  [the longest x1 0.45 us: fused(): lax.ppermute(give, 'rep', [(0, 1), (1, 0)])]
    all_to_all x1, waiting for transfers between devices: 0.01 us -> 3.23 us  [fused(): got = lax.all_to_all(packed, ('vocab', 'mp'), 0, 0)]
    ppermute x1, waiting for transfers between devices: 0.42 us -> 1.1 us  [from_peers(): lax.ppermute(value, axis, moves[k])]
    squeeze x0 -> x1, local copies, waits for them, and re-layouts: none -> 0.68 us  [fused(): lax.dynamic_index_in_dim(units, (m_i + k) % nm, 0, keepdims=False)]
    ppermute x3 -> x2, starting transfers between devices: 1.87 us -> 1.55 us  [the longest x1 1.55 us: fused(): lax.ppermute(units[k], 'mp', moves[k])]
  transfers between devices with their start and end apart: 8 -> 7, of which waited for: 5 -> 5; matrix products, arithmetic and copies ran while one was open for 4% -> 6% of each run, Pallas kernels for 12% -> 16%
where the time goes in v6:
time: 51.2 us; the launch traced here: 50.8 us
  starting transfers between devices  18.2 us (36%)
  waiting for transfers between devices  16.4 us (32%)
  Pallas kernels  12.5 us (24%)
  local copies, waits for them, and re-layouts  2.84 us (6%)
  between operations  0.8 us (2%)
    all_to_all x1, waiting for transfers between devices, fused(): back = lax.all_to_all(slab, everyone, 0, 0)  8.17 us
    all_to_all x1, starting transfers between devices, fused(): got = lax.all_to_all(packed, ('vocab', 'mp'), 0, 0)  7.26 us
    all_to_all x1, starting transfers between devices, fused(): theirs = lax.all_to_all(slab, everyone, 0, 0)  3.81 us
    all_to_all x1, starting transfers between devices, fused(): back = lax.all_to_all(slab, everyone, 0, 0)  3.54 us
    all_to_all x1, waiting for transfers between devices, fused(): theirs = lax.all_to_all(slab, everyone, 0, 0)  3.44 us
    pallas_call x1, Pallas kernels, fused(): call(outer_kernel, shape((2 * group + 16, model), f32), [pltpu.VMEM((4 *...  3.44 us
    all_to_all x1, waiting for transfers between devices, fused(): got = lax.all_to_all(packed, ('vocab', 'mp'), 0, 0)  3.23 us
    pallas_call x1, Pallas kernels, fused(): call(functools.partial(early_kernel, nv, nm), (pltpu.VMEM((model, voc), b...  2.63 us
  transfers between devices with their start and end apart: 7, of which 5 were waited for; matrix products, arithmetic and copies ran while one was open for 6% of the time, Pallas kernels for 16%

profile of v6, /device:TPU:0, one launch (start us, length us, event | category | flops | bytes accessed | tf_op | source)
XLA Modules:
  0.0 50.8 jit_solution(8381471902563794675)
XLA Ops:
  0.6 1.9 %shard_map.94 = (bf16[8,8,2432]{2,1,0:T(8,128)(2,1)}, f32[2,18,128]{2,1,0:T(8,128)S(1)}, bf16[2,8,4608]{2,1,0:T(8,128)(2,1)S(1)}, bf16[2,8,4608]{2,1,0:T(8,128)(2,1)S(1)}) custom-call(bf16[8,2304]{1,0:T(8,128)(2,1)} %base_hbm.1, bf16[8,18432]{1,0:T(8,128)(2,1)} %hidden_hbm.1, f32[1,18432]{1,0:T(1,128)} %bitcast.15, f32[18,128]{1,0:T(8,128)} %bitcast.16, ...), custom_call_target="tpu_custom_call" | custom-call | tf_op jit(solution)/shard_map/pallas_call | solution.py:568
  2.6 7.3 %all-to-all-start = ((bf16[8,8,2432]{2,1,0:T(8,128)(2,1)}), bf16[8,8,2432]{2,1,0:T(8,128)(2,1)S(1)}, u32[]{:S(2)}, u32[]{:S(2)}) async-start(bf16[8,8,2432]{2,1,0:T(8,128)(2,1)} %get-tuple-element.21), calls=%async_computation | async-start | bytes 622592 | tf_op jit(solution)/shard_map/all_to_all | solution.py:591
  9.8 2.0 %collective-permute-start.1 = (f32[2,18,128]{2,1,0:T(8,128)S(1)}, f32[2,18,128]{2,1,0:T(8,128)S(1)}, u32[]{:S(2)}, u32[]{:S(2)}) collective-permute-start(f32[2,18,128]{2,1,0:T(8,128)S(1)} %get-tuple-element.26), channel_id=1, source_target_pairs={{0,2},{2,0},{1,3},{3,1},{4,6},{6,4},{5,7},{7,5},{8,10},{10,8},{9,1... | collective-permute-start | bytes 55304 | tf_op jit(solution)/shard_map/ppermute | solution.py:27
  11.9 0.0 collective-permute-start.2
  11.9 0.7 %reshape.30 = s32[4,2,8]{2,1,0:T(2,128)S(1)} reshape(s32[64]{0:T(128)} %param.13) | data formatting | bytes 512 | tf_op jit(solution)/shard_map/reshape | solution.py:611
  12.7 0.1 reshape.34.ids_ref
  12.8 0.4 collective-permute-done.2
  13.3 0.7 %dynamic-slice_bitcast_fusion = (bf16[16,4608]{1,0:T(8,128)(2,1)}, bf16[16,4608]{1,0:T(8,128)(2,1)S(1)}) fusion(bf16[2,16,4608]{2,1,0:T(8,128)(2,1)S(1)} %constant_dynamic-update-slice_fusion, s32[]{:T(128)S(6)} %select_n.57, s32[]{:T(128)S(6)} %select_n.55), kind=kLoop, calls=%fused_computation | loop fusion | bytes 589832 | tf_op jit(solution)/shard_map/jit(dynamic_index_in_dim)/squeeze | solution.py:594
  13.9 1.1 %collective-permute-done.1 = f32[2,18,128]{2,1,0:T(8,128)S(1)} collective-permute-done((f32[2,18,128]{2,1,0:T(8,128)S(1)}, f32[2,18,128]{2,1,0:T(8,128)S(1)}, u32[]{:S(2)}, u32[]{:S(2)}) %collective-permute-start.1) | collective-permute-done | bytes 18464 | tf_op jit(solution)/shard_map/ppermute | solution.py:27
  15.0 1.5 %collective-permute-start.3 = (bf16[16,4608]{1,0:T(8,128)(2,1)}, bf16[16,4608]{1,0:T(8,128)(2,1)S(1)}, u32[]{:S(2)}, u32[]{:S(2)}) collective-permute-start(bf16[16,4608]{1,0:T(8,128)(2,1)} %get-tuple-element.34), channel_id=1, source_target_pairs={{0,2},{2,0},{1,3},{3,1},{4,6},{6,4},{5,7},{7,5},{8,10},{10,8},{9,1... | collective-permute-start | bytes 442376 | tf_op jit(solution)/shard_map/ppermute | solution.py:647
  16.6 3.2 %all-to-all-done.own_ref = bf16[8,8,2432]{2,1,0:T(8,128)(2,1)S(1)} async-done(((bf16[8,8,2432]{2,1,0:T(8,128)(2,1)}), bf16[8,8,2432]{2,1,0:T(8,128)(2,1)S(1)}, u32[]{:S(2)}, u32[]{:S(2)}) %all-to-all-start) | async-done | bytes 311328 | tf_op jit(solution)/shard_map/all_to_all | solution.py:591
  19.8 0.0 collective-permute-start
  19.8 2.6 %shard_map.95 = (bf16[4608,512]{1,0:T(8,128)(2,1)S(1)}, f32[80,512]{1,0:T(8,128)S(1)}, f32[32,128]{1,0:T(8,128)S(1)}) custom-call(bf16[8,8,2432]{2,1,0:T(8,128)(2,1)S(1)} %all-to-all-done.own_ref, f32[2,2,18,128]{3,2,1,0:T(8,128)S(1)} %pad_maximum_fusion.vec_ref.all_ref, bf16[4608,512]{1,0:T(8,128)(2,1)} %head_hbm.3), custom_call_target="tpu_custom_call" | custom-call | tf_op jit(solution)/shard_map/pallas_call | solution.py:599
  22.5 0.0 collective-permute-done.other_ref
  22.5 2.2 %shard_map.96 = (f32[16,8,128]{2,1,0:T(8,128)}, f32[64,128]{1,0:T(8,128)S(1)}, bf16[272,512]{1,0:T(8,128)(2,1)}) custom-call(bf16[8,8,2432]{2,1,0:T(8,128)(2,1)S(1)} %collective-permute-done.other_ref, f32[2,2,18,128]{3,2,1,0:T(8,128)S(1)} %pad_maximum_fusion.vec_ref.all_ref, s32[64,1]{1,0:T(8,128)S(1)} %reshape.34.ids_ref, ...), custom_call_target="tpu_custom_call" | custom-call | tf_op jit(solution)/shard_map/pallas_call | solution.py:616
  24.7 3.8 %all-to-all-start.1 = ((f32[16,8,128]{2,1,0:T(8,128)}), f32[16,8,128]{2,1,0:T(8,128)S(1)}, u32[]{:S(2)}, u32[]{:S(2)}) async-start(f32[16,8,128]{2,1,0:T(8,128)} %get-tuple-element.30), calls=%async_computation.1 | async-start | bytes 131072 | tf_op jit(solution)/shard_map/all_to_all | solution.py:632
  28.5 3.4 %shard_map.97.outer_ref = f32[144,4608]{1,0:T(8,128)S(1)} custom-call(bf16[272,512]{1,0:T(8,128)(2,1)} %get-tuple-element.32.ops_hbm, bf16[4608,512]{1,0:T(8,128)(2,1)} %head_hbm.3), custom_call_target="tpu_custom_call" | custom-call | tf_op jit(solution)/shard_map/pallas_call | solution.py:634
  31.9 0.0 collective-permute-done.3.refs_1_
  32.0 3.4 %all-to-all-done.1.theirs_ref = f32[16,8,128]{2,1,0:T(8,128)S(1)} async-done(((f32[16,8,128]{2,1,0:T(8,128)}), f32[16,8,128]{2,1,0:T(8,128)S(1)}, u32[]{:S(2)}, u32[]{:S(2)}) %all-to-all-start.1) | async-done | bytes 65568 | tf_op jit(solution)/shard_map/all_to_all | solution.py:632
  35.4 1.7 %shard_map.98 = (bf16[16,54,128]{2,1,0:T(8,128)(2,1)}, f32[8,128]{1,0:T(8,128)}) custom-call(f32[16,8,128]{2,1,0:T(8,128)S(1)} %all-to-all-done.1.theirs_ref, f32[64,128]{1,0:T(8,128)S(1)} %get-tuple-element.31.cols_ref, f32[144,4608]{1,0:T(8,128)S(1)} %shard_map.97.outer_ref, bf16[8,8,2432]{2,1,0:T(8,128)(2,1)S(1)} %all-to-all-done.own_ref, ...), custom_call_target="tpu_custom_call" | custom-call | tf_op jit(solution)/shard_map/pallas_call | solution.py:650
  37.1 3.5 %all-to-all-start.2 = ((bf16[16,54,128]{2,1,0:T(8,128)(2,1)}), bf16[16,54,128]{2,1,0:T(8,128)(2,1)S(1)}, u32[]{:S(2)}, u32[]{:S(2)}) async-start(bf16[16,54,128]{2,1,0:T(8,128)(2,1)} %get-tuple-element.36), calls=%async_computation.2 | async-start | bytes 458752 | tf_op jit(solution)/shard_map/all_to_all | solution.py:665
  40.6 1.3 %slice_reduce_fusion = f32[8]{0:T(128)} fusion(f32[8,128]{1,0:T(8,128)} %get-tuple-element.35), kind=kLoop, calls=%fused_computation.8 | loop fusion | bytes 64 | tf_op jit(solution)/shard_map/slice | solution.py:669
  41.9 8.2 %all-to-all-done.2.back_ref = bf16[16,54,128]{2,1,0:T(8,128)(2,1)S(1)} async-done(((bf16[16,54,128]{2,1,0:T(8,128)(2,1)}), bf16[16,54,128]{2,1,0:T(8,128)(2,1)S(1)}, u32[]{:S(2)}, u32[]{:S(2)}) %all-to-all-start.2) | async-done | bytes 221216 | tf_op jit(solution)/shard_map/all_to_all | solution.py:665
  50.1 0.7 %shard_map.99 = (f32[144,128]{1,0:T(8,128)}, f32[18,128]{1,0:T(8,128)}) custom-call(bf16[16,54,128]{2,1,0:T(8,128)(2,1)S(1)} %all-to-all-done.2.back_ref), custom_call_target="tpu_custom_call" | custom-call | tf_op jit(solution)/shard_map/pallas_call | solution.py:666
  (6 shorter events, 0.1 us)
Async XLA Ops:
  2.6 17.2 %all-to-all-start = ((bf16[8,8,2432]{2,1,0:T(8,128)(2,1)}), bf16[8,8,2432]{2,1,0:T(8,128)(2,1)S(1)}, u32[]{:S(2)}, u32[]{:S(2)}) async-start(bf16[8,8,2432]{2,1,0:T(8,128)(2,1)} %get-tuple-element.21), calls=%async_computation | async-start | bytes 622592 | tf_op jit(solution)/shard_map/all_to_all | solution.py:591
  9.8 5.2 %collective-permute-start.1 = (f32[2,18,128]{2,1,0:T(8,128)S(1)}, f32[2,18,128]{2,1,0:T(8,128)S(1)}, u32[]{:S(2)}, u32[]{:S(2)}) collective-permute-start(f32[2,18,128]{2,1,0:T(8,128)S(1)} %get-tuple-element.26), channel_id=1, source_target_pairs={{0,2},{2,0},{1,3},{3,1},{4,6},{6,4},{5,7},{7,5},{8,10},{10,8},{9,1... | collective-permute-start | bytes 55304 | tf_op jit(solution)/shard_map/ppermute | solution.py:27
  11.9 1.4 %collective-permute-start.2 = (bf16[2,8,4608]{2,1,0:T(8,128)(2,1)S(1)}, bf16[2,8,4608]{2,1,0:T(8,128)(2,1)S(1)}, u32[]{:S(2)}, u32[]{:S(2)}) collective-permute-start(bf16[2,8,4608]{2,1,0:T(8,128)(2,1)S(1)} %get-tuple-element.24), channel_id=1, source_target_pairs={{0,1},{1,0},{2,3},{3,2},{4,5},{5,4},{6,7},{7,6},{8,9},{9,8},{10,11... | collective-permute-start | bytes 442376 | tf_op jit(solution)/shard_map/ppermute | solution.py:593
  15.0 16.9 %collective-permute-start.3 = (bf16[16,4608]{1,0:T(8,128)(2,1)}, bf16[16,4608]{1,0:T(8,128)(2,1)S(1)}, u32[]{:S(2)}, u32[]{:S(2)}) collective-permute-start(bf16[16,4608]{1,0:T(8,128)(2,1)} %get-tuple-element.34), channel_id=1, source_target_pairs={{0,2},{2,0},{1,3},{3,1},{4,6},{6,4},{5,7},{7,5},{8,10},{10,8},{9,1... | collective-permute-start | bytes 442376 | tf_op jit(solution)/shard_map/ppermute | solution.py:647
  19.8 2.7 %collective-permute-start = (bf16[8,8,2432]{2,1,0:T(8,128)(2,1)S(1)}, bf16[8,8,2432]{2,1,0:T(8,128)(2,1)S(1)}, u32[]{:S(2)}, u32[]{:S(2)}) collective-permute-start(bf16[8,8,2432]{2,1,0:T(8,128)(2,1)S(1)} %all-to-all-done.own_ref), channel_id=1, source_target_pairs={{0,1},{1,0},{2,3},{3,2},{4,5},{5,4},{6,7},{7,6},{8,9},{9,8},{10,11... | collective-permute-start | bytes 933896 | tf_op jit(solution)/shard_map/ppermute | solution.py:592
  24.7 10.7 %all-to-all-start.1 = ((f32[16,8,128]{2,1,0:T(8,128)}), f32[16,8,128]{2,1,0:T(8,128)S(1)}, u32[]{:S(2)}, u32[]{:S(2)}) async-start(f32[16,8,128]{2,1,0:T(8,128)} %get-tuple-element.30), calls=%async_computation.1 | async-start | bytes 131072 | tf_op jit(solution)/shard_map/all_to_all | solution.py:632
  37.1 13.0 %all-to-all-start.2 = ((bf16[16,54,128]{2,1,0:T(8,128)(2,1)}), bf16[16,54,128]{2,1,0:T(8,128)(2,1)S(1)}, u32[]{:S(2)}, u32[]{:S(2)}) async-start(bf16[16,54,128]{2,1,0:T(8,128)(2,1)} %get-tuple-element.36), calls=%async_computation.2 | async-start | bytes 458752 | tf_op jit(solution)/shard_map/all_to_all | solution.py:665

commit v7 on v6

--- a/solution.py
+++ b/solution.py
@@ -289,15 +289,30 @@
                 x_ref[half + at : half + at + pair, d : d + 128] = (b * scale_b * gain).astype(bf16)
 
 
-def early_kernel(nv, nm, own_ref, vec_ref, head_hbm, head_ref, pre_ref, cols_ref, x_ref, sems):
-    model = head_hbm.shape[0]
-    part = model // sems.shape[0]
+def stage_kernel(after_ref, head_hbm, head_ref, sems):
+    part = head_ref.shape[0] // sems.shape[0]
     moves = []
     for i in range(sems.shape[0]):
         span = pl.ds(i * part, part)
         moves.append(pltpu.make_async_copy(head_hbm.at[span], head_ref.at[span], sems.at[i]))
+        moves[i].start()
     for move in moves:
+        move.wait()
+
+
+def early_kernel(nv, nm, own_ref, vec_ref, staged_ref, head_hbm, head_ref, pre_ref, cols_ref, x_ref, sems):
+    model = head_hbm.shape[0]
+    first = staged_ref.shape[0]
+    part = (model - first) // sems.shape[0]
+    moves = []
+    for i in range(sems.shape[0]):
+        move = pltpu.make_async_copy(
+            head_hbm.at[pl.ds(first + i * part, part)],
+            head_ref.at[pl.ds(i * part, part)],
+            sems.at[i],
+        )
         move.start()
+        moves.append(move)
     feat = own_ref.shape[2] - 128
     half = cols_ref.shape[0]
     normed_rows(nv, nm, own_ref, vec_ref, cols_ref, x_ref)
@@ -311,22 +326,27 @@
             block = jnp.where(sub == i, piece, block)
             rest = rest - piece
         x_ref[2 * half :, d : d + 128] = block.astype(bf16)
-    pre = None
+    pre = jnp.dot(x_ref[:, :first], staged_ref[...], preferred_element_type=f32)
     for i, move in enumerate(moves):
         move.wait()
-        span = slice(i * part, (i + 1) * part)
-        block = jnp.dot(x_ref[:, span], head_ref[span, :], preferred_element_type=f32)
-        pre = block if pre is None else pre + block
+        at = i * part
+        pre += jnp.dot(
+            x_ref[:, first + at : first + at + part],
+            head_ref[at : at + part, :],
+            preferred_element_type=f32,
+        )
     pre_ref[...] = pre
 
 
-def score_kernel(nv, nm, other_ref, vec_ref, ids_ref, head_ref, early_ref, early_cols_ref, slab_hbm, cols_ref, ops_hbm, x_ref, slab_ref, ops_ref, sems):
+def score_kernel(nv, nm, other_ref, vec_ref, ids_ref, staged_ref, head_ref, early_ref, early_cols_ref, slab_hbm, cols_ref, ops_hbm, x_ref, slab_ref, ops_ref, sems):
     voc = head_ref.shape[1]
     half = early_cols_ref.shape[0]
     group = 2 * half
     cols_ref[:half] = early_cols_ref[...]
     normed_rows(nv, nm, other_ref, vec_ref, cols_ref.at[half:], x_ref)
-    late = jnp.dot(x_ref[...], head_ref[...], preferred_element_type=f32)
+    first = staged_ref.shape[0]
+    late = jnp.dot(x_ref[:, :first], staged_ref[...], preferred_element_type=f32)
+    late += jnp.dot(x_ref[:, first:], head_ref[...], preferred_element_type=f32)
     pre_edit = jnp.concatenate([early_ref[:half], late[:half]], axis=0)
     pre_base = jnp.concatenate([early_ref[half:group], late[half:]], axis=0)
     toward = jnp.sum(early_ref[group:], axis=0, keepdims=True)
@@ -590,24 +610,37 @@
     )
     got = lax.all_to_all(packed, ("vocab", "mp"), 0, 0)
     other = lax.ppermute(got, "rep", [(0, 1), (1, 0)])
-    units = jnp.concatenate([keep, lax.ppermute(give, "rep", [(0, 1), (1, 0)])], axis=1)
-    units = [lax.dynamic_index_in_dim(units, (m_i + k) % nm, 0, keepdims=False) for k in range(nm)]
+    took = lax.ppermute(give, "rep", [(0, 1), (1, 0)])
+    units = [
+        jnp.concatenate(
+            [lax.dynamic_index_in_dim(a, (m_i + k) % nm, 0, keepdims=False) for a in (keep, took)]
+        )
+        for k in range(nm)
+    ]
     vectors = from_peers(vectors, "mp", nm)
-    vectors, units = lax.optimization_barrier((vectors, units))
+    first = model * 5 // 9
+    staged = call(
+        stage_kernel,
+        pltpu.VMEM((first, voc), bf16),
+        [pltpu.SemaphoreType.DMA((5,))],
+        in_specs=[vmem, hbm],
+        out_specs=vmem,
+    )(took, in_hbm(head))
+    vectors, units, staged = lax.optimization_barrier((vectors, units, staged))
     vectors = jnp.stack(in_order(vectors, m_i))
     half = group // 2
-    staged, early, early_cols = call(
+    unstaged, early, early_cols = call(
         functools.partial(early_kernel, nv, nm),
         (
-            pltpu.VMEM((model, voc), bf16),
+            pltpu.VMEM((model - first, voc), bf16),
             shape((group + 16, voc), f32),
             shape((half, 128), f32),
         ),
-        [pltpu.VMEM((group + 16, model), bf16), pltpu.SemaphoreType.DMA((6,))],
+        [pltpu.VMEM((group + 16, model), bf16), pltpu.SemaphoreType.DMA((4,))],
         8,
-        in_specs=[vmem, vmem, hbm],
+        in_specs=[vmem, vmem, vmem, hbm],
         out_specs=(vmem, vmem, vmem),
-    )(got, vectors, in_hbm(head))
+    )(got, vectors, staged, in_hbm(head))
     ids = token_ids.reshape(nv, nr, rows)
     ids = jnp.concatenate(
         [lax.dynamic_index_in_dim(ids, (r_i + k) % nr, 1, keepdims=False) for k in range(nr)]
@@ -626,9 +659,9 @@
             pltpu.VMEM((4 * group + 16, voc), bf16),
             pltpu.SemaphoreType.DMA((2,)),
         ],
-        in_specs=[vmem] * 6,
+        in_specs=[vmem] * 7,
         out_specs=(hbm, vmem, hbm),
-    )(other, vectors, ids, staged, early, early_cols)
+    )(other, vectors, ids, staged, unstaged, early, early_cols)
     theirs = lax.all_to_all(slab, everyone, 0, 0)
     parts = 3
     outer = call(

time: 51.2 us -> 50.6 us (0.988)
  Pallas kernels: 12.5 us -> 13.6 us
  waiting for transfers between devices: 16.4 us -> 15.3 us
  other arithmetic: 0.02 us -> 0.7 us
  local copies, waits for them, and re-layouts: 2.84 us -> 2.16 us
  starting transfers between devices: 18.2 us -> 17.6 us
    pallas_call x1 -> x2, Pallas kernels: 2.63 us -> 3.77 us  [the longest x1 2.06 us: fused(): call(functools.partial(early_kernel, nv, nm), (pltpu.VMEM((model - first,...]
    ppermute x1, waiting for transfers between devices: 1.1 us -> 0.01 us  [from_peers(): lax.ppermute(value, axis, moves[k])]
    concatenate x0 -> x1, other arithmetic: none -> 0.68 us  [fused(): jnp.concatenate([lax.dynamic_index_in_dim(a, (m_i + k) % nm, 0, keepdims=...]
    squeeze x1 -> x2, local copies, waits for them, and re-layouts: 0.68 us -> 0.02 us  [fused(): lax.dynamic_index_in_dim(a, (m_i + k) % nm, 0, keepdims=False)]
    ppermute x1, starting transfers between devices: 1.55 us -> 0.92 us  [fused(): lax.ppermute(units[k], 'mp', moves[k])]
  transfers between devices with their start and end apart: 7 -> 7, of which waited for: 5 -> 4; matrix products, arithmetic and copies ran while one was open for 6% -> 6% of each run, Pallas kernels for 16% -> 19%
where the time goes in v7:
time: 50.6 us; the launch traced here: 50.1 us
  starting transfers between devices  17.6 us (35%)
  waiting for transfers between devices  15.3 us (30%)
  Pallas kernels  13.6 us (27%)
  local copies, waits for them, and re-layouts  2.16 us (4%)
  between operations  0.79 us (2%)
  other arithmetic  0.7 us (1%)
    all_to_all x1, waiting for transfers between devices, fused(): back = lax.all_to_all(slab, everyone, 0, 0)  8.17 us
    all_to_all x1, starting transfers between devices, fused(): got = lax.all_to_all(packed, ('vocab', 'mp'), 0, 0)  7.26 us
    all_to_all x1, starting transfers between devices, fused(): theirs = lax.all_to_all(slab, everyone, 0, 0)  3.81 us
    all_to_all x1, starting transfers between devices, fused(): back = lax.all_to_all(slab, everyone, 0, 0)  3.54 us
    pallas_call x1, Pallas kernels, fused(): call(outer_kernel, shape((2 * group + 16, model), f32), [pltpu.VMEM((4 *...  3.44 us
    all_to_all x1, waiting for transfers between devices, fused(): theirs = lax.all_to_all(slab, everyone, 0, 0)  3.44 us
    all_to_all x1, waiting for transfers between devices, fused(): got = lax.all_to_all(packed, ('vocab', 'mp'), 0, 0)  3.23 us
    pallas_call x1, Pallas kernels, fused(): call(functools.partial(score_kernel, nv, nm), (pltpu.HBM((peers, 8, 128),...  2.14 us
  transfers between devices with their start and end apart: 7, of which 4 were waited for; matrix products, arithmetic and copies ran while one was open for 6% of the time, Pallas kernels for 19%

profile of v7, /device:TPU:0, one launch (start us, length us, event | category | flops | bytes accessed | tf_op | source)
XLA Modules:
  0.0 50.1 jit_solution(5362683232174623978)
XLA Ops:
  0.6 1.9 %shard_map.94 = (bf16[8,8,2432]{2,1,0:T(8,128)(2,1)}, f32[2,18,128]{2,1,0:T(8,128)S(1)}, bf16[2,8,4608]{2,1,0:T(8,128)(2,1)S(1)}, bf16[2,8,4608]{2,1,0:T(8,128)(2,1)S(1)}) custom-call(bf16[8,2304]{1,0:T(8,128)(2,1)} %base_hbm.1, bf16[8,18432]{1,0:T(8,128)(2,1)} %hidden_hbm.1, f32[1,18432]{1,0:T(1,128)} %bitcast.19, f32[18,128]{1,0:T(8,128)} %bitcast.20, ...), custom_call_target="tpu_custom_call" | custom-call | tf_op jit(solution)/shard_map/pallas_call | solution.py:588
  2.6 7.3 %all-to-all-start = ((bf16[8,8,2432]{2,1,0:T(8,128)(2,1)}), bf16[8,8,2432]{2,1,0:T(8,128)(2,1)S(1)}, u32[]{:S(2)}, u32[]{:S(2)}) async-start(bf16[8,8,2432]{2,1,0:T(8,128)(2,1)} %get-tuple-element.22), calls=%async_computation | async-start | bytes 622592 | tf_op jit(solution)/shard_map/all_to_all | solution.py:611
  9.8 2.0 %collective-permute-start.1 = (f32[2,18,128]{2,1,0:T(8,128)S(1)}, f32[2,18,128]{2,1,0:T(8,128)S(1)}, u32[]{:S(2)}, u32[]{:S(2)}) collective-permute-start(f32[2,18,128]{2,1,0:T(8,128)S(1)} %get-tuple-element.27), channel_id=1, source_target_pairs={{0,2},{2,0},{1,3},{3,1},{4,6},{6,4},{5,7},{7,5},{8,10},{10,8},{9,1... | collective-permute-start | bytes 55304 | tf_op jit(solution)/shard_map/ppermute | solution.py:27
  11.8 0.0 collective-permute-start.2
  11.9 0.7 %reshape.30 = s32[4,2,8]{2,1,0:T(2,128)S(1)} reshape(s32[64]{0:T(128)} %param.13) | data formatting | bytes 512 | tf_op jit(solution)/shard_map/reshape | solution.py:644
  12.7 0.1 reshape.34.ids_ref
  12.7 0.5 collective-permute-done.2.after_ref
  13.2 0.7 %pad_maximum_fusion = (bf16[16,4608]{1,0:T(8,128)(2,1)S(1)}, bf16[16,4608]{1,0:T(8,128)(2,1)}) fusion(bf16[8,4608]{1,0:T(8,128)(2,1)S(1)} %get-tuple-element.44, bf16[8,4608]{1,0:T(8,128)(2,1)S(1)} %get-tuple-element.42, bf16[8,4608]{1,0:T(8,128)(2,1)S(1)} %get-tuple-element.43, bf16[8,4608]{1,0:T(8,128)(2,1)S(1)} %get-tuple-element.41), kind=kLoop, calls=%fused_computation | loop fusion | flops 589824 | bytes 589824 | tf_op jit(solution)/shard_map/concatenate | solution.py:615
  13.9 1.7 %shard_map.95.staged_ref = bf16[2560,512]{1,0:T(8,128)(2,1)S(1)} custom-call(bf16[2,8,4608]{2,1,0:T(8,128)(2,1)S(1)} %collective-permute-done.2.after_ref, bf16[4608,512]{1,0:T(8,128)(2,1)} %head_hbm.5), custom_call_target="tpu_custom_call" | custom-call | tf_op jit(solution)/shard_map/pallas_call | solution.py:622
  15.6 0.0 collective-permute-done.1
  15.6 0.9 %collective-permute-start.3 = (bf16[16,4608]{1,0:T(8,128)(2,1)}, bf16[16,4608]{1,0:T(8,128)(2,1)S(1)}, u32[]{:S(2)}, u32[]{:S(2)}) collective-permute-start(bf16[16,4608]{1,0:T(8,128)(2,1)} %get-tuple-element.36), channel_id=1, source_target_pairs={{0,2},{2,0},{1,3},{3,1},{4,6},{6,4},{5,7},{7,5},{8,10},{10,8},{9,1... | collective-permute-start | bytes 442376 | tf_op jit(solution)/shard_map/ppermute | solution.py:680
  16.6 3.2 %all-to-all-done.own_ref = bf16[8,8,2432]{2,1,0:T(8,128)(2,1)S(1)} async-done(((bf16[8,8,2432]{2,1,0:T(8,128)(2,1)}), bf16[8,8,2432]{2,1,0:T(8,128)(2,1)S(1)}, u32[]{:S(2)}, u32[]{:S(2)}) %all-to-all-start) | async-done | bytes 311328 | tf_op jit(solution)/shard_map/all_to_all | solution.py:611
  19.8 0.0 collective-permute-start
  19.8 2.1 %shard_map.96 = (bf16[2048,512]{1,0:T(8,128)(2,1)S(1)}, f32[80,512]{1,0:T(8,128)S(1)}, f32[32,128]{1,0:T(8,128)S(1)}) custom-call(bf16[8,8,2432]{2,1,0:T(8,128)(2,1)S(1)} %all-to-all-done.own_ref, f32[2,2,18,128]{3,2,1,0:T(8,128)S(1)} %pad_maximum_fusion.2.vec_ref.all_ref, bf16[2560,512]{1,0:T(8,128)(2,1)S(1)} %shard_map.95.staged_ref, ...), custom_call_target="tpu_custom_call" | custom-call | tf_op jit(solution)/shard_map/pallas_call | solution.py:632
  21.9 0.0 collective-permute-done.other_ref
  21.9 2.1 %shard_map.97 = (f32[16,8,128]{2,1,0:T(8,128)}, f32[64,128]{1,0:T(8,128)S(1)}, bf16[272,512]{1,0:T(8,128)(2,1)}) custom-call(bf16[8,8,2432]{2,1,0:T(8,128)(2,1)S(1)} %collective-permute-done.other_ref, f32[2,2,18,128]{3,2,1,0:T(8,128)S(1)} %pad_maximum_fusion.2.vec_ref.all_ref, s32[64,1]{1,0:T(8,128)S(1)} %reshape.34.ids_ref, ...), custom_call_target="tpu_custom_call" | custom-call | tf_op jit(solution)/shard_map/pallas_call | solution.py:649
  24.1 3.8 %all-to-all-start.1 = ((f32[16,8,128]{2,1,0:T(8,128)}), f32[16,8,128]{2,1,0:T(8,128)S(1)}, u32[]{:S(2)}, u32[]{:S(2)}) async-start(f32[16,8,128]{2,1,0:T(8,128)} %get-tuple-element.32), calls=%async_computation.1 | async-start | bytes 131072 | tf_op jit(solution)/shard_map/all_to_all | solution.py:665
  27.9 3.4 %shard_map.98.outer_ref = f32[144,4608]{1,0:T(8,128)S(1)} custom-call(bf16[272,512]{1,0:T(8,128)(2,1)} %get-tuple-element.34.ops_hbm, bf16[4608,512]{1,0:T(8,128)(2,1)} %head_hbm.5), custom_call_target="tpu_custom_call" | custom-call | tf_op jit(solution)/shard_map/pallas_call | solution.py:667
  31.3 0.0 collective-permute-done.3.refs_1_
  31.3 3.4 %all-to-all-done.1.theirs_ref = f32[16,8,128]{2,1,0:T(8,128)S(1)} async-done(((f32[16,8,128]{2,1,0:T(8,128)}), f32[16,8,128]{2,1,0:T(8,128)S(1)}, u32[]{:S(2)}, u32[]{:S(2)}) %all-to-all-start.1) | async-done | bytes 65568 | tf_op jit(solution)/shard_map/all_to_all | solution.py:665
  34.8 1.7 %shard_map.99 = (bf16[16,54,128]{2,1,0:T(8,128)(2,1)}, f32[8,128]{1,0:T(8,128)}) custom-call(f32[16,8,128]{2,1,0:T(8,128)S(1)} %all-to-all-done.1.theirs_ref, f32[64,128]{1,0:T(8,128)S(1)} %get-tuple-element.33.cols_ref, f32[144,4608]{1,0:T(8,128)S(1)} %shard_map.98.outer_ref, bf16[8,8,2432]{2,1,0:T(8,128)(2,1)S(1)} %all-to-all-done.own_ref, ...), custom_call_target="tpu_custom_call" | custom-call | tf_op jit(solution)/shard_map/pallas_call | solution.py:683
  36.4 3.5 %all-to-all-start.2 = ((bf16[16,54,128]{2,1,0:T(8,128)(2,1)}), bf16[16,54,128]{2,1,0:T(8,128)(2,1)S(1)}, u32[]{:S(2)}, u32[]{:S(2)}) async-start(bf16[16,54,128]{2,1,0:T(8,128)(2,1)} %get-tuple-element.38), calls=%async_computation.2 | async-start | bytes 458752 | tf_op jit(solution)/shard_map/all_to_all | solution.py:698
  40.0 1.3 %slice_reduce_fusion = f32[8]{0:T(128)} fusion(f32[8,128]{1,0:T(8,128)} %get-tuple-element.37), kind=kLoop, calls=%fused_computation.10 | loop fusion | bytes 64 | tf_op jit(solution)/shard_map/slice | solution.py:702
  41.3 8.2 %all-to-all-done.2.back_ref = bf16[16,54,128]{2,1,0:T(8,128)(2,1)S(1)} async-done(((bf16[16,54,128]{2,1,0:T(8,128)(2,1)}), bf16[16,54,128]{2,1,0:T(8,128)(2,1)S(1)}, u32[]{:S(2)}, u32[]{:S(2)}) %all-to-all-start.2) | async-done | bytes 221216 | tf_op jit(solution)/shard_map/all_to_all | solution.py:698
  49.5 0.7 %shard_map.100 = (f32[144,128]{1,0:T(8,128)}, f32[18,128]{1,0:T(8,128)}) custom-call(bf16[16,54,128]{2,1,0:T(8,128)(2,1)S(1)} %all-to-all-done.2.back_ref), custom_call_target="tpu_custom_call" | custom-call | tf_op jit(solution)/shard_map/pallas_call | solution.py:699
  (6 shorter events, 0.1 us)
Async XLA Ops:
  2.6 17.2 %all-to-all-start = ((bf16[8,8,2432]{2,1,0:T(8,128)(2,1)}), bf16[8,8,2432]{2,1,0:T(8,128)(2,1)S(1)}, u32[]{:S(2)}, u32[]{:S(2)}) async-start(bf16[8,8,2432]{2,1,0:T(8,128)(2,1)} %get-tuple-element.22), calls=%async_computation | async-start | bytes 622592 | tf_op jit(solution)/shard_map/all_to_all | solution.py:611
  9.8 5.8 %collective-permute-start.1 = (f32[2,18,128]{2,1,0:T(8,128)S(1)}, f32[2,18,128]{2,1,0:T(8,128)S(1)}, u32[]{:S(2)}, u32[]{:S(2)}) collective-permute-start(f32[2,18,128]{2,1,0:T(8,128)S(1)} %get-tuple-element.27), channel_id=1, source_target_pairs={{0,2},{2,0},{1,3},{3,1},{4,6},{6,4},{5,7},{7,5},{8,10},{10,8},{9,1... | collective-permute-start | bytes 55304 | tf_op jit(solution)/shard_map/ppermute | solution.py:27
  11.8 1.4 %collective-permute-start.2 = (bf16[2,8,4608]{2,1,0:T(8,128)(2,1)S(1)}, bf16[2,8,4608]{2,1,0:T(8,128)(2,1)S(1)}, u32[]{:S(2)}, u32[]{:S(2)}) collective-permute-start(bf16[2,8,4608]{2,1,0:T(8,128)(2,1)S(1)} %get-tuple-element.25), channel_id=1, source_target_pairs={{0,1},{1,0},{2,3},{3,2},{4,5},{5,4},{6,7},{7,6},{8,9},{9,8},{10,11... | collective-permute-start | bytes 442376 | tf_op jit(solution)/shard_map/ppermute | solution.py:613
  15.6 15.7 %collective-permute-start.3 = (bf16[16,4608]{1,0:T(8,128)(2,1)}, bf16[16,4608]{1,0:T(8,128)(2,1)S(1)}, u32[]{:S(2)}, u32[]{:S(2)}) collective-permute-start(bf16[16,4608]{1,0:T(8,128)(2,1)} %get-tuple-element.36), channel_id=1, source_target_pairs={{0,2},{2,0},{1,3},{3,1},{4,6},{6,4},{5,7},{7,5},{8,10},{10,8},{9,1... | collective-permute-start | bytes 442376 | tf_op jit(solution)/shard_map/ppermute | solution.py:680
  19.8 2.1 %collective-permute-start = (bf16[8,8,2432]{2,1,0:T(8,128)(2,1)S(1)}, bf16[8,8,2432]{2,1,0:T(8,128)(2,1)S(1)}, u32[]{:S(2)}, u32[]{:S(2)}) collective-permute-start(bf16[8,8,2432]{2,1,0:T(8,128)(2,1)S(1)} %all-to-all-done.own_ref), channel_id=1, source_target_pairs={{0,1},{1,0},{2,3},{3,2},{4,5},{5,4},{6,7},{7,6},{8,9},{9,8},{10,11... | collective-permute-start | bytes 933896 | tf_op jit(solution)/shard_map/ppermute | solution.py:612
  24.1 10.7 %all-to-all-start.1 = ((f32[16,8,128]{2,1,0:T(8,128)}), f32[16,8,128]{2,1,0:T(8,128)S(1)}, u32[]{:S(2)}, u32[]{:S(2)}) async-start(f32[16,8,128]{2,1,0:T(8,128)} %get-tuple-element.32), calls=%async_computation.1 | async-start | bytes 131072 | tf_op jit(solution)/shard_map/all_to_all | solution.py:665
  36.4 13.0 %all-to-all-start.2 = ((bf16[16,54,128]{2,1,0:T(8,128)(2,1)}), bf16[16,54,128]{2,1,0:T(8,128)(2,1)S(1)}, u32[]{:S(2)}, u32[]{:S(2)}) async-start(bf16[16,54,128]{2,1,0:T(8,128)(2,1)} %get-tuple-element.38), calls=%async_computation.2 | async-start | bytes 458752 | tf_op jit(solution)/shard_map/all_to_all | solution.py:698

commit v8 on v7

--- a/solution.py
+++ b/solution.py
@@ -217,10 +217,13 @@
     put_base.start()
     get_hidden.wait()
     get_in.wait()
-    total = jnp.zeros((rows, 128), f32)
-    for c in range(0, hidden, 128):
-        total += hidden_ref[:, c : c + 128].astype(f32) * in_ref[:, c : c + 128]
-    mix = jnp.sum(total, axis=1, keepdims=True)
+    totals = [jnp.zeros((rows, 128), f32)] * 8
+    for i, c in enumerate(range(0, hidden, 128)):
+        product = hidden_ref[:, c : c + 128].astype(f32) * in_ref[:, c : c + 128]
+        totals[i % 8] = totals[i % 8] + product
+    while len(totals) > 1:
+        totals = [a + b for a, b in zip(totals[::2], totals[1::2])]
+    mix = jnp.sum(totals[0], axis=1, keepdims=True)
     lane = lax.broadcasted_iota(jnp.int32, (rows, 128), 1)
     cols = jnp.zeros((rows, 128), f32)
     for i in range(3):
@@ -445,7 +448,7 @@
 
 def close_kernel(nv, nm, theirs_ref, cols_ref, outer_ref, own_ref, all_ref, *refs):
     units = refs[:nm]
-    slab_hbm, penalty_hbm, coeff_ref, pen_ref, pull_ref, vec_ref, slab_ref, second_ref, sems = refs[nm:]
+    slab_hbm, penalty_hbm, coeff_ref, pen_ref, pull_ref, vec_ref, slab_ref, second_ref, line_ref, sems = refs[nm:]
     rows = own_ref.shape[1]
     feat = own_ref.shape[2] - 128
     model = outer_ref.shape[1]
@@ -482,9 +485,12 @@
     pull = weight * shrink
     coeff_ref[...] = jnp.broadcast_to(coeff, (group, 128))
     pen_ref[...] = jnp.broadcast_to(penalty, (group, 128))
-    put_pen = pltpu.make_async_copy(
-        pen_ref.at[pl.ds(pl.multiple_of(v_i * rows, rows), rows)], penalty_hbm, sems.at[0]
-    )
+    mine = pen_ref[pl.ds(pl.multiple_of(v_i * rows, rows), rows), :]
+    diagonal = lax.broadcasted_iota(jnp.int32, (rows, 128), 0) == lax.broadcasted_iota(
+        jnp.int32, (rows, 128), 1
+    )
+    line_ref[...] = jnp.sum(jnp.where(diagonal, mine, 0.0), axis=0, keepdims=True)[:, :rows]
+    put_pen = pltpu.make_async_copy(line_ref, penalty_hbm, sems.at[0])
     put_pen.start()
 
     pull_ref[...] = jnp.broadcast_to(pull, (group, 128))
@@ -521,15 +527,10 @@
                 m_i == m, second_ref[t : t + 1, :], 0.0
             )
             vec_ref[m, t : t + 1, :] = row
-        block = vec_ref[m].astype(bf16)
-        for v in range(nv):
-            for r in range(2):
-                slab_ref[m, 2 * v + r] = block
+        slab_ref[m] = vec_ref[m].astype(bf16)
         for v in range(nv):
             put = pltpu.make_async_copy(
-                slab_ref.at[m, pl.ds(2 * v, 2)],
-                slab_hbm.at[pl.ds((v * nm + m) * 2, 2)],
-                sems.at[1 + v * nm + m],
+                slab_ref.at[m], slab_hbm.at[v * nm + m], sems.at[1 + v * nm + m]
             )
             put.start()
             puts.append(put)
@@ -538,19 +539,30 @@
         put.wait()
 
 
-def sum_kernel(back_ref, in_ref, out_ref):
-    peers = back_ref.shape[0]
-    tiles = out_ref.shape[0]
-    units = back_ref.shape[1] - tiles
-    pieces = in_ref.shape[0] // units
+def sum_kernel(nm, back_ref, sums_ref):
+    senders = back_ref.shape[0]
+    units = (sums_ref.shape[0] - back_ref.shape[1]) // (nm - 1)
+    tiles = back_ref.shape[1] - units
     wide = jnp.zeros((tiles, 128), f32)
-    for q in range(pieces):
-        total = back_ref[q].astype(f32)
-        for p in range(q + pieces, peers, pieces):
+    for m in range(nm):
+        total = back_ref[m].astype(f32)
+        for p in range(m + nm, senders, nm):
             total += back_ref[p].astype(f32)
         wide += total[:tiles]
-        in_ref[q * units : (q + 1) * units, :] = total[tiles:]
-    out_ref[...] = wide
+        sums_ref[m * units : (m + 1) * units, :] = total[tiles:]
+    sums_ref[nm * units :, :] = wide
+
+
+def join_kernel(nm, own_ref, other_ref, in_ref, out_ref):
+    units = in_ref.shape[0] // (2 * nm)
+    even = lax.axis_index("rep") == 0
+    for m in range(nm):
+        own = own_ref[m * units : (m + 1) * units, :]
+        other = other_ref[m * units : (m + 1) * units, :]
+        at = 2 * m * units
+        in_ref[at : at + units, :] = jnp.where(even, own, other)
+        in_ref[at + units : at + 2 * units, :] = jnp.where(even, other, own)
+    out_ref[...] = own_ref[nm * units :, :] + other_ref[nm * units :, :]
 
 
 def in_hbm(value):
@@ -682,31 +694,37 @@
     width = (feat + quarter) // 128
     slab, penalty = call(
         functools.partial(close_kernel, nv, nm),
-        (pltpu.HBM((peers, width, 128), bf16), pltpu.HBM((rows, 128), f32)),
+        (pltpu.HBM((nv * nm, width, 128), bf16), pltpu.HBM((1, rows), f32)),
         [
             pltpu.VMEM((group, 128), f32),
             pltpu.VMEM((group, 128), f32),
             pltpu.VMEM((group, 128), f32),
             pltpu.VMEM((nm, width, 128), f32),
-            pltpu.VMEM((nm, 2 * nv, width, 128), bf16),
+            pltpu.VMEM((nm, width, 128), bf16),
             pltpu.VMEM((tiles, 128), f32),
+            pltpu.VMEM((1, rows), f32),
             pltpu.SemaphoreType.DMA((1 + nm * nv,)),
         ],
         in_specs=[vmem] * (5 + nm),
         out_specs=(hbm, hbm),
     )(theirs, cols, outer, got, vectors, *units)
-    back = lax.all_to_all(slab, everyone, 0, 0)
+    back = lax.all_to_all(slab, ("vocab", "mp"), 0, 0)
+    sums = call(
+        functools.partial(sum_kernel, nm), shape((nm * quarter // 128 + tiles, 128), f32)
+    )(back)
+    others = lax.ppermute(sums, "rep", [(0, 1), (1, 0)])
     grad_in, grad_out = call(
-        sum_kernel, (shape((hidden // 128, 128), f32), shape((tiles, 128), f32))
-    )(back)
-    return (penalty[:, 0], grad_in.reshape(hidden), grad_out.reshape(feat))
+        functools.partial(join_kernel, nm),
+        (shape((hidden // 128, 128), f32), shape((tiles, 128), f32)),
+    )(sums, others)
+    return (penalty.reshape(rows), grad_in.reshape(hidden), grad_out.reshape(feat))
 
 
 def local(nv, nm, nr, resid_base, mlp_hidden, *rest):
     rows, feat = resid_base.shape
     quarter = mlp_hidden.shape[1] // (nm * nr)
     whole_tiles = rows == 8 and feat % 128 == 0 and quarter % 128 == 0
-    small = nr == 2 and nv % 2 == 0 and nv * nr * rows == 64
+    small = nr == 2 and nm > 1 and nv % 2 == 0 and nv * nr * rows == 64
     step = fused if whole_tiles and small else plain
     return step(nv, nm, nr, resid_base, mlp_hidden, *rest)
 

time: 50.6 us -> 49.2 us (0.972)
  blocking collectives: 0 us -> 10.5 us
  waiting for transfers between devices: 15.3 us -> 8.37 us
  starting transfers between devices: 17.6 us -> 14.1 us
  local copies, waits for them, and re-layouts: 2.16 us -> 0.84 us
    all_to_all x0 -> x1, blocking collectives: none -> 10.5 us  [fused(): back = lax.all_to_all(slab, ('vocab', 'mp'), 0, 0)]
    all_to_all x1 -> x0, waiting for transfers between devices: 8.17 us -> none  [fused(): back = lax.all_to_all(slab, everyone, 0, 0)]
    all_to_all x1 -> x0, starting transfers between devices: 3.54 us -> none  [fused(): back = lax.all_to_all(slab, everyone, 0, 0)]
    slice x1 -> x0, local copies, waits for them, and re-layouts: 1.31 us -> none  [fused(): return (penalty[:, 0], grad_in.reshape(hidden), grad_out.reshape(feat))]
    ppermute x0 -> x1, waiting for transfers between devices: none -> 1.22 us  [fused(): others = lax.ppermute(sums, 'rep', [(0, 1), (1, 0)])]
    pallas_call x2 -> x3, Pallas kernels: 2.33 us -> 2.26 us  [the longest x1 1.6 us: fused(): call(functools.partial(close_kernel, nv, nm), (pltpu.HBM((nv * nm, width,...]
  transfers between devices with their start and end apart: 7 -> 7, of which waited for: 4 -> 4; matrix products, arithmetic and copies ran while one was open for 6% -> 3% of each run, Pallas kernels for 19% -> 19%
where the time goes in v8:
time: 49.2 us; the launch traced here: 48.8 us
  starting transfers between devices  14.1 us (29%)
  Pallas kernels  13.5 us (27%)
  blocking collectives  10.5 us (21%)
  waiting for transfers between devices  8.37 us (17%)
  local copies, waits for them, and re-layouts  0.84 us (2%)
  between operations  0.79 us (2%)
  other arithmetic  0.7 us (1%)
    all_to_all x1, blocking collectives, fused(): back = lax.all_to_all(slab, ('vocab', 'mp'), 0, 0)  10.5 us
    all_to_all x1, starting transfers between devices, fused(): got = lax.all_to_all(packed, ('vocab', 'mp'), 0, 0)  7.26 us
    all_to_all x1, starting transfers between devices, fused(): theirs = lax.all_to_all(slab, everyone, 0, 0)  3.81 us
    all_to_all x1, waiting for transfers between devices, fused(): theirs = lax.all_to_all(slab, everyone, 0, 0)  3.44 us
    pallas_call x1, Pallas kernels, fused(): call(outer_kernel, shape((2 * group + 16, model), f32), [pltpu.VMEM((4 *...  3.44 us
    all_to_all x1, waiting for transfers between devices, fused(): got = lax.all_to_all(packed, ('vocab', 'mp'), 0, 0)  3.23 us
    pallas_call x1, Pallas kernels, fused(): call(functools.partial(score_kernel, nv, nm), (pltpu.HBM((peers, 8, 128),...  2.15 us
    pallas_call x1, Pallas kernels, fused(): call(functools.partial(early_kernel, nv, nm), (pltpu.VMEM((model - first,...  2.06 us
  transfers between devices with their start and end apart: 7, of which 4 were waited for; matrix products, arithmetic and copies ran while one was open for 3% of the time, Pallas kernels for 19%

profile of v8, /device:TPU:0, one launch (start us, length us, event | category | flops | bytes accessed | tf_op | source)
XLA Modules:
  0.0 48.8 jit_solution(17224655537168710966)
XLA Ops:
  0.6 1.8 %shard_map.94 = (bf16[8,8,2432]{2,1,0:T(8,128)(2,1)}, f32[2,18,128]{2,1,0:T(8,128)S(1)}, bf16[2,8,4608]{2,1,0:T(8,128)(2,1)S(1)}, bf16[2,8,4608]{2,1,0:T(8,128)(2,1)S(1)}) custom-call(bf16[8,2304]{1,0:T(8,128)(2,1)} %base_hbm.1, bf16[8,18432]{1,0:T(8,128)(2,1)} %hidden_hbm.1, f32[1,18432]{1,0:T(1,128)} %bitcast.20, f32[18,128]{1,0:T(8,128)} %bitcast.21, ...), custom_call_target="tpu_custom_call" | custom-call | tf_op jit(solution)/shard_map/pallas_call | solution.py:600
  2.5 7.3 %all-to-all-start = ((bf16[8,8,2432]{2,1,0:T(8,128)(2,1)}), bf16[8,8,2432]{2,1,0:T(8,128)(2,1)S(1)}, u32[]{:S(2)}, u32[]{:S(2)}) async-start(bf16[8,8,2432]{2,1,0:T(8,128)(2,1)} %get-tuple-element.22), calls=%async_computation | async-start | bytes 622592 | tf_op jit(solution)/shard_map/all_to_all | solution.py:623
  9.7 2.0 %collective-permute-start.1 = (f32[2,18,128]{2,1,0:T(8,128)S(1)}, f32[2,18,128]{2,1,0:T(8,128)S(1)}, u32[]{:S(2)}, u32[]{:S(2)}) collective-permute-start(f32[2,18,128]{2,1,0:T(8,128)S(1)} %get-tuple-element.27), channel_id=1, source_target_pairs={{0,2},{2,0},{1,3},{3,1},{4,6},{6,4},{5,7},{7,5},{8,10},{10,8},{9,1... | collective-permute-start | bytes 55304 | tf_op jit(solution)/shard_map/ppermute | solution.py:27
  11.8 0.0 collective-permute-start.2
  11.8 0.7 %reshape.33 = s32[4,2,8]{2,1,0:T(2,128)S(1)} reshape(s32[64]{0:T(128)} %param.13) | data formatting | bytes 512 | tf_op jit(solution)/shard_map/reshape | solution.py:656
  12.6 0.1 reshape.38.ids_ref
  12.7 0.5 collective-permute-done.2.after_ref
  13.1 0.7 %pad_maximum_fusion = (bf16[16,4608]{1,0:T(8,128)(2,1)S(1)}, bf16[16,4608]{1,0:T(8,128)(2,1)}) fusion(bf16[8,4608]{1,0:T(8,128)(2,1)S(1)} %get-tuple-element.44, bf16[8,4608]{1,0:T(8,128)(2,1)S(1)} %get-tuple-element.42, bf16[8,4608]{1,0:T(8,128)(2,1)S(1)} %get-tuple-element.43, bf16[8,4608]{1,0:T(8,128)(2,1)S(1)} %get-tuple-element.41), kind=kLoop, calls=%fused_computation | loop fusion | flops 589824 | bytes 589824 | tf_op jit(solution)/shard_map/concatenate | solution.py:627
  13.8 1.7 %shard_map.95.staged_ref = bf16[2560,512]{1,0:T(8,128)(2,1)S(1)} custom-call(bf16[2,8,4608]{2,1,0:T(8,128)(2,1)S(1)} %collective-permute-done.2.after_ref, bf16[4608,512]{1,0:T(8,128)(2,1)} %head_hbm.5), custom_call_target="tpu_custom_call" | custom-call | tf_op jit(solution)/shard_map/pallas_call | solution.py:634
  15.5 0.0 collective-permute-done.1
  15.6 0.9 %collective-permute-start.3 = (bf16[16,4608]{1,0:T(8,128)(2,1)}, bf16[16,4608]{1,0:T(8,128)(2,1)S(1)}, u32[]{:S(2)}, u32[]{:S(2)}) collective-permute-start(bf16[16,4608]{1,0:T(8,128)(2,1)} %get-tuple-element.36), channel_id=1, source_target_pairs={{0,2},{2,0},{1,3},{3,1},{4,6},{6,4},{5,7},{7,5},{8,10},{10,8},{9,1... | collective-permute-start | bytes 442376 | tf_op jit(solution)/shard_map/ppermute | solution.py:692
  16.5 3.2 %all-to-all-done.own_ref = bf16[8,8,2432]{2,1,0:T(8,128)(2,1)S(1)} async-done(((bf16[8,8,2432]{2,1,0:T(8,128)(2,1)}), bf16[8,8,2432]{2,1,0:T(8,128)(2,1)S(1)}, u32[]{:S(2)}, u32[]{:S(2)}) %all-to-all-start) | async-done | bytes 311328 | tf_op jit(solution)/shard_map/all_to_all | solution.py:623
  19.7 0.0 collective-permute-start
  19.7 2.1 %shard_map.96 = (bf16[2048,512]{1,0:T(8,128)(2,1)S(1)}, f32[80,512]{1,0:T(8,128)S(1)}, f32[32,128]{1,0:T(8,128)S(1)}) custom-call(bf16[8,8,2432]{2,1,0:T(8,128)(2,1)S(1)} %all-to-all-done.own_ref, f32[2,2,18,128]{3,2,1,0:T(8,128)S(1)} %pad_maximum_fusion.2.vec_ref.all_ref, bf16[2560,512]{1,0:T(8,128)(2,1)S(1)} %shard_map.95.staged_ref, ...), custom_call_target="tpu_custom_call" | custom-call | tf_op jit(solution)/shard_map/pallas_call | solution.py:644
  21.8 0.0 collective-permute-done.other_ref
  21.8 2.2 %shard_map.97 = (f32[16,8,128]{2,1,0:T(8,128)}, f32[64,128]{1,0:T(8,128)S(1)}, bf16[272,512]{1,0:T(8,128)(2,1)}) custom-call(bf16[8,8,2432]{2,1,0:T(8,128)(2,1)S(1)} %collective-permute-done.other_ref, f32[2,2,18,128]{3,2,1,0:T(8,128)S(1)} %pad_maximum_fusion.2.vec_ref.all_ref, s32[64,1]{1,0:T(8,128)S(1)} %reshape.38.ids_ref, ...), custom_call_target="tpu_custom_call" | custom-call | tf_op jit(solution)/shard_map/pallas_call | solution.py:661
  24.0 3.8 %all-to-all-start.1 = ((f32[16,8,128]{2,1,0:T(8,128)}), f32[16,8,128]{2,1,0:T(8,128)S(1)}, u32[]{:S(2)}, u32[]{:S(2)}) async-start(f32[16,8,128]{2,1,0:T(8,128)} %get-tuple-element.32), calls=%async_computation.1 | async-start | bytes 131072 | tf_op jit(solution)/shard_map/all_to_all | solution.py:677
  27.8 3.4 %shard_map.98.outer_ref = f32[144,4608]{1,0:T(8,128)S(1)} custom-call(bf16[272,512]{1,0:T(8,128)(2,1)} %get-tuple-element.34.ops_hbm, bf16[4608,512]{1,0:T(8,128)(2,1)} %head_hbm.5), custom_call_target="tpu_custom_call" | custom-call | tf_op jit(solution)/shard_map/pallas_call | solution.py:679
  31.2 0.0 collective-permute-done.3.refs_1_
  31.2 3.4 %all-to-all-done.1.theirs_ref = f32[16,8,128]{2,1,0:T(8,128)S(1)} async-done(((f32[16,8,128]{2,1,0:T(8,128)}), f32[16,8,128]{2,1,0:T(8,128)S(1)}, u32[]{:S(2)}, u32[]{:S(2)}) %all-to-all-start.1) | async-done | bytes 65568 | tf_op jit(solution)/shard_map/all_to_all | solution.py:677
  34.7 1.6 %shard_map.99 = (bf16[8,54,128]{2,1,0:T(8,128)(2,1)}, f32[1,8]{1,0:T(1,128)}) custom-call(f32[16,8,128]{2,1,0:T(8,128)S(1)} %all-to-all-done.1.theirs_ref, f32[64,128]{1,0:T(8,128)S(1)} %get-tuple-element.33.cols_ref, f32[144,4608]{1,0:T(8,128)S(1)} %shard_map.98.outer_ref, bf16[8,8,2432]{2,1,0:T(8,128)(2,1)S(1)} %all-to-all-done.own_ref, ...), custom_call_target="tpu_custom_call" | custom-call | tf_op jit(solution)/shard_map/pallas_call | solution.py:695
  36.3 10.5 %all_to_all.15.back_ref = bf16[8,54,128]{2,1,0:T(8,128)(2,1)S(1)} all-to-all(bf16[8,54,128]{2,1,0:T(8,128)(2,1)} %get-tuple-element.38), channel_id=1, replica_groups=mesh['parts'=2,'vocab'=4,'mp'=2,'rep'=2] {'vocab','mp'}, dimensions={0} | all-to-all | bytes 221184 | tf_op jit(solution)/shard_map/all_to_all | solution.py:711
  46.8 0.1 collective-permute-start.4
  46.9 1.2 %collective-permute-done.4.other_ref = f32[90,128]{1,0:T(8,128)S(1)} collective-permute-done((f32[90,128]{1,0:T(8,128)S(1)}, f32[90,128]{1,0:T(8,128)S(1)}, u32[]{:S(2)}, u32[]{:S(2)}) %collective-permute-start.4) | collective-permute-done | bytes 46112 | tf_op jit(solution)/shard_map/ppermute | solution.py:715
  48.1 0.6 %shard_map.101 = (f32[144,128]{1,0:T(8,128)}, f32[18,128]{1,0:T(8,128)}) custom-call(f32[90,128]{1,0:T(8,128)S(1)} %shard_map.100.own_ref, f32[90,128]{1,0:T(8,128)S(1)} %collective-permute-done.4.other_ref), custom_call_target="tpu_custom_call" | custom-call | tf_op jit(solution)/shard_map/pallas_call | solution.py:716
  (7 shorter events, 0.1 us)
Async XLA Ops:
  2.5 17.2 %all-to-all-start = ((bf16[8,8,2432]{2,1,0:T(8,128)(2,1)}), bf16[8,8,2432]{2,1,0:T(8,128)(2,1)S(1)}, u32[]{:S(2)}, u32[]{:S(2)}) async-start(bf16[8,8,2432]{2,1,0:T(8,128)(2,1)} %get-tuple-element.22), calls=%async_computation | async-start | bytes 622592 | tf_op jit(solution)/shard_map/all_to_all | solution.py:623
  9.7 5.8 %collective-permute-start.1 = (f32[2,18,128]{2,1,0:T(8,128)S(1)}, f32[2,18,128]{2,1,0:T(8,128)S(1)}, u32[]{:S(2)}, u32[]{:S(2)}) collective-permute-start(f32[2,18,128]{2,1,0:T(8,128)S(1)} %get-tuple-element.27), channel_id=1, source_target_pairs={{0,2},{2,0},{1,3},{3,1},{4,6},{6,4},{5,7},{7,5},{8,10},{10,8},{9,1... | collective-permute-start | bytes 55304 | tf_op jit(solution)/shard_map/ppermute | solution.py:27
  11.8 1.4 %collective-permute-start.2 = (bf16[2,8,4608]{2,1,0:T(8,128)(2,1)S(1)}, bf16[2,8,4608]{2,1,0:T(8,128)(2,1)S(1)}, u32[]{:S(2)}, u32[]{:S(2)}) collective-permute-start(bf16[2,8,4608]{2,1,0:T(8,128)(2,1)S(1)} %get-tuple-element.25), channel_id=1, source_target_pairs={{0,1},{1,0},{2,3},{3,2},{4,5},{5,4},{6,7},{7,6},{8,9},{9,8},{10,11... | collective-permute-start | bytes 442376 | tf_op jit(solution)/shard_map/ppermute | solution.py:625
  15.6 15.7 %collective-permute-start.3 = (bf16[16,4608]{1,0:T(8,128)(2,1)}, bf16[16,4608]{1,0:T(8,128)(2,1)S(1)}, u32[]{:S(2)}, u32[]{:S(2)}) collective-permute-start(bf16[16,4608]{1,0:T(8,128)(2,1)} %get-tuple-element.36), channel_id=1, source_target_pairs={{0,2},{2,0},{1,3},{3,1},{4,6},{6,4},{5,7},{7,5},{8,10},{10,8},{9,1... | collective-permute-start | bytes 442376 | tf_op jit(solution)/shard_map/ppermute | solution.py:692
  19.7 2.1 %collective-permute-start = (bf16[8,8,2432]{2,1,0:T(8,128)(2,1)S(1)}, bf16[8,8,2432]{2,1,0:T(8,128)(2,1)S(1)}, u32[]{:S(2)}, u32[]{:S(2)}) collective-permute-start(bf16[8,8,2432]{2,1,0:T(8,128)(2,1)S(1)} %all-to-all-done.own_ref), channel_id=1, source_target_pairs={{0,1},{1,0},{2,3},{3,2},{4,5},{5,4},{6,7},{7,6},{8,9},{9,8},{10,11... | collective-permute-start | bytes 933896 | tf_op jit(solution)/shard_map/ppermute | solution.py:624
  24.0 10.7 %all-to-all-start.1 = ((f32[16,8,128]{2,1,0:T(8,128)}), f32[16,8,128]{2,1,0:T(8,128)S(1)}, u32[]{:S(2)}, u32[]{:S(2)}) async-start(f32[16,8,128]{2,1,0:T(8,128)} %get-tuple-element.32), calls=%async_computation.1 | async-start | bytes 131072 | tf_op jit(solution)/shard_map/all_to_all | solution.py:677
  46.8 1.3 %collective-permute-start.4 = (f32[90,128]{1,0:T(8,128)S(1)}, f32[90,128]{1,0:T(8,128)S(1)}, u32[]{:S(2)}, u32[]{:S(2)}) collective-permute-start(f32[90,128]{1,0:T(8,128)S(1)} %shard_map.100.own_ref), channel_id=1, source_target_pairs={{0,1},{1,0},{2,3},{3,2},{4,5},{5,4},{6,7},{7,6},{8,9},{9,8},{10,11... | collective-permute-start | bytes 138248 | tf_op jit(solution)/shard_map/ppermute | solution.py:715

commit v9 on v8

--- a/solution.py
+++ b/solution.py
@@ -385,32 +385,36 @@
     put_ops = pltpu.make_async_copy(ops_ref, ops_hbm, sems.at[1])
     put_ops.start()
 
-    def total(a):
-        return jnp.sum(a, axis=1, keepdims=True)
-
-    sums = [
-        total(exp_edit),
-        total(exp_base),
-        total(exp_base * diff),
-        total(jnp.where(hit, diff, 0.0)),
-        total(pe * pre_edit),
-        total(pb * pre_edit),
-        total(po * pre_edit),
-        total(pe * toward),
-        total(pb * toward),
-        total(po * toward),
+    def lanes(a):
+        part = a[:, :128]
+        for c in range(128, voc, 128):
+            part += a[:, c : c + 128]
+        return part
+
+    parts = [
+        lanes(a)
+        for a in (
+            exp_edit,
+            exp_base,
+            exp_base * diff,
+            jnp.where(hit, diff, 0.0),
+            pe * pre_edit,
+            pb * pre_edit,
+            po * pre_edit,
+            pe * toward,
+            pb * toward,
+            po * toward,
+        )
     ]
-    lane = lax.broadcasted_iota(jnp.int32, (group, 128), 1)
-    first = jnp.zeros((group, 128), f32)
-    second = jnp.zeros((group, 128), f32)
-    for i in range(8):
-        first = jnp.where(lane == i, sums[i], first)
-    for i in range(8, 10):
-        second = jnp.where(lane == i - 8, sums[i], second)
-    straight = jnp.concatenate([first, second], axis=0)
-    swapped = jnp.concatenate([first[half:], first[:half], second[half:], second[:half]], axis=0)
-    table = jnp.where(lax.axis_index("rep") == 0, straight, swapped)
-    table = table.T[:8]
+    even = lax.axis_index("rep") == 0
+    sub = lax.broadcasted_iota(jnp.int32, (8, 128), 0)
+    table = jnp.zeros((8, 128), f32)
+    for i in range(5):
+        a, b = parts[i], parts[i + 5]
+        straight = jnp.concatenate([a, b], axis=0)
+        swapped = jnp.concatenate([a[half:], a[:half], b[half:], b[:half]], axis=0)
+        row = jnp.sum(jnp.where(even, straight, swapped).T, axis=0, keepdims=True)
+        table = jnp.where(sub == i, row, table)
     for p in range(slab_ref.shape[0]):
         slab_ref[p] = table
     put_slab = pltpu.make_async_copy(slab_ref, slab_hbm, sems.at[0])
@@ -469,8 +473,8 @@
     swap_second = jnp.concatenate([second[half:], second[:half]], axis=0)
     first = jnp.where(r_i == 0, first, swap_first)
     second = jnp.where(r_i == 0, second, swap_second)
-    se, sb, kl, gap, ae, ab, ao, te = [first[:, i : i + 1] for i in range(8)]
-    tb, to = second[:, 0:1], second[:, 1:2]
+    se, sb, kl, gap, ae = [first[:, i : i + 1] for i in range(5)]
+    ab, ao, te, tb, to = [second[:, i : i + 1] for i in range(5)]
     mix = cols_ref[:, 0:1]
     scale = cols_ref[:, 1:2]
     along = cols_ref[:, 2:3]

time: 49.2 us -> 49.2 us (level)
  no operation moved by 1% of the time
where the time goes in v9:
time: 49.2 us; the launch traced here: 48.8 us
  starting transfers between devices  14.1 us (29%)
  Pallas kernels  13.4 us (27%)
  blocking collectives  10.5 us (21%)
  waiting for transfers between devices  8.37 us (17%)
  local copies, waits for them, and re-layouts  0.84 us (2%)
  between operations  0.79 us (2%)
  other arithmetic  0.7 us (1%)
    all_to_all x1, blocking collectives, fused(): back = lax.all_to_all(slab, ('vocab', 'mp'), 0, 0)  10.5 us
    all_to_all x1, starting transfers between devices, fused(): got = lax.all_to_all(packed, ('vocab', 'mp'), 0, 0)  7.26 us
    all_to_all x1, starting transfers between devices, fused(): theirs = lax.all_to_all(slab, everyone, 0, 0)  3.81 us
    all_to_all x1, waiting for transfers between devices, fused(): theirs = lax.all_to_all(slab, everyone, 0, 0)  3.44 us
    pallas_call x1, Pallas kernels, fused(): call(outer_kernel, shape((2 * group + 16, model), f32), [pltpu.VMEM((4 *...  3.43 us
    all_to_all x1, waiting for transfers between devices, fused(): got = lax.all_to_all(packed, ('vocab', 'mp'), 0, 0)  3.23 us
    pallas_call x1, Pallas kernels, fused(): call(functools.partial(score_kernel, nv, nm), (pltpu.HBM((peers, 8, 128),...  2.15 us
    pallas_call x1, Pallas kernels, fused(): call(functools.partial(early_kernel, nv, nm), (pltpu.VMEM((model - first,...  2.06 us
  transfers between devices with their start and end apart: 7, of which 4 were waited for; matrix products, arithmetic and copies ran while one was open for 3% of the time, Pallas kernels for 19%

profile of v9, /device:TPU:0, one launch (start us, length us, event | category | flops | bytes accessed | tf_op | source)
XLA Modules:
  0.0 48.8 jit_solution(11559840138770529538)
XLA Ops:
  0.6 1.8 %shard_map.94 = (bf16[8,8,2432]{2,1,0:T(8,128)(2,1)}, f32[2,18,128]{2,1,0:T(8,128)S(1)}, bf16[2,8,4608]{2,1,0:T(8,128)(2,1)S(1)}, bf16[2,8,4608]{2,1,0:T(8,128)(2,1)S(1)}) custom-call(bf16[8,2304]{1,0:T(8,128)(2,1)} %base_hbm.1, bf16[8,18432]{1,0:T(8,128)(2,1)} %hidden_hbm.1, f32[1,18432]{1,0:T(1,128)} %bitcast.20, f32[18,128]{1,0:T(8,128)} %bitcast.21, ...), custom_call_target="tpu_custom_call" | custom-call | tf_op jit(solution)/shard_map/pallas_call | solution.py:604
  2.5 7.3 %all-to-all-start = ((bf16[8,8,2432]{2,1,0:T(8,128)(2,1)}), bf16[8,8,2432]{2,1,0:T(8,128)(2,1)S(1)}, u32[]{:S(2)}, u32[]{:S(2)}) async-start(bf16[8,8,2432]{2,1,0:T(8,128)(2,1)} %get-tuple-element.22), calls=%async_computation | async-start | bytes 622592 | tf_op jit(solution)/shard_map/all_to_all | solution.py:627
  9.7 2.0 %collective-permute-start.1 = (f32[2,18,128]{2,1,0:T(8,128)S(1)}, f32[2,18,128]{2,1,0:T(8,128)S(1)}, u32[]{:S(2)}, u32[]{:S(2)}) collective-permute-start(f32[2,18,128]{2,1,0:T(8,128)S(1)} %get-tuple-element.27), channel_id=1, source_target_pairs={{0,2},{2,0},{1,3},{3,1},{4,6},{6,4},{5,7},{7,5},{8,10},{10,8},{9,1... | collective-permute-start | bytes 55304 | tf_op jit(solution)/shard_map/ppermute | solution.py:27
  11.8 0.0 collective-permute-start.2
  11.8 0.7 %reshape.33 = s32[4,2,8]{2,1,0:T(2,128)S(1)} reshape(s32[64]{0:T(128)} %param.13) | data formatting | bytes 512 | tf_op jit(solution)/shard_map/reshape | solution.py:660
  12.6 0.1 reshape.38.ids_ref
  12.7 0.5 collective-permute-done.2.after_ref
  13.1 0.7 %pad_maximum_fusion = (bf16[16,4608]{1,0:T(8,128)(2,1)S(1)}, bf16[16,4608]{1,0:T(8,128)(2,1)}) fusion(bf16[8,4608]{1,0:T(8,128)(2,1)S(1)} %get-tuple-element.44, bf16[8,4608]{1,0:T(8,128)(2,1)S(1)} %get-tuple-element.42, bf16[8,4608]{1,0:T(8,128)(2,1)S(1)} %get-tuple-element.43, bf16[8,4608]{1,0:T(8,128)(2,1)S(1)} %get-tuple-element.41), kind=kLoop, calls=%fused_computation | loop fusion | flops 589824 | bytes 589824 | tf_op jit(solution)/shard_map/concatenate | solution.py:631
  13.8 1.7 %shard_map.95.staged_ref = bf16[2560,512]{1,0:T(8,128)(2,1)S(1)} custom-call(bf16[2,8,4608]{2,1,0:T(8,128)(2,1)S(1)} %collective-permute-done.2.after_ref, bf16[4608,512]{1,0:T(8,128)(2,1)} %head_hbm.5), custom_call_target="tpu_custom_call" | custom-call | tf_op jit(solution)/shard_map/pallas_call | solution.py:638
  15.5 0.0 collective-permute-done.1
  15.6 0.9 %collective-permute-start.3 = (bf16[16,4608]{1,0:T(8,128)(2,1)}, bf16[16,4608]{1,0:T(8,128)(2,1)S(1)}, u32[]{:S(2)}, u32[]{:S(2)}) collective-permute-start(bf16[16,4608]{1,0:T(8,128)(2,1)} %get-tuple-element.36), channel_id=1, source_target_pairs={{0,2},{2,0},{1,3},{3,1},{4,6},{6,4},{5,7},{7,5},{8,10},{10,8},{9,1... | collective-permute-start | bytes 442376 | tf_op jit(solution)/shard_map/ppermute | solution.py:696
  16.5 3.2 %all-to-all-done.own_ref = bf16[8,8,2432]{2,1,0:T(8,128)(2,1)S(1)} async-done(((bf16[8,8,2432]{2,1,0:T(8,128)(2,1)}), bf16[8,8,2432]{2,1,0:T(8,128)(2,1)S(1)}, u32[]{:S(2)}, u32[]{:S(2)}) %all-to-all-start) | async-done | bytes 311328 | tf_op jit(solution)/shard_map/all_to_all | solution.py:627
  19.7 0.0 collective-permute-start
  19.7 2.1 %shard_map.96 = (bf16[2048,512]{1,0:T(8,128)(2,1)S(1)}, f32[80,512]{1,0:T(8,128)S(1)}, f32[32,128]{1,0:T(8,128)S(1)}) custom-call(bf16[8,8,2432]{2,1,0:T(8,128)(2,1)S(1)} %all-to-all-done.own_ref, f32[2,2,18,128]{3,2,1,0:T(8,128)S(1)} %pad_maximum_fusion.2.vec_ref.all_ref, bf16[2560,512]{1,0:T(8,128)(2,1)S(1)} %shard_map.95.staged_ref, ...), custom_call_target="tpu_custom_call" | custom-call | tf_op jit(solution)/shard_map/pallas_call | solution.py:648
  21.8 0.0 collective-permute-done.other_ref
  21.8 2.2 %shard_map.97 = (f32[16,8,128]{2,1,0:T(8,128)}, f32[64,128]{1,0:T(8,128)S(1)}, bf16[272,512]{1,0:T(8,128)(2,1)}) custom-call(bf16[8,8,2432]{2,1,0:T(8,128)(2,1)S(1)} %collective-permute-done.other_ref, f32[2,2,18,128]{3,2,1,0:T(8,128)S(1)} %pad_maximum_fusion.2.vec_ref.all_ref, s32[64,1]{1,0:T(8,128)S(1)} %reshape.38.ids_ref, ...), custom_call_target="tpu_custom_call" | custom-call | tf_op jit(solution)/shard_map/pallas_call | solution.py:665
  24.0 3.8 %all-to-all-start.1 = ((f32[16,8,128]{2,1,0:T(8,128)}), f32[16,8,128]{2,1,0:T(8,128)S(1)}, u32[]{:S(2)}, u32[]{:S(2)}) async-start(f32[16,8,128]{2,1,0:T(8,128)} %get-tuple-element.32), calls=%async_computation.1 | async-start | bytes 131072 | tf_op jit(solution)/shard_map/all_to_all | solution.py:681
  27.8 3.4 %shard_map.98.outer_ref = f32[144,4608]{1,0:T(8,128)S(1)} custom-call(bf16[272,512]{1,0:T(8,128)(2,1)} %get-tuple-element.34.ops_hbm, bf16[4608,512]{1,0:T(8,128)(2,1)} %head_hbm.5), custom_call_target="tpu_custom_call" | custom-call | tf_op jit(solution)/shard_map/pallas_call | solution.py:683
  31.2 0.0 collective-permute-done.3.refs_1_
  31.2 3.4 %all-to-all-done.1.theirs_ref = f32[16,8,128]{2,1,0:T(8,128)S(1)} async-done(((f32[16,8,128]{2,1,0:T(8,128)}), f32[16,8,128]{2,1,0:T(8,128)S(1)}, u32[]{:S(2)}, u32[]{:S(2)}) %all-to-all-start.1) | async-done | bytes 65568 | tf_op jit(solution)/shard_map/all_to_all | solution.py:681
  34.7 1.6 %shard_map.99 = (bf16[8,54,128]{2,1,0:T(8,128)(2,1)}, f32[1,8]{1,0:T(1,128)}) custom-call(f32[16,8,128]{2,1,0:T(8,128)S(1)} %all-to-all-done.1.theirs_ref, f32[64,128]{1,0:T(8,128)S(1)} %get-tuple-element.33.cols_ref, f32[144,4608]{1,0:T(8,128)S(1)} %shard_map.98.outer_ref, bf16[8,8,2432]{2,1,0:T(8,128)(2,1)S(1)} %all-to-all-done.own_ref, ...), custom_call_target="tpu_custom_call" | custom-call | tf_op jit(solution)/shard_map/pallas_call | solution.py:699
  36.3 10.5 %all_to_all.15.back_ref = bf16[8,54,128]{2,1,0:T(8,128)(2,1)S(1)} all-to-all(bf16[8,54,128]{2,1,0:T(8,128)(2,1)} %get-tuple-element.38), channel_id=1, replica_groups=mesh['parts'=2,'vocab'=4,'mp'=2,'rep'=2] {'vocab','mp'}, dimensions={0} | all-to-all | bytes 221184 | tf_op jit(solution)/shard_map/all_to_all | solution.py:715
  46.8 0.1 collective-permute-start.4
  46.9 1.2 %collective-permute-done.4.other_ref = f32[90,128]{1,0:T(8,128)S(1)} collective-permute-done((f32[90,128]{1,0:T(8,128)S(1)}, f32[90,128]{1,0:T(8,128)S(1)}, u32[]{:S(2)}, u32[]{:S(2)}) %collective-permute-start.4) | collective-permute-done | bytes 46112 | tf_op jit(solution)/shard_map/ppermute | solution.py:719
  48.1 0.6 %shard_map.101 = (f32[144,128]{1,0:T(8,128)}, f32[18,128]{1,0:T(8,128)}) custom-call(f32[90,128]{1,0:T(8,128)S(1)} %shard_map.100.own_ref, f32[90,128]{1,0:T(8,128)S(1)} %collective-permute-done.4.other_ref), custom_call_target="tpu_custom_call" | custom-call | tf_op jit(solution)/shard_map/pallas_call | solution.py:720
  (7 shorter events, 0.1 us)
Async XLA Ops:
  2.5 17.2 %all-to-all-start = ((bf16[8,8,2432]{2,1,0:T(8,128)(2,1)}), bf16[8,8,2432]{2,1,0:T(8,128)(2,1)S(1)}, u32[]{:S(2)}, u32[]{:S(2)}) async-start(bf16[8,8,2432]{2,1,0:T(8,128)(2,1)} %get-tuple-element.22), calls=%async_computation | async-start | bytes 622592 | tf_op jit(solution)/shard_map/all_to_all | solution.py:627
  9.7 5.8 %collective-permute-start.1 = (f32[2,18,128]{2,1,0:T(8,128)S(1)}, f32[2,18,128]{2,1,0:T(8,128)S(1)}, u32[]{:S(2)}, u32[]{:S(2)}) collective-permute-start(f32[2,18,128]{2,1,0:T(8,128)S(1)} %get-tuple-element.27), channel_id=1, source_target_pairs={{0,2},{2,0},{1,3},{3,1},{4,6},{6,4},{5,7},{7,5},{8,10},{10,8},{9,1... | collective-permute-start | bytes 55304 | tf_op jit(solution)/shard_map/ppermute | solution.py:27
  11.8 1.4 %collective-permute-start.2 = (bf16[2,8,4608]{2,1,0:T(8,128)(2,1)S(1)}, bf16[2,8,4608]{2,1,0:T(8,128)(2,1)S(1)}, u32[]{:S(2)}, u32[]{:S(2)}) collective-permute-start(bf16[2,8,4608]{2,1,0:T(8,128)(2,1)S(1)} %get-tuple-element.25), channel_id=1, source_target_pairs={{0,1},{1,0},{2,3},{3,2},{4,5},{5,4},{6,7},{7,6},{8,9},{9,8},{10,11... | collective-permute-start | bytes 442376 | tf_op jit(solution)/shard_map/ppermute | solution.py:629
  15.6 15.7 %collective-permute-start.3 = (bf16[16,4608]{1,0:T(8,128)(2,1)}, bf16[16,4608]{1,0:T(8,128)(2,1)S(1)}, u32[]{:S(2)}, u32[]{:S(2)}) collective-permute-start(bf16[16,4608]{1,0:T(8,128)(2,1)} %get-tuple-element.36), channel_id=1, source_target_pairs={{0,2},{2,0},{1,3},{3,1},{4,6},{6,4},{5,7},{7,5},{8,10},{10,8},{9,1... | collective-permute-start | bytes 442376 | tf_op jit(solution)/shard_map/ppermute | solution.py:696
  19.7 2.1 %collective-permute-start = (bf16[8,8,2432]{2,1,0:T(8,128)(2,1)S(1)}, bf16[8,8,2432]{2,1,0:T(8,128)(2,1)S(1)}, u32[]{:S(2)}, u32[]{:S(2)}) collective-permute-start(bf16[8,8,2432]{2,1,0:T(8,128)(2,1)S(1)} %all-to-all-done.own_ref), channel_id=1, source_target_pairs={{0,1},{1,0},{2,3},{3,2},{4,5},{5,4},{6,7},{7,6},{8,9},{9,8},{10,11... | collective-permute-start | bytes 933896 | tf_op jit(solution)/shard_map/ppermute | solution.py:628
  24.0 10.7 %all-to-all-start.1 = ((f32[16,8,128]{2,1,0:T(8,128)}), f32[16,8,128]{2,1,0:T(8,128)S(1)}, u32[]{:S(2)}, u32[]{:S(2)}) async-start(f32[16,8,128]{2,1,0:T(8,128)} %get-tuple-element.32), calls=%async_computation.1 | async-start | bytes 131072 | tf_op jit(solution)/shard_map/all_to_all | solution.py:681
  46.8 1.3 %collective-permute-start.4 = (f32[90,128]{1,0:T(8,128)S(1)}, f32[90,128]{1,0:T(8,128)S(1)}, u32[]{:S(2)}, u32[]{:S(2)}) collective-permute-start(f32[90,128]{1,0:T(8,128)S(1)} %shard_map.100.own_ref), channel_id=1, source_target_pairs={{0,1},{1,0},{2,3},{3,2},{4,5},{5,4},{6,7},{7,6},{8,9},{9,8},{10,11... | collective-permute-start | bytes 138248 | tf_op jit(solution)/shard_map/ppermute | solution.py:719

commit v10 on v8

--- a/solution.py
+++ b/solution.py
@@ -411,12 +411,13 @@
     swapped = jnp.concatenate([first[half:], first[:half], second[half:], second[:half]], axis=0)
     table = jnp.where(lax.axis_index("rep") == 0, straight, swapped)
     table = table.T[:8]
-    for p in range(slab_ref.shape[0]):
-        slab_ref[p] = table
-    put_slab = pltpu.make_async_copy(slab_ref, slab_hbm, sems.at[0])
-    put_slab.start()
-
-    put_slab.wait()
+    slab_ref[...] = table
+    puts = []
+    for p in range(slab_hbm.shape[0]):
+        puts.append(pltpu.make_async_copy(slab_ref, slab_hbm.at[p], sems.at[2 + p]))
+        puts[p].start()
+    for put in puts:
+        put.wait()
     put_ops.wait()
 
 
@@ -667,9 +668,9 @@
         ),
         [
             pltpu.VMEM((group, model), bf16),
-            pltpu.VMEM((peers, 8, 128), f32),
+            pltpu.VMEM((8, 128), f32),
             pltpu.VMEM((4 * group + 16, voc), bf16),
-            pltpu.SemaphoreType.DMA((2,)),
+            pltpu.SemaphoreType.DMA((2 + peers,)),
         ],
         in_specs=[vmem] * 7,
         out_specs=(hbm, vmem, hbm),

time: 49.2 us -> 49.4 us (level)
  no operation moved by 1% of the time
where the time goes in v10:
time: 49.4 us; the launch traced here: 48.9 us
  starting transfers between devices  14.1 us (29%)
  Pallas kernels  13.6 us (28%)
  blocking collectives  10.5 us (21%)
  waiting for transfers between devices  8.37 us (17%)
  local copies, waits for them, and re-layouts  0.84 us (2%)
  between operations  0.79 us (2%)
  other arithmetic  0.7 us (1%)
    all_to_all x1, blocking collectives, fused(): back = lax.all_to_all(slab, ('vocab', 'mp'), 0, 0)  10.5 us
    all_to_all x1, starting transfers between devices, fused(): got = lax.all_to_all(packed, ('vocab', 'mp'), 0, 0)  7.26 us
    all_to_all x1, starting transfers between devices, fused(): theirs = lax.all_to_all(slab, everyone, 0, 0)  3.81 us
    all_to_all x1, waiting for transfers between devices, fused(): theirs = lax.all_to_all(slab, everyone, 0, 0)  3.44 us
    pallas_call x1, Pallas kernels, fused(): call(outer_kernel, shape((2 * group + 16, model), f32), [pltpu.VMEM((4 *...  3.43 us
    all_to_all x1, waiting for transfers between devices, fused(): got = lax.all_to_all(packed, ('vocab', 'mp'), 0, 0)  3.23 us
    pallas_call x1, Pallas kernels, fused(): call(functools.partial(score_kernel, nv, nm), (pltpu.HBM((peers, 8, 128),...  2.32 us
    pallas_call x1, Pallas kernels, fused(): call(functools.partial(early_kernel, nv, nm), (pltpu.VMEM((model - first,...  2.06 us
  transfers between devices with their start and end apart: 7, of which 4 were waited for; matrix products, arithmetic and copies ran while one was open for 3% of the time, Pallas kernels for 19%

profile of v10, /device:TPU:0, one launch (start us, length us, event | category | flops | bytes accessed | tf_op | source)
XLA Modules:
  0.0 48.9 jit_solution(7700593330727893782)
XLA Ops:
  0.6 1.8 %shard_map.94 = (bf16[8,8,2432]{2,1,0:T(8,128)(2,1)}, f32[2,18,128]{2,1,0:T(8,128)S(1)}, bf16[2,8,4608]{2,1,0:T(8,128)(2,1)S(1)}, bf16[2,8,4608]{2,1,0:T(8,128)(2,1)S(1)}) custom-call(bf16[8,2304]{1,0:T(8,128)(2,1)} %base_hbm.1, bf16[8,18432]{1,0:T(8,128)(2,1)} %hidden_hbm.1, f32[1,18432]{1,0:T(1,128)} %bitcast.20, f32[18,128]{1,0:T(8,128)} %bitcast.21, ...), custom_call_target="tpu_custom_call" | custom-call | tf_op jit(solution)/shard_map/pallas_call | solution.py:601
  2.5 7.3 %all-to-all-start = ((bf16[8,8,2432]{2,1,0:T(8,128)(2,1)}), bf16[8,8,2432]{2,1,0:T(8,128)(2,1)S(1)}, u32[]{:S(2)}, u32[]{:S(2)}) async-start(bf16[8,8,2432]{2,1,0:T(8,128)(2,1)} %get-tuple-element.22), calls=%async_computation | async-start | bytes 622592 | tf_op jit(solution)/shard_map/all_to_all | solution.py:624
  9.7 2.0 %collective-permute-start.1 = (f32[2,18,128]{2,1,0:T(8,128)S(1)}, f32[2,18,128]{2,1,0:T(8,128)S(1)}, u32[]{:S(2)}, u32[]{:S(2)}) collective-permute-start(f32[2,18,128]{2,1,0:T(8,128)S(1)} %get-tuple-element.27), channel_id=1, source_target_pairs={{0,2},{2,0},{1,3},{3,1},{4,6},{6,4},{5,7},{7,5},{8,10},{10,8},{9,1... | collective-permute-start | bytes 55304 | tf_op jit(solution)/shard_map/ppermute | solution.py:27
  11.8 0.0 collective-permute-start.2
  11.8 0.7 %reshape.33 = s32[4,2,8]{2,1,0:T(2,128)S(1)} reshape(s32[64]{0:T(128)} %param.13) | data formatting | bytes 512 | tf_op jit(solution)/shard_map/reshape | solution.py:657
  12.6 0.1 reshape.38.ids_ref
  12.7 0.5 collective-permute-done.2.after_ref
  13.1 0.7 %pad_maximum_fusion = (bf16[16,4608]{1,0:T(8,128)(2,1)S(1)}, bf16[16,4608]{1,0:T(8,128)(2,1)}) fusion(bf16[8,4608]{1,0:T(8,128)(2,1)S(1)} %get-tuple-element.44, bf16[8,4608]{1,0:T(8,128)(2,1)S(1)} %get-tuple-element.42, bf16[8,4608]{1,0:T(8,128)(2,1)S(1)} %get-tuple-element.43, bf16[8,4608]{1,0:T(8,128)(2,1)S(1)} %get-tuple-element.41), kind=kLoop, calls=%fused_computation | loop fusion | flops 589824 | bytes 589824 | tf_op jit(solution)/shard_map/concatenate | solution.py:628
  13.8 1.7 %shard_map.95.staged_ref = bf16[2560,512]{1,0:T(8,128)(2,1)S(1)} custom-call(bf16[2,8,4608]{2,1,0:T(8,128)(2,1)S(1)} %collective-permute-done.2.after_ref, bf16[4608,512]{1,0:T(8,128)(2,1)} %head_hbm.5), custom_call_target="tpu_custom_call" | custom-call | tf_op jit(solution)/shard_map/pallas_call | solution.py:635
  15.5 0.0 collective-permute-done.1
  15.6 0.9 %collective-permute-start.3 = (bf16[16,4608]{1,0:T(8,128)(2,1)}, bf16[16,4608]{1,0:T(8,128)(2,1)S(1)}, u32[]{:S(2)}, u32[]{:S(2)}) collective-permute-start(bf16[16,4608]{1,0:T(8,128)(2,1)} %get-tuple-element.36), channel_id=1, source_target_pairs={{0,2},{2,0},{1,3},{3,1},{4,6},{6,4},{5,7},{7,5},{8,10},{10,8},{9,1... | collective-permute-start | bytes 442376 | tf_op jit(solution)/shard_map/ppermute | solution.py:693
  16.5 3.2 %all-to-all-done.own_ref = bf16[8,8,2432]{2,1,0:T(8,128)(2,1)S(1)} async-done(((bf16[8,8,2432]{2,1,0:T(8,128)(2,1)}), bf16[8,8,2432]{2,1,0:T(8,128)(2,1)S(1)}, u32[]{:S(2)}, u32[]{:S(2)}) %all-to-all-start) | async-done | bytes 311328 | tf_op jit(solution)/shard_map/all_to_all | solution.py:624
  19.7 0.0 collective-permute-start
  19.7 2.1 %shard_map.96 = (bf16[2048,512]{1,0:T(8,128)(2,1)S(1)}, f32[80,512]{1,0:T(8,128)S(1)}, f32[32,128]{1,0:T(8,128)S(1)}) custom-call(bf16[8,8,2432]{2,1,0:T(8,128)(2,1)S(1)} %all-to-all-done.own_ref, f32[2,2,18,128]{3,2,1,0:T(8,128)S(1)} %pad_maximum_fusion.2.vec_ref.all_ref, bf16[2560,512]{1,0:T(8,128)(2,1)S(1)} %shard_map.95.staged_ref, ...), custom_call_target="tpu_custom_call" | custom-call | tf_op jit(solution)/shard_map/pallas_call | solution.py:645
  21.8 0.0 collective-permute-done.other_ref
  21.8 2.3 %shard_map.97 = (f32[16,8,128]{2,1,0:T(8,128)}, f32[64,128]{1,0:T(8,128)S(1)}, bf16[272,512]{1,0:T(8,128)(2,1)}) custom-call(bf16[8,8,2432]{2,1,0:T(8,128)(2,1)S(1)} %collective-permute-done.other_ref, f32[2,2,18,128]{3,2,1,0:T(8,128)S(1)} %pad_maximum_fusion.2.vec_ref.all_ref, s32[64,1]{1,0:T(8,128)S(1)} %reshape.38.ids_ref, ...), custom_call_target="tpu_custom_call" | custom-call | tf_op jit(solution)/shard_map/pallas_call | solution.py:662
  24.1 3.8 %all-to-all-start.1 = ((f32[16,8,128]{2,1,0:T(8,128)}), f32[16,8,128]{2,1,0:T(8,128)S(1)}, u32[]{:S(2)}, u32[]{:S(2)}) async-start(f32[16,8,128]{2,1,0:T(8,128)} %get-tuple-element.32), calls=%async_computation.1 | async-start | bytes 131072 | tf_op jit(solution)/shard_map/all_to_all | solution.py:678
  28.0 3.4 %shard_map.98.outer_ref = f32[144,4608]{1,0:T(8,128)S(1)} custom-call(bf16[272,512]{1,0:T(8,128)(2,1)} %get-tuple-element.34.ops_hbm, bf16[4608,512]{1,0:T(8,128)(2,1)} %head_hbm.5), custom_call_target="tpu_custom_call" | custom-call | tf_op jit(solution)/shard_map/pallas_call | solution.py:680
  31.4 0.0 collective-permute-done.3.refs_1_
  31.4 3.4 %all-to-all-done.1.theirs_ref = f32[16,8,128]{2,1,0:T(8,128)S(1)} async-done(((f32[16,8,128]{2,1,0:T(8,128)}), f32[16,8,128]{2,1,0:T(8,128)S(1)}, u32[]{:S(2)}, u32[]{:S(2)}) %all-to-all-start.1) | async-done | bytes 65568 | tf_op jit(solution)/shard_map/all_to_all | solution.py:678
  34.9 1.6 %shard_map.99 = (bf16[8,54,128]{2,1,0:T(8,128)(2,1)}, f32[1,8]{1,0:T(1,128)}) custom-call(f32[16,8,128]{2,1,0:T(8,128)S(1)} %all-to-all-done.1.theirs_ref, f32[64,128]{1,0:T(8,128)S(1)} %get-tuple-element.33.cols_ref, f32[144,4608]{1,0:T(8,128)S(1)} %shard_map.98.outer_ref, bf16[8,8,2432]{2,1,0:T(8,128)(2,1)S(1)} %all-to-all-done.own_ref, ...), custom_call_target="tpu_custom_call" | custom-call | tf_op jit(solution)/shard_map/pallas_call | solution.py:696
  36.5 10.5 %all_to_all.15.back_ref = bf16[8,54,128]{2,1,0:T(8,128)(2,1)S(1)} all-to-all(bf16[8,54,128]{2,1,0:T(8,128)(2,1)} %get-tuple-element.38), channel_id=1, replica_groups=mesh['parts'=2,'vocab'=4,'mp'=2,'rep'=2] {'vocab','mp'}, dimensions={0} | all-to-all | bytes 221184 | tf_op jit(solution)/shard_map/all_to_all | solution.py:712
  47.0 0.1 collective-permute-start.4
  47.1 1.2 %collective-permute-done.4.other_ref = f32[90,128]{1,0:T(8,128)S(1)} collective-permute-done((f32[90,128]{1,0:T(8,128)S(1)}, f32[90,128]{1,0:T(8,128)S(1)}, u32[]{:S(2)}, u32[]{:S(2)}) %collective-permute-start.4) | collective-permute-done | bytes 46112 | tf_op jit(solution)/shard_map/ppermute | solution.py:716
  48.3 0.6 %shard_map.101 = (f32[144,128]{1,0:T(8,128)}, f32[18,128]{1,0:T(8,128)}) custom-call(f32[90,128]{1,0:T(8,128)S(1)} %shard_map.100.own_ref, f32[90,128]{1,0:T(8,128)S(1)} %collective-permute-done.4.other_ref), custom_call_target="tpu_custom_call" | custom-call | tf_op jit(solution)/shard_map/pallas_call | solution.py:717
  (7 shorter events, 0.1 us)
Async XLA Ops:
  2.5 17.2 %all-to-all-start = ((bf16[8,8,2432]{2,1,0:T(8,128)(2,1)}), bf16[8,8,2432]{2,1,0:T(8,128)(2,1)S(1)}, u32[]{:S(2)}, u32[]{:S(2)}) async-start(bf16[8,8,2432]{2,1,0:T(8,128)(2,1)} %get-tuple-element.22), calls=%async_computation | async-start | bytes 622592 | tf_op jit(solution)/shard_map/all_to_all | solution.py:624
  9.7 5.8 %collective-permute-start.1 = (f32[2,18,128]{2,1,0:T(8,128)S(1)}, f32[2,18,128]{2,1,0:T(8,128)S(1)}, u32[]{:S(2)}, u32[]{:S(2)}) collective-permute-start(f32[2,18,128]{2,1,0:T(8,128)S(1)} %get-tuple-element.27), channel_id=1, source_target_pairs={{0,2},{2,0},{1,3},{3,1},{4,6},{6,4},{5,7},{7,5},{8,10},{10,8},{9,1... | collective-permute-start | bytes 55304 | tf_op jit(solution)/shard_map/ppermute | solution.py:27
  11.8 1.4 %collective-permute-start.2 = (bf16[2,8,4608]{2,1,0:T(8,128)(2,1)S(1)}, bf16[2,8,4608]{2,1,0:T(8,128)(2,1)S(1)}, u32[]{:S(2)}, u32[]{:S(2)}) collective-permute-start(bf16[2,8,4608]{2,1,0:T(8,128)(2,1)S(1)} %get-tuple-element.25), channel_id=1, source_target_pairs={{0,1},{1,0},{2,3},{3,2},{4,5},{5,4},{6,7},{7,6},{8,9},{9,8},{10,11... | collective-permute-start | bytes 442376 | tf_op jit(solution)/shard_map/ppermute | solution.py:626
  15.6 15.8 %collective-permute-start.3 = (bf16[16,4608]{1,0:T(8,128)(2,1)}, bf16[16,4608]{1,0:T(8,128)(2,1)S(1)}, u32[]{:S(2)}, u32[]{:S(2)}) collective-permute-start(bf16[16,4608]{1,0:T(8,128)(2,1)} %get-tuple-element.36), channel_id=1, source_target_pairs={{0,2},{2,0},{1,3},{3,1},{4,6},{6,4},{5,7},{7,5},{8,10},{10,8},{9,1... | collective-permute-start | bytes 442376 | tf_op jit(solution)/shard_map/ppermute | solution.py:693
  19.7 2.1 %collective-permute-start = (bf16[8,8,2432]{2,1,0:T(8,128)(2,1)S(1)}, bf16[8,8,2432]{2,1,0:T(8,128)(2,1)S(1)}, u32[]{:S(2)}, u32[]{:S(2)}) collective-permute-start(bf16[8,8,2432]{2,1,0:T(8,128)(2,1)S(1)} %all-to-all-done.own_ref), channel_id=1, source_target_pairs={{0,1},{1,0},{2,3},{3,2},{4,5},{5,4},{6,7},{7,6},{8,9},{9,8},{10,11... | collective-permute-start | bytes 933896 | tf_op jit(solution)/shard_map/ppermute | solution.py:625
  24.1 10.7 %all-to-all-start.1 = ((f32[16,8,128]{2,1,0:T(8,128)}), f32[16,8,128]{2,1,0:T(8,128)S(1)}, u32[]{:S(2)}, u32[]{:S(2)}) async-start(f32[16,8,128]{2,1,0:T(8,128)} %get-tuple-element.32), calls=%async_computation.1 | async-start | bytes 131072 | tf_op jit(solution)/shard_map/all_to_all | solution.py:678
  47.0 1.3 %collective-permute-start.4 = (f32[90,128]{1,0:T(8,128)S(1)}, f32[90,128]{1,0:T(8,128)S(1)}, u32[]{:S(2)}, u32[]{:S(2)}) collective-permute-start(f32[90,128]{1,0:T(8,128)S(1)} %shard_map.100.own_ref), channel_id=1, source_target_pairs={{0,1},{1,0},{2,3},{3,2},{4,5},{5,4},{6,7},{7,6},{8,9},{9,8},{10,11... | collective-permute-start | bytes 138248 | tf_op jit(solution)/shard_map/ppermute | solution.py:716
